TPU v7x, 256 devices: a whole 4x4x8 slice. The times are simulated.
256 devices in a mesh: pair: 64 (over z, x, core), virt: 4 (over y).
Axes of the slice: x: 4, y: 4, z: 8, core: 2. Of those that a mesh axis runs over, the one named last changes fastest.
Arguments:
- amps: bfloat16 [2048, 480, 480], P('pair', 'virt'), may hold values from -6 to 6
- integrals: bfloat16 [2304, 230400], P(None, ('virt', 'pair')), may hold values from -0.01171875 to 0.01171875
- slot_pair: int32 [2048], P('pair'), may hold values from -1 to 1175, as said below
- occ_energy: float32 [48], replicated, may hold values from -1.2 to -0.4
- virt_energy: float32 [48], replicated, may hold values from 0.3 to 1.5
Outputs:
- update: float32 [2048, 48, 48], P('pair', 'virt')
Inputs may be any that keep to these rules, and one draw needn't show every extreme that they name: `slot_pair`: each of the 1176 pairs i <= j stands in exactly one slot, -1 marks an empty slot; the 32 slots of one index of pair hold uneven numbers of pairs, and some index has all 32 filled.
All inputs are finite; a program needn't handle non-finite values.
Results may differ from a plain program's by a relative error of at most 0.0003.
Values may be sent and summed in bfloat16 or wider, within the bound.
No kernel may reach another device: no remote copies, remote signals or barrier semaphores. Data moves between devices by JAX's collectives and lax.ppermute only.
A program may use at most 192 MiB of HBM per device.

v0:
```python
import jax
import jax.numpy as jnp
from jax import lax
from jax.sharding import PartitionSpec as P


def pair_energy(slot_pair, occ_energy):
    nocc_count = occ_energy.shape[0]
    orbital = jnp.arange(nocc_count, dtype=jnp.int32)
    starts_row = orbital * nocc_count - orbital * (orbital - 1) // 2
    row_index = jnp.sum((starts_row[None, 1:] <= slot_pair[:, None]).astype(jnp.int32), axis=1)
    same_row = orbital[None, :] == row_index[:, None]
    row_start = jnp.sum(jnp.where(same_row, starts_row[None, :], 0), axis=1)
    column_index = slot_pair - row_start + row_index
    first_energy = jnp.sum(
        jnp.where(same_row, occ_energy[None, :], jnp.zeros_like(occ_energy)[None, :]), axis=1
    )
    same_column = orbital[None, :] == column_index[:, None]
    second_energy = jnp.sum(
        jnp.where(same_column, occ_energy[None, :], jnp.zeros_like(occ_energy)[None, :]), axis=1
    )
    return (first_energy + second_energy, slot_pair >= 0)


def ladder_term(row_block, columns):
    partial_value = lax.dot_general(
        row_block, columns, (((1,), (1,)), ((), ())), preferred_element_type=jnp.float32
    )
    return partial_value


def body(amps, integrals, slot_pair, occ_energy, virt_energy):
    slot_count = amps.shape[0]
    local_width = amps.shape[1] * amps.shape[2]
    flattened = amps.reshape(slot_count, local_width)
    window = virt_energy.shape[0]
    virt_count = lax.axis_size("virt")
    local_rows = window // virt_count
    panels = lax.all_to_all(flattened, "pair", split_axis=1, concat_axis=0, tiled=True)
    owned = lax.psum_scatter(
        ladder_term(panels, integrals), "pair", scatter_dimension=0, tiled=True
    )
    owned = lax.psum_scatter(
        owned.reshape(slot_count, window, window), "virt", scatter_dimension=1, tiled=True
    )
    flipped = lax.all_to_all(owned, "virt", split_axis=2, concat_axis=1, tiled=True)
    residual = owned + jnp.transpose(flipped, (0, 2, 1))
    pair_sum, filled = pair_energy(slot_pair, occ_energy)
    local_energy = lax.dynamic_slice_in_dim(
        virt_energy, lax.axis_index("virt") * local_rows, local_rows
    )
    denominator = pair_sum[:, None, None] - local_energy[None, :, None] - virt_energy[None, None, :]
    return jnp.where(filled[:, None, None], residual / denominator, jnp.zeros_like(residual))


def solution(mesh):
    placed = (P("pair", "virt", None), P(None, ("virt", "pair")), P("pair"), P(), P())
    return jax.shard_map(
        body, mesh=mesh, in_specs=placed, out_specs=P("pair", "virt", None), check_vma=False
    )
```

profile of v0, /device:TPU:2, one launch (start us, length us, event | category | flops | bytes accessed | tf_op | source)
XLA Modules:
  0.0 388.0 jit_solution(6737655725469831264)
XLA Ops:
  6.5 0.0 reduce-scatter.3.cloned.1.call-start
  6.5 12.9 %all_to_all.27 = bf16[32,64,900]{2,1,0:T(8,128)(2,1)} reshape(bf16[32,120,480]{2,1,0:T(8,128)(2,1)} %param.5) | data formatting | bytes 7372800 | tf_op jit(solution)/shard_map/all_to_all | solution.py:39
  19.5 4.5 %copy.18 = bf16[32,64,900]{2,0,1:T(8,128)(2,1)S(1)} copy(bf16[32,64,900]{2,1,0:T(8,128)(2,1)} %all_to_all.27) | data formatting | bytes 7372800 | tf_op jit(solution)/shard_map/all_to_all | solution.py:39
  24.0 0.0 copy-start.3
  24.0 108.3 %all_to_all.37 = bf16[32,64,900]{2,0,1:T(8,128)(2,1)S(1)} all-to-all(bf16[32,64,900]{2,0,1:T(8,128)(2,1)S(1)} %copy.18), channel_id=1, replica_groups=mesh['pair'=64,'virt'=4] {'pair'}, dimensions={1} | all-to-all | bytes 7372800 | tf_op jit(solution)/shard_map/all_to_all | solution.py:39
  132.3 0.0 copy-done.3
  132.3 13.1 %fusion.3 = f32[2048,2304]{1,0:T(8,128)} fusion(bf16[2048,900]{1,0:T(8,128)(2,1)S(1)} %bitcast.23, bf16[2304,900]{0,1:T(8,128)(2,1)S(1)} %copy-done.3), kind=kOutput, calls=%fused_computation.21 | convolution fusion | flops 8493465600 | bytes 26707968 | tf_op jit(solution)/shard_map/dot_general | solution.py:26
  145.3 0.0 copy-start.2
  145.3 0.0 copy-start
  145.4 0.0 copy-start.1
  145.4 0.0 reduce-scatter.3.cloned.1.call-update
  145.4 0.0 reduce-scatter.5.cloned.1.call-start
  145.4 0.1 slice.3
  145.5 0.5 copy-done.2
  146.0 0.2 convert_reduce_fusion
  146.2 192.1 %reduce-scatter.3.cloned.1.call-done = f32[32,2304]{1,0:T(8,128)} async-done(((f32[2048,2304]{1,0:T(8,128)}), f32[32,2304]{1,0:T(8,128)}) %reduce-scatter.3.cloned.1.call-update) | async-done | bytes 294928 | tf_op jit(solution)/shard_map/reduce_scatter | solution.py:40
  338.3 2.3 copy.24
  340.7 0.0 reduce-scatter.5.cloned.1.call-update
  340.7 0.2 select_reduce_fusion.1
  340.9 0.0 copy-done
  340.9 0.1 dynamic_slice.3
  341.0 0.0 copy-done.1
  341.0 0.2 select_reduce_fusion
  341.2 0.1 broadcast_subtract_fusion
  341.2 25.7 %reduce-scatter.5.cloned.1.call-done = f32[32,12,48]{0,2,1:T(8,128)} async-done(((f32[32,48,48]{0,2,1:T(8,128)}), f32[32,12,48]{0,2,1:T(8,128)}) %reduce-scatter.5.cloned.1.call-update) | async-done | bytes 73744 | tf_op jit(solution)/shard_map/reduce_scatter | solution.py:43
  366.9 1.1 copy.28
  368.0 0.8 reshape.76
  368.8 3.3 all-to-all-start.1
  372.1 5.6 %all-to-all-done.1 = f32[4,1,4608]{2,1,0:T(1,128)S(1)} async-done(((f32[4,1,4608]{2,1,0:T(1,128)}), f32[4,1,4608]{2,1,0:T(1,128)S(1)}, u32[]{:S(2)}, u32[]{:S(2)}) %all-to-all-start.1) | async-done | bytes 73760 | tf_op jit(solution)/shard_map/all_to_all | solution.py:46
  377.7 0.5 broadcast.80
  378.2 0.8 reduce
  379.1 0.1 reshape.77
  379.3 1.1 fusion.1
  380.4 0.8 copy.23
  (6 shorter events, 0.1 us)
Async XLA Ops:
  6.5 331.8 %reduce-scatter.3.cloned.1.call-start = ((), (), s32[]{:S(2)}) async-start(), calls=%async_computation.4 | async-start | bytes 19169280 | tf_op jit(solution)/shard_map/reduce_scatter | solution.py:40
  24.0 108.3 %copy-start.3 = (bf16[2304,900]{0,1:T(8,128)(2,1)S(1)}, bf16[2304,900]{0,1:T(8,128)(2,1)}, u32[]{:S(2)}) copy-start(bf16[2304,900]{0,1:T(8,128)(2,1)} %param.6) | copy-start | bytes 12441604
  145.3 0.7 copy-start.2
  145.3 195.5 %copy-start = (f32[48]{0:T(128)S(1)}, f32[48]{0:T(128)}, u32[]{:S(2)}) copy-start(f32[48]{0:T(128)} %param.9) | copy-start | bytes 580
  145.4 195.6 %copy-start.1 = (f32[48]{0:T(128)S(1)}, f32[48]{0:T(128)}, u32[]{:S(2)}) copy-start(f32[48]{0:T(128)} %param.8) | copy-start | bytes 580
  145.4 221.5 %reduce-scatter.5.cloned.1.call-start = ((), (), s32[]{:S(2)}) async-start(), calls=%async_computation.5 | async-start | bytes 1474560 | tf_op jit(solution)/shard_map/reduce_scatter | solution.py:43
  368.8 8.9 %all-to-all-start.1 = ((f32[4,1,4608]{2,1,0:T(1,128)}), f32[4,1,4608]{2,1,0:T(1,128)S(1)}, u32[]{:S(2)}, u32[]{:S(2)}) async-start(f32[4,1,4608]{2,1,0:T(1,128)} %reshape.76), calls=%async_computation.3 | async-start | bytes 147456 | tf_op jit(solution)/shard_map/all_to_all | solution.py:46
Sparse Core Ops, SparseCore 0:
  145.5 192.7 reduce-scatter.2
  340.9 25.9 reduce-scatter.4
where the time goes:
time: 388 us
  waiting for transfers between devices  223 us (57%)
  blocking collectives  108 us (28%)
  local copies, waits for them, and re-layouts  23.8 us (6%)
  between operations  13.5 us (3%)
  matrix products  13.1 us (3%)
    reduce_scatter x1, waiting for transfers between devices, body(): lax.psum_scatter(ladder_term(panels, integrals), 'pair', scatter_dimensio...  192 us
    all_to_all x1, blocking collectives, body(): lax.all_to_all(flattened, 'pair', split_axis=1, concat_axis=0, tiled=True)  108 us
    reduce_scatter x1, waiting for transfers between devices, body(): lax.psum_scatter(owned.reshape(slot_count, window, window), 'virt', scatt...  25.7 us
    all_to_all x2, local copies, waits for them, and re-layouts, body(): lax.all_to_all(flattened, 'pair', split_axis=1, concat_axis=0, tiled=True)  17.5 us
    dot_general x1, matrix products, ladder_term(): lax.dot_general(row_block, columns, (((1,), (1,)), ((), ())), preferred_e...  13.1 us
  transfers between devices with their start and end apart: 3, of which 3 were waited for; matrix products, arithmetic and copies ran while one was open for 0% of the time, Pallas kernels for 0%

commit v1 on v0

v1 whole, which is shorter than its diff:
```python
import jax
import jax.numpy as jnp
import numpy as np
from jax import lax
from jax.experimental import pallas as pl
from jax.experimental.pallas import tpu as pltpu
from jax.sharding import PartitionSpec as P

CHUNK = 8
LANES = 128
BF = jnp.bfloat16
F32 = jnp.float32


def params(mib=60):
    return pltpu.CompilerParams(vmem_limit_bytes=mib * 1024 * 1024)


def pair_energy(slot_pair, occ_energy):
    nocc_count = occ_energy.shape[0]
    orbital = jnp.arange(nocc_count, dtype=jnp.int32)
    starts_row = orbital * nocc_count - orbital * (orbital - 1) // 2
    row_index = jnp.sum((starts_row[None, 1:] <= slot_pair[:, None]).astype(jnp.int32), axis=1)
    same_row = orbital[None, :] == row_index[:, None]
    row_start = jnp.sum(jnp.where(same_row, starts_row[None, :], 0), axis=1)
    column_index = slot_pair - row_start + row_index
    first_energy = jnp.sum(
        jnp.where(same_row, occ_energy[None, :], jnp.zeros_like(occ_energy)[None, :]), axis=1
    )
    same_column = orbital[None, :] == column_index[:, None]
    second_energy = jnp.sum(
        jnp.where(same_column, occ_energy[None, :], jnp.zeros_like(occ_energy)[None, :]), axis=1
    )
    return (first_energy + second_energy, slot_pair >= 0)


def unique_pairs(window):
    a, b = np.triu_indices(window)
    count = -(-a.size // 256) * 256
    one = np.full((1, count), -1, np.int32)
    two = np.full((1, count), -1, np.int32)
    one[0, : a.size] = a * window + b
    two[0, : a.size] = b * window + a
    return one, two


def flatten_kernel(dests, width, tiles, x_ref, o_ref, rows, flat):
    count, inner = x_ref.shape[1], x_ref.shape[2]
    for k in range(0, inner, LANES):
        part = min(LANES, inner - k)
        for s in range(CHUNK):
            rows[k // LANES, pl.ds(s * count, count), :part] = x_ref[s, :, k : k + part].astype(F32)
    for c in range(count):
        for k in range(0, inner, LANES):
            part = min(LANES, inner - k)
            piece = rows[k // LANES, pl.ds(c, CHUNK, stride=count), :]
            flat[:, c * inner + k : c * inner + k + part] = piece[:, :part]
    flat[:, count * inner :] = jnp.zeros((CHUNK, flat.shape[1] - count * inner), F32)
    for q in range(dests):
        for t in range(tiles):
            at = q * width + t * LANES
            o_ref[q, t] = flat[:, at : at + LANES].astype(BF)


def flatten(amps, chunk, dests):
    slots, count, inner = amps.shape
    width = count * inner // dests
    tiles = -(-width // LANES)
    return pl.pallas_call(
        lambda *refs: flatten_kernel(dests, width, tiles, *refs),
        grid=(1,),
        in_specs=[pl.BlockSpec((CHUNK, count, inner), lambda i: (chunk, 0, 0))],
        out_specs=pl.BlockSpec((dests, tiles, CHUNK, LANES), lambda i: (0, 0, 0, 0)),
        out_shape=jax.ShapeDtypeStruct((dests, tiles, CHUNK, LANES), BF),
        scratch_shapes=[
            pltpu.VMEM((-(-inner // LANES), CHUNK * count, LANES), F32),
            pltpu.VMEM((CHUNK, count * inner + 2 * LANES), F32),
        ],
        compiler_params=params(),
        cost_estimate=pl.CostEstimate(flops=0, bytes_accessed=4_000_000, transcendentals=0),
    )(amps)


def fold_kernel(one_ref, two_ref, b_ref, hi_ref, lo_ref):
    width, full = b_ref.shape
    row = lax.broadcasted_iota(jnp.int32, (full, one_ref.shape[1]), 0)
    pick = (row == one_ref[...]).astype(F32) + (row == two_ref[...]).astype(F32)
    both = jnp.dot(b_ref[...], pick.astype(BF), preferred_element_type=F32)
    hi = both.astype(BF)
    rest = hi_ref.shape[0] - width
    hi_ref[:width] = hi
    lo_ref[:width] = (both - hi.astype(F32)).astype(BF)
    hi_ref[width:] = jnp.zeros((rest, hi.shape[1]), BF)
    lo_ref[width:] = jnp.zeros((rest, hi.shape[1]), BF)


def fold(columns, one, two):
    width, full = columns.shape
    padded = -(-width // LANES) * LANES
    count, block = one.shape[1], 256
    return pl.pallas_call(
        fold_kernel,
        grid=(count // block,),
        in_specs=[
            pl.BlockSpec((1, block), lambda i: (0, i)),
            pl.BlockSpec((1, block), lambda i: (0, i)),
            pl.BlockSpec((width, full), lambda i: (0, 0), pipeline_mode=pl.Buffered(1)),
        ],
        out_specs=[pl.BlockSpec((padded, block), lambda i: (0, i))] * 2,
        out_shape=[jax.ShapeDtypeStruct((padded, count), BF)] * 2,
        compiler_params=params(),
        cost_estimate=pl.CostEstimate(
            flops=2 * width * full * count, bytes_accessed=10_000_000, transcendentals=0
        ),
    )(one, two, columns)


def ladder_kernel(x_ref, hi_ref, lo_ref, o_ref):
    group, tiles = x_ref.shape[0], x_ref.shape[1]
    total = None
    for t in range(tiles):
        a = x_ref[:, t].astype(F32).reshape(group * CHUNK, LANES).astype(BF)
        at = pl.ds(t * LANES, LANES)
        part = jnp.dot(a, hi_ref[at, :], preferred_element_type=F32)
        part += jnp.dot(a, lo_ref[at, :], preferred_element_type=F32)
        total = part if total is None else total + part
    o_ref[...] = total.reshape(o_ref.shape)


def ladder(panels, hi, lo):
    dests, tiles = panels.shape[0], panels.shape[1]
    padded, count = hi.shape
    group = 16
    return pl.pallas_call(
        ladder_kernel,
        grid=(dests // group,),
        in_specs=[
            pl.BlockSpec((group, tiles, CHUNK, LANES), lambda i: (i, 0, 0, 0)),
            pl.BlockSpec((padded, count), lambda i: (0, 0), pipeline_mode=pl.Buffered(1)),
            pl.BlockSpec((padded, count), lambda i: (0, 0), pipeline_mode=pl.Buffered(1)),
        ],
        out_specs=pl.BlockSpec((group, CHUNK, count), lambda i: (i, 0, 0)),
        out_shape=jax.ShapeDtypeStruct((dests, CHUNK, count), F32),
        compiler_params=params(),
        cost_estimate=pl.CostEstimate(
            flops=4 * dests * CHUNK * padded * count, bytes_accessed=10_000_000, transcendentals=0
        ),
    )(panels, hi, lo)


def update_kernel(window, g_ref, col_ref, pair_ref, ea_ref, eb_ref, o_ref):
    total = jnp.sum(g_ref[...], axis=0)
    slots, count = total.shape
    hi = total.astype(BF).astype(F32)
    mid = (total - hi).astype(BF).astype(F32)
    low = total - hi - mid
    parts = jnp.concatenate([hi, mid, low], axis=0).astype(BF)
    row = lax.broadcasted_iota(jnp.int32, (count, col_ref.shape[1]), 0)
    pick = (row == col_ref[...]).astype(F32).astype(BF)
    wide = jnp.dot(parts, pick, preferred_element_type=F32)
    residual = wide[:slots] + wide[slots : 2 * slots] + wide[2 * slots :]
    denominator = pair_ref[...] - ea_ref[...] - eb_ref[...]
    o_ref[...] = residual / denominator


def body(amps, integrals, slot_pair, occ_energy, virt_energy):
    slots = amps.shape[0]
    window = virt_energy.shape[0]
    pairs = lax.axis_size("pair")
    local_rows = window // lax.axis_size("virt")
    one, two = unique_pairs(window)
    count = one.shape[1]
    hi, lo = fold(integrals.T, jnp.asarray(one), jnp.asarray(two))
    owned = []
    for chunk in range(slots // CHUNK):
        panels = lax.all_to_all(flatten(amps, chunk, pairs), "pair", 0, 0, tiled=True)
        partial = ladder(panels, hi, lo)
        owned.append(lax.psum_scatter(partial, "pair", scatter_dimension=0, tiled=True))
    mine = jnp.concatenate(owned, axis=0).reshape(slots, count)
    everyone = lax.all_gather(mine, "virt", tiled=False)

    pair_sum, filled = pair_energy(slot_pair, occ_energy)
    first = lax.axis_index("virt") * local_rows
    a = jnp.repeat(first + jnp.arange(local_rows, dtype=jnp.int32), window)
    b = jnp.tile(jnp.arange(window, dtype=jnp.int32), local_rows)
    low, high = jnp.minimum(a, b), jnp.maximum(a, b)
    column = low * window - low * (low - 1) // 2 + high - low
    wide = local_rows * window
    full = -(-wide // LANES) * LANES
    column = jnp.pad(column, (0, full - wide), constant_values=-1)[None]
    local_energy = lax.dynamic_slice_in_dim(virt_energy, first, local_rows)
    ea = jnp.pad(jnp.repeat(local_energy, window), (0, full - wide))[None]
    eb = jnp.pad(jnp.tile(virt_energy, local_rows), (0, full - wide))[None]
    update = pl.pallas_call(
        lambda *refs: update_kernel(window, *refs),
        out_shape=jax.ShapeDtypeStruct((slots, full), F32),
        compiler_params=params(),
    )(everyone, column, pair_sum[:, None], ea, eb)
    update = update[:, :wide].reshape(slots, local_rows, window)
    return jnp.where(filled[:, None, None], update, jnp.zeros_like(update))


def solution(mesh):
    placed = (P("pair", "virt", None), P(None, ("virt", "pair")), P("pair"), P(), P())
    return jax.shard_map(
        body, mesh=mesh, in_specs=placed, out_specs=P("pair", "virt", None), check_vma=False
    )
```

time: 388 us -> 664 us (1.71)
  waiting for transfers between devices: 223 us -> 444 us
  Pallas kernels: 0 us -> 63.5 us
  local copies, waits for them, and re-layouts: 23.8 us -> 6.38 us
  matrix products: 13.1 us -> 0 us
  blocking collectives: 108 us -> 121 us
  starting transfers between devices: 3.33 us -> 12.2 us
    unnamed x2 -> x8, waiting for transfers between devices: 0.03 us -> 426 us
    reduce_scatter x2 -> x0, waiting for transfers between devices: 218 us -> none  [the longest x1 192 us: body(): lax.psum_scatter(ladder_term(panels, integrals), 'pair', scatter_dimensio...]
    pallas_call x0 -> x10, Pallas kernels: none -> 63.5 us  [the longest x4 38.4 us: ladder(): pl.pallas_call(ladder_kernel, grid=(dests // group,), in_specs=[pl.BlockS...]
    all_to_all x5 -> x0, local copies, waits for them, and re-layouts: 18 us -> none  [the longest x2 17.5 us: body(): lax.all_to_all(flattened, 'pair', split_axis=1, concat_axis=0, tiled=True)]
    all_gather x0 -> x1, blocking collectives: none -> 14.2 us  [body(): everyone = lax.all_gather(mine, 'virt', tiled=False)]
    all_to_all x1, waiting for transfers between devices: 5.62 us -> 18.7 us  [body(): lax.all_to_all(flatten(amps, chunk, pairs), 'pair', 0, 0, tiled=True)]
    dot_general x1 -> x0, matrix products: 13.1 us -> none  [ladder_term(): lax.dot_general(row_block, columns, (((1,), (1,)), ((), ())), preferred_e...]
    all_to_all x1, starting transfers between devices: 3.29 us -> 12 us  [body(): lax.all_to_all(flatten(amps, chunk, pairs), 'pair', 0, 0, tiled=True)]
  transfers between devices with their start and end apart: 3 -> 5, of which waited for: 3 -> 4; matrix products, arithmetic and copies ran while one was open for 0% -> 1% of each run, Pallas kernels for 0% -> 7%
where the time goes in v1:
time: 664 us; the launch traced here: 663 us
  waiting for transfers between devices  444 us (67%)
  blocking collectives  121 us (18%)
  Pallas kernels  63.5 us (10%)
  between operations  13.2 us (2%)
  starting transfers between devices  12.2 us (2%)
    unnamed x8, waiting for transfers between devices  426 us
    all_to_all x3, blocking collectives, body(): lax.all_to_all(flatten(amps, chunk, pairs), 'pair', 0, 0, tiled=True)  107 us
    pallas_call x4, Pallas kernels, ladder(): pl.pallas_call(ladder_kernel, grid=(dests // group,), in_specs=[pl.BlockS...  38.4 us
    all_to_all x1, waiting for transfers between devices, body(): lax.all_to_all(flatten(amps, chunk, pairs), 'pair', 0, 0, tiled=True)  18.7 us
    all_gather x1, blocking collectives, body(): everyone = lax.all_gather(mine, 'virt', tiled=False)  14.2 us
  transfers between devices with their start and end apart: 5, of which 4 were waited for; matrix products, arithmetic and copies ran while one was open for 1% of the time, Pallas kernels for 7%

profile of v1, /device:TPU:2, one launch (start us, length us, event | category | flops | bytes accessed | tf_op | source)
XLA Modules:
  0.0 662.6 jit_solution(12154492496312933628)
XLA Ops:
  6.5 3.2 shard_map.73
  9.8 12.0 %all-to-all-start = ((bf16[64,8,8,128]{3,2,1,0:T(8,128)(2,1)}), bf16[64,8,8,128]{3,2,1,0:T(8,128)(2,1)S(1)}, u32[]{:S(2)}, u32[]{:S(2)}) async-start(bf16[64,8,8,128]{3,2,1,0:T(8,128)(2,1)} %shard_map.73), calls=%async_computation | async-start | bytes 2097152 | tf_op jit(solution)/shard_map/all_to_all | solution.py:176
  21.8 0.0 reduce-scatter.13.cloned.1.call-start
  21.8 10.0 %shard_map.74 = (bf16[1024,1280]{1,0:T(8,128)(2,1)}, bf16[1024,1280]{1,0:T(8,128)(2,1)}) custom-call(s32[1,1280]{1,0:T(1,128)} %constant.49.clone.one_ref, s32[1,1280]{1,0:T(1,128)} %constant.50.clone.two_ref, bf16[900,2304]{1,0:T(8,128)(2,1)} %bitcast.8), custom_call_target="tpu_custom_call" | custom-call | flops 5308416000 | bytes 10000000 | tf_op jit(solution)/shard_map/pallas_call | solution.py:101
  31.9 18.7 %all-to-all-done.x_ref = bf16[64,8,8,128]{3,2,1,0:T(8,128)(2,1)S(1)} async-done(((bf16[64,8,8,128]{3,2,1,0:T(8,128)(2,1)}), bf16[64,8,8,128]{3,2,1,0:T(8,128)(2,1)S(1)}, u32[]{:S(2)}, u32[]{:S(2)}) %all-to-all-start) | async-done | bytes 1048608 | tf_op jit(solution)/shard_map/all_to_all | solution.py:176
  50.6 0.0 copy-start
  50.6 1.1 copy-done
  51.6 9.5 %shard_map.75 = f32[64,8,1280]{2,1,0:T(8,128)} custom-call(bf16[64,8,8,128]{3,2,1,0:T(8,128)(2,1)} %copy-done, bf16[1024,1280]{1,0:T(8,128)(2,1)} %get-tuple-element.7.hi_ref, bf16[1024,1280]{1,0:T(8,128)(2,1)} %get-tuple-element.8.lo_ref), custom_call_target="tpu_custom_call" | custom-call | flops 2684354560 | bytes 10000000 | tf_op jit(solution)/shard_map/pallas_call | solution.py:134
  61.2 0.0 reduce-scatter.13.cloned.1.call-update
  61.2 0.0 reduce-scatter.15.cloned.1.call-start
  61.2 3.3 shard_map.76
  64.6 34.6 %all_to_all.20.x_ref = bf16[64,8,8,128]{3,2,1,0:T(8,128)(2,1)} all-to-all(bf16[64,8,8,128]{3,2,1,0:T(8,128)(2,1)} %shard_map.76), channel_id=1, replica_groups=mesh['pair'=64,'virt'=4] {'pair'}, dimensions={0} | all-to-all | bytes 2097152 | tf_op jit(solution)/shard_map/all_to_all | solution.py:176
  99.1 9.6 %shard_map.77 = f32[64,8,1280]{2,1,0:T(8,128)} custom-call(bf16[64,8,8,128]{3,2,1,0:T(8,128)(2,1)} %all_to_all.20.x_ref, bf16[1024,1280]{1,0:T(8,128)(2,1)} %get-tuple-element.7.hi_ref, bf16[1024,1280]{1,0:T(8,128)(2,1)} %get-tuple-element.8.lo_ref), custom_call_target="tpu_custom_call" | custom-call | flops 2684354560 | bytes 10000000 | tf_op jit(solution)/shard_map/pallas_call | solution.py:134
  108.7 0.0 reduce-scatter.15.cloned.1.call-update
  108.7 0.0 reduce-scatter.17.cloned.1.call-start
  108.8 3.2 shard_map.78
  112.0 36.4 %all_to_all.21.x_ref = bf16[64,8,8,128]{3,2,1,0:T(8,128)(2,1)} all-to-all(bf16[64,8,8,128]{3,2,1,0:T(8,128)(2,1)} %shard_map.78), channel_id=1, replica_groups=mesh['pair'=64,'virt'=4] {'pair'}, dimensions={0} | all-to-all | bytes 2097152 | tf_op jit(solution)/shard_map/all_to_all | solution.py:176
  148.4 9.6 %shard_map.79 = f32[64,8,1280]{2,1,0:T(8,128)} custom-call(bf16[64,8,8,128]{3,2,1,0:T(8,128)(2,1)} %all_to_all.21.x_ref, bf16[1024,1280]{1,0:T(8,128)(2,1)} %get-tuple-element.7.hi_ref, bf16[1024,1280]{1,0:T(8,128)(2,1)} %get-tuple-element.8.lo_ref), custom_call_target="tpu_custom_call" | custom-call | flops 2684354560 | bytes 10000000 | tf_op jit(solution)/shard_map/pallas_call | solution.py:134
  158.0 0.0 reduce-scatter.17.cloned.1.call-update
  158.1 0.0 reduce-scatter.19.cloned.1.call-start
  158.1 3.2 shard_map.80
  161.4 36.2 %all_to_all.22.x_ref = bf16[64,8,8,128]{3,2,1,0:T(8,128)(2,1)} all-to-all(bf16[64,8,8,128]{3,2,1,0:T(8,128)(2,1)} %shard_map.80), channel_id=1, replica_groups=mesh['pair'=64,'virt'=4] {'pair'}, dimensions={0} | all-to-all | bytes 2097152 | tf_op jit(solution)/shard_map/all_to_all | solution.py:176
  197.6 9.6 %shard_map.81 = f32[64,8,1280]{2,1,0:T(8,128)} custom-call(bf16[64,8,8,128]{3,2,1,0:T(8,128)(2,1)} %all_to_all.22.x_ref, bf16[1024,1280]{1,0:T(8,128)(2,1)} %get-tuple-element.7.hi_ref, bf16[1024,1280]{1,0:T(8,128)(2,1)} %get-tuple-element.8.lo_ref), custom_call_target="tpu_custom_call" | custom-call | flops 2684354560 | bytes 10000000 | tf_op jit(solution)/shard_map/pallas_call | solution.py:134
  207.1 0.0 copy-start.3
  207.1 0.0 copy-start.1
  207.1 0.0 copy-start.2
  207.2 0.0 reduce-scatter.19.cloned.1.call-update
  207.2 0.1 slice.6
  207.3 0.5 copy-done.3
  207.8 0.2 convert_reduce_fusion
  208.0 0.2 select_reduce_fusion.1
  208.2 0.0 copy-done.1
  208.2 0.2 select_reduce_fusion
  208.4 0.7 copy.14.refs_2_
  209.1 0.0 copy-done.2
  209.1 0.1 dynamic_slice.3
  209.1 0.1 broadcast_in_dim.78
  209.2 0.1 reshape.52
  209.3 0.6 broadcast_in_dim.79.refs_3_
  209.9 0.1 iota_maximum_fusion
  210.0 0.1 max.7
  210.1 0.1 min.7
  210.2 0.6 broadcast_in_dim.73.refs_1_
  210.8 0.1 tile.21
  210.8 0.6 broadcast_in_dim.80.refs_4_
  211.5 0.0 reduce-scatter.13.cloned.1.call-done
  211.5 135.8 %reduce-scatter.15.cloned.1.call-done = f32[1,8,1280]{2,1,0:T(8,128)} async-done(((f32[64,8,1280]{2,1,0:T(8,128)}), f32[1,8,1280]{2,1,0:T(8,128)}) %reduce-scatter.15.cloned.1.call-update) | async-done | bytes 40976
  347.3 145.0 %reduce-scatter.17.cloned.1.call-done = f32[1,8,1280]{2,1,0:T(8,128)} async-done(((f32[64,8,1280]{2,1,0:T(8,128)}), f32[1,8,1280]{2,1,0:T(8,128)}) %reduce-scatter.17.cloned.1.call-update) | async-done | bytes 40976
  492.2 144.8 %reduce-scatter.19.cloned.1.call-done = f32[1,8,1280]{2,1,0:T(8,128)} async-done(((f32[64,8,1280]{2,1,0:T(8,128)}), f32[1,8,1280]{2,1,0:T(8,128)}) %reduce-scatter.19.cloned.1.call-update) | async-done | bytes 40976
  637.0 0.8 maximum_bitcast_fusion
  637.9 14.2 %all_gather.3.refs_0_ = f32[4,32,1280]{2,1,0:T(8,128)} all-gather(f32[1,32,1280]{2,1,0:T(8,128)S(1)} %maximum_bitcast_fusion), channel_id=1, replica_groups=mesh['pair'=64,'virt'=4] {'virt'}, dimensions={0}, use_global_device_ids=true | all-gather | bytes 819200 | tf_op jit(solution)/shard_map/all_gather | solution.py:180
  652.1 2.2 shard_map.82
  654.2 1.0 reshape.53
  655.2 0.1 broadcast_select_fusion
  655.3 0.7 copy.15
  (10 shorter events, 0.1 us)
Async XLA Ops:
  9.8 40.8 %all-to-all-start = ((bf16[64,8,8,128]{3,2,1,0:T(8,128)(2,1)}), bf16[64,8,8,128]{3,2,1,0:T(8,128)(2,1)S(1)}, u32[]{:S(2)}, u32[]{:S(2)}) async-start(bf16[64,8,8,128]{3,2,1,0:T(8,128)(2,1)} %shard_map.73), calls=%async_computation | async-start | bytes 2097152 | tf_op jit(solution)/shard_map/all_to_all | solution.py:176
  21.8 189.7 %reduce-scatter.13.cloned.1.call-start = ((), (), s32[]{:S(2)}) async-start(), calls=%async_computation.8 | async-start | bytes 2662400
  50.6 1.1 copy-start
  61.2 286.1 %reduce-scatter.15.cloned.1.call-start = ((), (), s32[]{:S(2)}) async-start(), calls=%async_computation.9 | async-start | bytes 2662400
  108.7 383.5 %reduce-scatter.17.cloned.1.call-start = ((), (), s32[]{:S(2)}) async-start(), calls=%async_computation.10 | async-start | bytes 2662400
  158.1 478.9 %reduce-scatter.19.cloned.1.call-start = ((), (), s32[]{:S(2)}) async-start(), calls=%async_computation.11 | async-start | bytes 2662400
  207.1 0.7 copy-start.3
  207.1 1.0 copy-start.1
  207.1 1.9 copy-start.2
Sparse Core Ops, SparseCore 0:
  61.3 140.7 reduce-scatter.12
  206.3 140.9 reduce-scatter.14
  351.4 140.7 reduce-scatter.16
  496.2 140.7 reduce-scatter.18

commit v2 on v1

v2 whole, which is shorter than its diff:
```python
import jax
import jax.numpy as jnp
import numpy as np
from jax import lax
from jax.experimental import pallas as pl
from jax.experimental.pallas import tpu as pltpu
from jax.sharding import Mesh, PartitionSpec as P

ROWS = 8
LEFT = 16
COPIES = 2
LANES = 128
BF = jnp.bfloat16
F32 = jnp.float32


def params(mib=60):
    return pltpu.CompilerParams(vmem_limit_bytes=mib * 1024 * 1024)


def pair_energy(slot_pair, occ_energy):
    nocc_count = occ_energy.shape[0]
    orbital = jnp.arange(nocc_count, dtype=jnp.int32)
    starts_row = orbital * nocc_count - orbital * (orbital - 1) // 2
    row_index = jnp.sum((starts_row[None, 1:] <= slot_pair[:, None]).astype(jnp.int32), axis=1)
    same_row = orbital[None, :] == row_index[:, None]
    row_start = jnp.sum(jnp.where(same_row, starts_row[None, :], 0), axis=1)
    column_index = slot_pair - row_start + row_index
    first_energy = jnp.sum(
        jnp.where(same_row, occ_energy[None, :], jnp.zeros_like(occ_energy)[None, :]), axis=1
    )
    same_column = orbital[None, :] == column_index[:, None]
    second_energy = jnp.sum(
        jnp.where(same_column, occ_energy[None, :], jnp.zeros_like(occ_energy)[None, :]), axis=1
    )
    return (first_energy + second_energy, slot_pair >= 0)


def unique_pairs(window):
    a, b = np.triu_indices(window)
    count = -(-a.size // 256) * 256
    one = np.full((1, count), -1, np.int32)
    two = np.full((1, count), -1, np.int32)
    one[0, : a.size] = a * window + b
    two[0, : a.size] = b * window + a
    return one, two


def flatten_kernel(xs, zs, width, where_ref, x_ref, o_ref, rows, flat):
    parts, count, inner = x_ref.shape[0], x_ref.shape[3], x_ref.shape[4]
    core = where_ref[0]
    for k in range(0, inner, LANES):
        part = min(LANES, inner - k)
        for s in range(ROWS):
            rows[k // LANES, pl.ds(s * count, count), :part] = x_ref[
                lax.rem(where_ref[1] + s // COPIES, parts), 0, s % COPIES, :, k : k + part
            ].astype(F32)
    for c in range(count):
        for k in range(0, inner, LANES):
            part = min(LANES, inner - k)
            piece = rows[k // LANES, pl.ds(c, ROWS, stride=count), :]
            flat[:, c * inner + k : c * inner + k + part] = piece[:, :part]
    flat[:, count * inner :] = jnp.zeros((ROWS, flat.shape[1] - count * inner), F32)
    whole = width // LANES
    main = whole * LANES
    lane = lax.broadcasted_iota(jnp.int32, (ROWS, LANES), 1)
    for z in range(zs):
        for x in range(xs):
            base = (z * xs + x) * 2 * width
            q = x * zs + z
            for half in range(2):
                place = lax.bitwise_xor(core, half) * whole
                for t in range(whole):
                    at = base + half * width + t * LANES
                    o_ref[q, 0, place + t] = flat[:, at : at + LANES].astype(BF)
            low, high = base + main, base + width + main
            own = jnp.where(core == 0, flat[:, low : low + LANES], flat[:, high : high + LANES])
            low, high = low - LEFT, high - LEFT
            other = jnp.where(core == 0, flat[:, high : high + LANES], flat[:, low : low + LANES])
            o_ref[q, 0, 2 * whole] = jnp.where(lane < LEFT, own, other).astype(BF)


def flatten(amps, start, size, where, xs, zs):
    slots, count, inner = amps.shape
    width = count * inner // (xs * zs * 2)
    tiles = width // LANES * 2 + 1
    parts = ROWS // COPIES
    view = amps.reshape(parts, slots // ROWS, COPIES, count, inner)
    return pl.pallas_call(
        lambda *refs: flatten_kernel(xs, zs, width, *refs),
        grid_spec=pltpu.PrefetchScalarGridSpec(
            num_scalar_prefetch=1,
            grid=(size,),
            in_specs=[
                pl.BlockSpec((parts, 1, COPIES, count, inner), lambda i, where: (0, start + i, 0, 0, 0))
            ],
            out_specs=pl.BlockSpec((xs * zs, 1, tiles, ROWS, LANES), lambda i, where: (0, i, 0, 0, 0)),
            scratch_shapes=[
                pltpu.VMEM((-(-inner // LANES), ROWS * count, LANES), F32),
                pltpu.VMEM((ROWS, count * inner + 2 * LANES), F32),
            ],
        ),
        out_shape=jax.ShapeDtypeStruct((xs * zs, size, tiles, ROWS, LANES), BF),
        compiler_params=params(),
        cost_estimate=pl.CostEstimate(flops=0, bytes_accessed=8_000_000, transcendentals=0),
    )(where, view)


def fold_kernel(one_ref, two_ref, b_ref, o_ref):
    width, full = b_ref.shape
    row = lax.broadcasted_iota(jnp.int32, (full, one_ref.shape[1]), 0)
    pick = (row == one_ref[...]).astype(F32) + (row == two_ref[...]).astype(F32)
    both = jnp.dot(b_ref[...], pick.astype(BF), preferred_element_type=F32)
    rest = o_ref.shape[1] - width
    both = jnp.concatenate([both, jnp.zeros((rest, both.shape[1]), F32)], axis=0)
    hi = both.astype(BF)
    o_ref[0] = hi
    o_ref[1] = (both - hi.astype(F32)).astype(BF)


def fold(columns, one, two):
    width, full = columns.shape
    padded = width // LANES * LANES + LEFT
    count, block = one.shape[1], 256
    return pl.pallas_call(
        fold_kernel,
        grid=(count // block,),
        in_specs=[
            pl.BlockSpec((1, block), lambda i: (0, i)),
            pl.BlockSpec((1, block), lambda i: (0, i)),
            pl.BlockSpec((width, full), lambda i: (0, 0), pipeline_mode=pl.Buffered(1)),
        ],
        out_specs=pl.BlockSpec((2, padded, block), lambda i: (0, 0, i)),
        out_shape=jax.ShapeDtypeStruct((2, padded, count), BF),
        compiler_params=params(),
        cost_estimate=pl.CostEstimate(
            flops=2 * width * full * count, bytes_accessed=10_000_000, transcendentals=0
        ),
    )(one, two, columns)


def ladder_kernel(xs, where_ref, x_ref, own_ref, other_ref, *o_refs):
    chips, tiles = x_ref.shape[0], x_ref.shape[2]
    zs = chips // xs
    whole = tiles // 2
    main = whole * LANES
    start = where_ref[2]

    def rows_of(t):
        pieces = []
        for r in range(xs):
            at = pl.ds(lax.rem(start + r, xs) * zs, zs)
            pieces.append(x_ref[at, 0, t].astype(F32).reshape(zs * ROWS, LANES))
        return jnp.concatenate(pieces, axis=0).astype(BF)

    left = jnp.concatenate([rows_of(t) for t in range(whole)], axis=1)
    right = jnp.concatenate([rows_of(whole + t) for t in range(whole)], axis=1)
    rest = rows_of(2 * whole)[:, : 2 * LEFT]
    count, block = own_ref.shape[2], 256
    for n in range(0, count, block):
        at = slice(n, n + block)
        total = jnp.zeros((chips * ROWS, block), F32)
        for part in range(2):
            total += jnp.dot(left, own_ref[part, :main, at], preferred_element_type=F32)
            total += jnp.dot(right, other_ref[part, :main, at], preferred_element_type=F32)
            edge = jnp.concatenate([own_ref[part, main:, at], other_ref[part, main:, at]], axis=0)
            total += jnp.dot(rest, edge, preferred_element_type=F32)
        total = total.reshape(xs, zs, ROWS, block)
        for k, o_ref in enumerate(o_refs):
            o_ref[:, 0, :, :, at] = total[:, :, k * COPIES : (k + 1) * COPIES, :]


def ladder(panels, own, other, where, xs, ys):
    chips, size, tiles = panels.shape[:3]
    zs = chips // xs
    count = own.shape[2]
    once = pl.Buffered(1)
    return pl.pallas_call(
        lambda *refs: ladder_kernel(xs, *refs),
        grid_spec=pltpu.PrefetchScalarGridSpec(
            num_scalar_prefetch=1,
            grid=(size,),
            in_specs=[
                pl.BlockSpec((chips, 1, tiles, ROWS, LANES), lambda i, where: (0, i, 0, 0, 0)),
                pl.BlockSpec(own.shape, lambda i, where: (0, 0, 0), pipeline_mode=once),
                pl.BlockSpec(own.shape, lambda i, where: (0, 0, 0), pipeline_mode=once),
            ],
            out_specs=[
                pl.BlockSpec((xs, 1, zs, COPIES, count), lambda i, where: (0, i, 0, 0, 0))
            ] * ys,
        ),
        out_shape=[jax.ShapeDtypeStruct((xs, size, zs, COPIES, count), F32)] * ys,
        compiler_params=params(),
        cost_estimate=pl.CostEstimate(
            flops=4 * size * chips * ROWS * tiles * LANES * count,
            bytes_accessed=size * 3_000_000 + 9_000_000,
            transcendentals=0,
        ),
    )(where, panels, own, other)


def further(block, axis, hops):
    if hops == 0:
        return block
    size = lax.axis_size(axis)
    return lax.ppermute(block, axis, [(i, (i + hops) % size) for i in range(size)])


def update_kernel(place_ref, g_ref, col_ref, pair_ref, ea_ref, eb_ref, o_ref, slots_of):
    parts, rows, count = g_ref.shape
    for k in range(parts):
        slots_of[lax.rem(place_ref[0] + parts - k, parts)] = g_ref[k]
    total = slots_of[...].reshape(parts * rows, count)
    slots = parts * rows
    hi = total.astype(BF).astype(F32)
    mid = (total - hi).astype(BF).astype(F32)
    low = total - hi - mid
    split = jnp.concatenate([hi, mid, low], axis=0).astype(BF)
    row = lax.broadcasted_iota(jnp.int32, (count, col_ref.shape[1]), 0)
    pick = (row == col_ref[...]).astype(F32).astype(BF)
    wide = jnp.dot(split, pick, preferred_element_type=F32)
    residual = wide[:slots] + wide[slots : 2 * slots] + wide[2 * slots :]
    denominator = pair_ref[...] - ea_ref[...] - eb_ref[...]
    o_ref[...] = residual / denominator


def body(amps, integrals, slot_pair, occ_energy, virt_energy):
    slots = amps.shape[0]
    window = virt_energy.shape[0]
    xs, zs, ys = lax.axis_size("x"), lax.axis_size("z"), lax.axis_size("y")
    local_rows = window // ys
    one, two = unique_pairs(window)
    count = one.shape[1]
    where = jnp.stack([lax.axis_index(axis).astype(jnp.int32) for axis in ("c", "y", "x")])
    place = lax.axis_index("y").astype(jnp.int32)
    own = fold(integrals.T, jnp.asarray(one), jnp.asarray(two))
    other = lax.ppermute(own, "c", [(0, 1), (1, 0)])
    reduced = []
    start = 0
    for size in SIZES:
        flat = flatten(amps, start, size, where, xs, zs)
        start += size
        panels = lax.all_to_all(flat, ("x", "z"), 0, 0, tiled=True)
        partial = ladder(panels, own, other, where, xs, ys)
        partial = [further(block, "y", k) for k, block in enumerate(partial)]
        partial = [sum((block[r] for block in partial[1:]), partial[0][r]) for r in range(xs)]
        partial = [further(block, "x", r) for r, block in enumerate(partial)]
        reduced.append(sum(partial[1:], partial[0]))
    mine = jnp.swapaxes(jnp.concatenate(reduced, axis=0), 0, 1).reshape(zs, slots // ys, count)
    mine = jnp.sum(lax.all_to_all(mine, "z", 0, 0, tiled=True), axis=0)
    everyone = jnp.stack([further(mine, "y", k) for k in range(ys)])

    pair_sum, filled = pair_energy(slot_pair, occ_energy)
    first = place * local_rows
    a = jnp.repeat(first + jnp.arange(local_rows, dtype=jnp.int32), window)
    b = jnp.tile(jnp.arange(window, dtype=jnp.int32), local_rows)
    low, high = jnp.minimum(a, b), jnp.maximum(a, b)
    column = low * window - low * (low - 1) // 2 + high - low
    wide = local_rows * window
    full = -(-wide // LANES) * LANES
    column = jnp.pad(column, (0, full - wide), constant_values=-1)[None]
    local_energy = lax.dynamic_slice_in_dim(virt_energy, first, local_rows)
    ea = jnp.pad(jnp.repeat(local_energy, window), (0, full - wide))[None]
    eb = jnp.pad(jnp.tile(virt_energy, local_rows), (0, full - wide))[None]
    update = pl.pallas_call(
        update_kernel,
        in_specs=[pl.BlockSpec(memory_space=pltpu.SMEM)] + [pl.BlockSpec(memory_space=pltpu.VMEM)] * 5,
        out_shape=jax.ShapeDtypeStruct((slots, full), F32),
        scratch_shapes=[pltpu.VMEM(everyone.shape, F32)],
        compiler_params=params(),
    )(place[None], everyone, column, pair_sum[:, None], ea, eb)
    update = update[:, :wide].reshape(slots, local_rows, window)
    return jnp.where(filled[:, None, None], update, jnp.zeros_like(update))


SIZES = (2, 1, 1)


def solution(mesh):
    grid = Mesh(mesh.devices.reshape(8, 4, 2, mesh.shape["virt"]), ("z", "x", "c", "y"))
    placed = (P(("z", "x", "c"), "y", None), P(None, ("y", "z", "x", "c")), P(("z", "x", "c")), P(), P())
    return jax.shard_map(
        body, mesh=grid, in_specs=placed, out_specs=P(("z", "x", "c"), "y", None), check_vma=False
    )
```

time: 664 us -> 219 us (0.33)
  waiting for transfers between devices: 444 us -> 72.1 us
  blocking collectives: 121 us -> 0 us
  starting transfers between devices: 12.2 us -> 71.3 us
  between operations: 13.2 us -> 0.19 us
    unnamed x8 -> x0, waiting for transfers between devices: 426 us -> none
    all_to_all x3 -> x0, blocking collectives: 107 us -> none  [body(): lax.all_to_all(flatten(amps, chunk, pairs), 'pair', 0, 0, tiled=True)]
    ppermute x0 -> x22, starting transfers between devices: none -> 38.7 us  [the longest x21 38.7 us: further(): lax.ppermute(block, axis, [(i, (i + hops) % size) for i in range(size)])]
    all_to_all x1 -> x4, waiting for transfers between devices: 18.7 us -> 49.6 us  [the longest x3 37.2 us: body(): panels = lax.all_to_all(flat, ('x', 'z'), 0, 0, tiled=True)]
    ppermute x0 -> x22, waiting for transfers between devices: none -> 22.5 us  [the longest x21 22.5 us: further(): lax.ppermute(block, axis, [(i, (i + hops) % size) for i in range(size)])]
    all_to_all x1 -> x4, starting transfers between devices: 12 us -> 32.7 us  [the longest x3 26.6 us: body(): panels = lax.all_to_all(flat, ('x', 'z'), 0, 0, tiled=True)]
    all_gather x1 -> x0, blocking collectives: 14.2 us -> none  [body(): everyone = lax.all_gather(mine, 'virt', tiled=False)]
    pallas_call x9 -> x7, Pallas kernels: 53.5 us -> 53.4 us  [the longest x3 30.4 us: ladder(): pl.pallas_call(lambda *refs: ladder_kernel(xs, *refs), grid_spec=pltpu.Pr...]
  transfers between devices with their start and end apart: 5 -> 26, of which waited for: 4 -> 12; matrix products, arithmetic and copies ran while one was open for 1% -> 3% of each run, Pallas kernels for 7% -> 25%
where the time goes in v2:
time: 219 us; the launch traced here: 218 us
  waiting for transfers between devices  72.1 us (33%)
  starting transfers between devices  71.3 us (33%)
  Pallas kernels  63.4 us (29%)
  local copies, waits for them, and re-layouts  5.62 us (3%)
  other arithmetic  5.48 us (3%)
    ppermute x21, starting transfers between devices, further(): lax.ppermute(block, axis, [(i, (i + hops) % size) for i in range(size)])  38.7 us
    all_to_all x3, waiting for transfers between devices, body(): panels = lax.all_to_all(flat, ('x', 'z'), 0, 0, tiled=True)  37.2 us
    pallas_call x3, Pallas kernels, ladder(): pl.pallas_call(lambda *refs: ladder_kernel(xs, *refs), grid_spec=pltpu.Pr...  30.4 us
    all_to_all x3, starting transfers between devices, body(): panels = lax.all_to_all(flat, ('x', 'z'), 0, 0, tiled=True)  26.6 us
    ppermute x21, waiting for transfers between devices, further(): lax.ppermute(block, axis, [(i, (i + hops) % size) for i in range(size)])  22.5 us
    pallas_call x3, Pallas kernels, flatten(): pl.pallas_call(lambda *refs: flatten_kernel(xs, zs, width, *refs), grid_s...  21 us
    all_to_all x1, waiting for transfers between devices, body(): mine = jnp.sum(lax.all_to_all(mine, 'z', 0, 0, tiled=True), axis=0)  12.3 us
    pallas_call x1, Pallas kernels, fold(): pl.pallas_call(fold_kernel, grid=(count // block,), in_specs=[pl.BlockSpe...  9.98 us
  transfers between devices with their start and end apart: 26, of which 12 were waited for; matrix products, arithmetic and copies ran while one was open for 3% of the time, Pallas kernels for 25%

profile of v2, /device:TPU:2, one launch (start us, length us, event | category | flops | bytes accessed | tf_op | source)
XLA Modules:
  0.0 218.1 jit_solution(18138231586594794563)
XLA Ops:
  0.0 0.6 pad_add_fusion.refs_0_
  0.6 5.9 %shard_map.76 = bf16[32,1,15,8,128]{4,3,2,1,0:T(8,128)(2,1)} custom-call(s32[3]{0:T(128)} %pad_add_fusion.refs_0_, bf16[4,4,2,120,480]{4,3,2,1,0:T(8,128)(2,1)} %bitcast.57), custom_call_target="tpu_custom_call" | custom-call | bytes 8000000 | tf_op jit(solution)/shard_map/pallas_call | solution.py:89
  6.5 11.6 %all-to-all-start.1 = ((bf16[32,1,15,8,128]{4,3,2,1,0:T(8,128)(2,1)}), bf16[32,1,15,8,128]{4,3,2,1,0:T(8,128)(2,1)S(1)}, u32[]{:S(2)}, u32[]{:S(2)}) async-start(bf16[32,1,15,8,128]{4,3,2,1,0:T(8,128)(2,1)} %shard_map.76), calls=%async_computation.1 | async-start | bytes 1966080 | tf_op jit(solution)/shard_map/all_to_all | solution.py:243
  18.1 10.0 %shard_map.74.refs_2_ = bf16[2,912,1280]{2,1,0:T(8,128)(2,1)} custom-call(s32[1,1280]{1,0:T(1,128)} %constant.57.clone.one_ref, s32[1,1280]{1,0:T(1,128)} %constant.58.clone.two_ref, bf16[900,2304]{1,0:T(8,128)(2,1)} %bitcast.66), custom_call_target="tpu_custom_call" | custom-call | flops 5308416000 | bytes 10000000 | tf_op jit(solution)/shard_map/pallas_call | solution.py:125
  28.1 5.9 %shard_map.78 = bf16[32,1,15,8,128]{4,3,2,1,0:T(8,128)(2,1)} custom-call(s32[3]{0:T(128)} %pad_add_fusion.refs_0_, bf16[4,4,2,120,480]{4,3,2,1,0:T(8,128)(2,1)} %bitcast.58), custom_call_target="tpu_custom_call" | custom-call | bytes 8000000 | tf_op jit(solution)/shard_map/pallas_call | solution.py:89
  34.0 8.9 %all-to-all-done.1.refs_1_ = bf16[32,1,15,8,128]{4,3,2,1,0:T(8,128)(2,1)S(1)} async-done(((bf16[32,1,15,8,128]{4,3,2,1,0:T(8,128)(2,1)}), bf16[32,1,15,8,128]{4,3,2,1,0:T(8,128)(2,1)S(1)}, u32[]{:S(2)}, u32[]{:S(2)}) %all-to-all-start.1) | async-done | bytes 983072 | tf_op jit(solution)/shard_map/all_to_all | solution.py:243
  42.9 7.6 %all-to-all-start.2 = ((bf16[32,1,15,8,128]{4,3,2,1,0:T(8,128)(2,1)}), bf16[32,1,15,8,128]{4,3,2,1,0:T(8,128)(2,1)S(1)}, u32[]{:S(2)}, u32[]{:S(2)}) async-start(bf16[32,1,15,8,128]{4,3,2,1,0:T(8,128)(2,1)} %shard_map.78), calls=%async_computation.2 | async-start | bytes 1966080 | tf_op jit(solution)/shard_map/all_to_all | solution.py:243
  50.4 9.2 %shard_map.73 = bf16[32,2,15,8,128]{4,3,2,1,0:T(8,128)(2,1)} custom-call(s32[3]{0:T(128)} %pad_add_fusion.refs_0_, bf16[4,4,2,120,480]{4,3,2,1,0:T(8,128)(2,1)} %bitcast.59), custom_call_target="tpu_custom_call" | custom-call | bytes 8000000 | tf_op jit(solution)/shard_map/pallas_call | solution.py:89
  59.6 15.3 %all-to-all-done.2.refs_1_ = bf16[32,1,15,8,128]{4,3,2,1,0:T(8,128)(2,1)S(1)} async-done(((bf16[32,1,15,8,128]{4,3,2,1,0:T(8,128)(2,1)}), bf16[32,1,15,8,128]{4,3,2,1,0:T(8,128)(2,1)S(1)}, u32[]{:S(2)}, u32[]{:S(2)}) %all-to-all-start.2) | async-done | bytes 983072 | tf_op jit(solution)/shard_map/all_to_all | solution.py:243
  74.9 7.4 %all-to-all-start = ((bf16[32,2,15,8,128]{4,3,2,1,0:T(8,128)(2,1)}), bf16[32,2,15,8,128]{4,3,2,1,0:T(8,128)(2,1)}, u32[]{:S(2)}, u32[]{:S(2)}) async-start(bf16[32,2,15,8,128]{4,3,2,1,0:T(8,128)(2,1)} %shard_map.73), calls=%async_computation | async-start | bytes 3932160 | tf_op jit(solution)/shard_map/all_to_all | solution.py:243
  82.4 0.2 convert_reduce_fusion
  82.6 9.0 %shard_map.77 = (f32[4,1,8,2,1280]{4,3,2,1,0:T(2,128)}, f32[4,1,8,2,1280]{4,3,2,1,0:T(2,128)}, f32[4,1,8,2,1280]{4,3,2,1,0:T(2,128)}, f32[4,1,8,2,1280]{4,3,2,1,0:T(2,128)}) custom-call(s32[3]{0:T(128)} %pad_add_fusion.refs_0_, bf16[32,1,15,8,128]{4,3,2,1,0:T(8,128)(2,1)} %copy-done.1, bf16[2,912,1280]{2,1,0:T(8,128)(2,1)} %shard_map.74.refs_2_, ...), custom_call_target="tpu_custom_call" | custom-call | flops 2516582400 | bytes 12000000 | tf_op jit(solution)/shard_map/pallas_call | solution.py:178
  91.6 1.6 collective-permute-start.7
  93.2 2.9 %collective-permute-start.8 = (f32[4,1,8,2,1280]{4,3,2,1,0:T(2,128)}, f32[4,1,8,2,1280]{4,3,2,1,0:T(2,128)S(1)}, u32[]{:S(2)}, u32[]{:S(2)}) collective-permute-start(f32[4,1,8,2,1280]{4,3,2,1,0:T(2,128)} %get-tuple-element.23), channel_id=1, source_target_pairs={{0,2},{1,3},{2,0},{3,1},{4,6},{5,7},{6,4},{7,5},{8,10},{9,11},{10,... | collective-permute-start | bytes 983048 | tf_op jit(solution)/shard_map/ppermute | solution.py:206
  96.1 1.3 collective-permute-start.9
  97.5 0.2 select_reduce_fusion.1
  97.6 9.1 %shard_map.79 = (f32[4,1,8,2,1280]{4,3,2,1,0:T(2,128)}, f32[4,1,8,2,1280]{4,3,2,1,0:T(2,128)}, f32[4,1,8,2,1280]{4,3,2,1,0:T(2,128)}, f32[4,1,8,2,1280]{4,3,2,1,0:T(2,128)}) custom-call(s32[3]{0:T(128)} %pad_add_fusion.refs_0_, bf16[32,1,15,8,128]{4,3,2,1,0:T(8,128)(2,1)} %copy-done, bf16[2,912,1280]{2,1,0:T(8,128)(2,1)} %shard_map.74.refs_2_, ...), custom_call_target="tpu_custom_call" | custom-call | flops 2516582400 | bytes 12000000 | tf_op jit(solution)/shard_map/pallas_call | solution.py:178
  106.8 0.7 collective-permute-start.13
  107.5 0.8 collective-permute-start.14
  108.2 1.9 collective-permute-start.15
  110.1 1.8 collective-permute-done.8
  111.9 0.2 fusion.16
  112.1 1.5 collective-permute-start.10
  113.7 13.1 %all-to-all-done.refs_1_ = bf16[32,2,15,8,128]{4,3,2,1,0:T(8,128)(2,1)} async-done(((bf16[32,2,15,8,128]{4,3,2,1,0:T(8,128)(2,1)}), bf16[32,2,15,8,128]{4,3,2,1,0:T(8,128)(2,1)}, u32[]{:S(2)}, u32[]{:S(2)}) %all-to-all-start) | async-done | bytes 1966112 | tf_op jit(solution)/shard_map/all_to_all | solution.py:243
  126.7 12.3 %shard_map.75 = (f32[4,2,8,2,1280]{4,3,2,1,0:T(2,128)}, f32[4,2,8,2,1280]{4,3,2,1,0:T(2,128)}, f32[4,2,8,2,1280]{4,3,2,1,0:T(2,128)}, f32[4,2,8,2,1280]{4,3,2,1,0:T(2,128)}) custom-call(s32[3]{0:T(128)} %pad_add_fusion.refs_0_, bf16[32,2,15,8,128]{4,3,2,1,0:T(8,128)(2,1)} %all-to-all-done.refs_1_, bf16[2,912,1280]{2,1,0:T(8,128)(2,1)} %shard_map.74.refs_2_, ...), custom_call_target="tpu_custom_call" | custom-call | flops 5033164800 | bytes 15000000 | tf_op jit(solution)/shard_map/pallas_call | solution.py:178
  139.0 1.6 collective-permute-start.1
  140.6 2.9 %collective-permute-start.2 = (f32[4,2,8,2,1280]{4,3,2,1,0:T(2,128)}, f32[4,2,8,2,1280]{4,3,2,1,0:T(2,128)S(1)}, u32[]{:S(2)}, u32[]{:S(2)}) collective-permute-start(f32[4,2,8,2,1280]{4,3,2,1,0:T(2,128)} %get-tuple-element.19), channel_id=1, source_target_pairs={{0,2},{1,3},{2,0},{3,1},{4,6},{5,7},{6,4},{7,5},{8,10},{9,11},{10,... | collective-permute-start | bytes 1966088 | tf_op jit(solution)/shard_map/ppermute | solution.py:206
  143.5 1.3 collective-permute-start.3
  144.9 2.4 %collective-permute-start.11 = (f32[1,8,2,1280]{3,2,1,0:T(2,128)S(1)}, f32[1,8,2,1280]{3,2,1,0:T(2,128)S(1)}, u32[]{:S(2)}, u32[]{:S(2)}) collective-permute-start(f32[1,8,2,1280]{3,2,1,0:T(2,128)S(1)} %get-tuple-element.36), channel_id=1, source_target_pairs={{0,16},{8,24},{16,0},{24,8},{1,17},{9,25},{17,1},{25,9},{2,18},{10... | collective-permute-start | bytes 245768 | tf_op jit(solution)/shard_map/ppermute | solution.py:206
  147.3 1.2 collective-permute-start.12
  148.5 0.2 fusion.9
  148.7 2.1 collective-permute-done.11
  150.8 1.7 collective-permute-start.16
  152.5 4.2 %collective-permute-start.17 = (f32[1,8,2,1280]{3,2,1,0:T(2,128)S(1)}, f32[1,8,2,1280]{3,2,1,0:T(2,128)S(1)}, u32[]{:S(2)}, u32[]{:S(2)}) collective-permute-start(f32[1,8,2,1280]{3,2,1,0:T(2,128)S(1)} %get-tuple-element.39), channel_id=1, source_target_pairs={{0,16},{8,24},{16,0},{24,8},{1,17},{9,25},{17,1},{25,9},{2,18},{10... | collective-permute-start | bytes 245768 | tf_op jit(solution)/shard_map/ppermute | solution.py:206
  156.7 0.1 fusion.20
  156.8 0.2 collective-permute-done.1
  156.9 2.8 %collective-permute-start.18 = (f32[1,8,2,1280]{3,2,1,0:T(2,128)S(1)}, f32[1,8,2,1280]{3,2,1,0:T(2,128)S(1)}, u32[]{:S(2)}, u32[]{:S(2)}) collective-permute-start(f32[1,8,2,1280]{3,2,1,0:T(2,128)S(1)} %get-tuple-element.38), channel_id=1, source_target_pairs={{0,24},{8,0},{16,8},{24,16},{1,25},{9,1},{17,9},{25,17},{2,26},{10... | collective-permute-start | bytes 245768 | tf_op jit(solution)/shard_map/ppermute | solution.py:206
  159.7 11.4 %collective-permute-done.2 = f32[4,2,8,2,1280]{4,3,2,1,0:T(2,128)S(1)} collective-permute-done((f32[4,2,8,2,1280]{4,3,2,1,0:T(2,128)}, f32[4,2,8,2,1280]{4,3,2,1,0:T(2,128)S(1)}, u32[]{:S(2)}, u32[]{:S(2)}) %collective-permute-start.2) | collective-permute-done | bytes 655392 | tf_op jit(solution)/shard_map/ppermute | solution.py:206
  171.1 1.5 fusion.2
  172.6 1.1 collective-permute-start.4
  173.7 3.4 %collective-permute-start.5 = (f32[2,8,2,1280]{3,2,1,0:T(2,128)S(1)}, f32[2,8,2,1280]{3,2,1,0:T(2,128)S(1)}, u32[]{:S(2)}, u32[]{:S(2)}) collective-permute-start(f32[2,8,2,1280]{3,2,1,0:T(2,128)S(1)} %get-tuple-element.33), channel_id=1, source_target_pairs={{0,16},{8,24},{16,0},{24,8},{1,17},{9,25},{17,1},{25,9},{2,18},{10... | collective-permute-start | bytes 491528 | tf_op jit(solution)/shard_map/ppermute | solution.py:206
  177.1 0.2 collective-permute-start.6
  177.2 0.1 fusion.13
  177.4 2.3 %collective-permute-done.4 = f32[2,8,2,1280]{3,2,1,0:T(2,128)S(1)} collective-permute-done((f32[2,8,2,1280]{3,2,1,0:T(2,128)S(1)}, f32[2,8,2,1280]{3,2,1,0:T(2,128)S(1)}, u32[]{:S(2)}, u32[]{:S(2)}) %collective-permute-start.4) | collective-permute-done | bytes 163872 | tf_op jit(solution)/shard_map/ppermute | solution.py:206
  179.7 1.9 collective-permute-done.5
  181.6 1.7 collective-permute-done.6
  183.2 1.1 fusion.6
  184.4 0.2 maximum_bitcast_fusion
  184.6 0.8 copy.18
  185.4 6.1 %all-to-all-start.3 = ((f32[8,8,1280]{2,1,0:T(8,128)}), f32[8,8,1280]{2,1,0:T(8,128)S(1)}, u32[]{:S(2)}, u32[]{:S(2)}) async-start(f32[8,8,1280]{2,1,0:T(8,128)} %copy.18), calls=%async_computation.3 | async-start | bytes 655360 | tf_op jit(solution)/shard_map/all_to_all | solution.py:250
  191.7 0.2 select_reduce_fusion
  191.9 12.3 %all-to-all-done.3 = f32[8,8,1280]{2,1,0:T(8,128)S(1)} async-done(((f32[8,8,1280]{2,1,0:T(8,128)}), f32[8,8,1280]{2,1,0:T(8,128)S(1)}, u32[]{:S(2)}, u32[]{:S(2)}) %all-to-all-start.3) | async-done | bytes 327712 | tf_op jit(solution)/shard_map/all_to_all | solution.py:250
  204.2 2.0 collective-permute-start.19
  206.3 3.3 %collective-permute-start.20 = (f32[8,1280]{1,0:T(8,128)S(1)}, f32[8,1280]{1,0:T(8,128)S(1)}, u32[]{:S(2)}, u32[]{:S(2)}) collective-permute-start(f32[8,1280]{1,0:T(8,128)S(1)} %reduce_sum.45), channel_id=1, source_target_pairs={{0,2},{1,3},{2,0},{3,1},{4,6},{5,7},{6,4},{7,5},{8,10},{9,11},{10,... | collective-permute-start | bytes 122888 | tf_op jit(solution)/shard_map/ppermute | solution.py:206
  209.5 0.7 copy.19.pair_ref
  210.5 0.6 broadcast_in_dim.83.ea_ref
  211.1 0.6 broadcast_in_dim.77.col_ref
  211.7 0.6 broadcast_in_dim.84.eb_ref
  212.3 1.2 collective-permute-done.21
  213.5 0.7 pad_maximum_fusion.g_ref
  214.2 2.0 shard_map.80
  216.2 1.0 reshape.451
  217.2 0.1 broadcast_select_fusion
  217.3 0.7 copy.20
  (50 shorter events, 0.8 us)
Async XLA Ops:
  6.5 36.4 %all-to-all-start.1 = ((bf16[32,1,15,8,128]{4,3,2,1,0:T(8,128)(2,1)}), bf16[32,1,15,8,128]{4,3,2,1,0:T(8,128)(2,1)S(1)}, u32[]{:S(2)}, u32[]{:S(2)}) async-start(bf16[32,1,15,8,128]{4,3,2,1,0:T(8,128)(2,1)} %shard_map.76), calls=%async_computation.1 | async-start | bytes 1966080 | tf_op jit(solution)/shard_map/all_to_all | solution.py:243
  28.1 54.5 %collective-permute-start = (bf16[2,912,1280]{2,1,0:T(8,128)(2,1)}, bf16[2,912,1280]{2,1,0:T(8,128)(2,1)}, u32[]{:S(2)}, u32[]{:S(2)}) collective-permute-start(bf16[2,912,1280]{2,1,0:T(8,128)(2,1)} %shard_map.74.refs_2_), channel_id=1, source_target_pairs={{0,4},{4,0},{1,5},{5,1},{2,6},{6,2},{3,7},{7,3},{8,12},{12,8},{9,1... | collective-permute-start | bytes 14008328 | tf_op jit(solution)/shard_map/ppermute | solution.py:237
  42.9 32.0 %copy-start.1 = (bf16[32,1,15,8,128]{4,3,2,1,0:T(8,128)(2,1)}, bf16[32,1,15,8,128]{4,3,2,1,0:T(8,128)(2,1)S(1)}, u32[]{:S(2)}) copy-start(bf16[32,1,15,8,128]{4,3,2,1,0:T(8,128)(2,1)S(1)} %all-to-all-done.1.refs_1_) | copy-start | bytes 2949124
  42.9 32.0 %all-to-all-start.2 = ((bf16[32,1,15,8,128]{4,3,2,1,0:T(8,128)(2,1)}), bf16[32,1,15,8,128]{4,3,2,1,0:T(8,128)(2,1)S(1)}, u32[]{:S(2)}, u32[]{:S(2)}) async-start(bf16[32,1,15,8,128]{4,3,2,1,0:T(8,128)(2,1)} %shard_map.78), calls=%async_computation.2 | async-start | bytes 1966080 | tf_op jit(solution)/shard_map/all_to_all | solution.py:243
  50.4 32.0 %copy-start.6 = (s32[32]{0:T(128)S(1)}, s32[32]{0:T(128)}, u32[]{:S(2)}) copy-start(s32[32]{0:T(128)} %param.9) | copy-start | bytes 388
  74.9 16.7 %copy-start = (bf16[32,1,15,8,128]{4,3,2,1,0:T(8,128)(2,1)}, bf16[32,1,15,8,128]{4,3,2,1,0:T(8,128)(2,1)S(1)}, u32[]{:S(2)}) copy-start(bf16[32,1,15,8,128]{4,3,2,1,0:T(8,128)(2,1)S(1)} %all-to-all-done.2.refs_1_) | copy-start | bytes 2949124
  74.9 51.9 %all-to-all-start = ((bf16[32,2,15,8,128]{4,3,2,1,0:T(8,128)(2,1)}), bf16[32,2,15,8,128]{4,3,2,1,0:T(8,128)(2,1)}, u32[]{:S(2)}, u32[]{:S(2)}) async-start(bf16[32,2,15,8,128]{4,3,2,1,0:T(8,128)(2,1)} %shard_map.73), calls=%async_computation | async-start | bytes 3932160 | tf_op jit(solution)/shard_map/all_to_all | solution.py:243
  91.6 16.6 %collective-permute-start.7 = (f32[4,1,8,2,1280]{4,3,2,1,0:T(2,128)}, f32[4,1,8,2,1280]{4,3,2,1,0:T(2,128)S(1)}, u32[]{:S(2)}, u32[]{:S(2)}) collective-permute-start(f32[4,1,8,2,1280]{4,3,2,1,0:T(2,128)} %get-tuple-element.22), channel_id=1, source_target_pairs={{0,1},{1,2},{2,3},{3,0},{4,5},{5,6},{6,7},{7,4},{8,9},{9,10},{10,1... | collective-permute-start | bytes 983048 | tf_op jit(solution)/shard_map/ppermute | solution.py:206
  93.2 18.7 %collective-permute-start.8 = (f32[4,1,8,2,1280]{4,3,2,1,0:T(2,128)}, f32[4,1,8,2,1280]{4,3,2,1,0:T(2,128)S(1)}, u32[]{:S(2)}, u32[]{:S(2)}) collective-permute-start(f32[4,1,8,2,1280]{4,3,2,1,0:T(2,128)} %get-tuple-element.23), channel_id=1, source_target_pairs={{0,2},{1,3},{2,0},{3,1},{4,6},{5,7},{6,4},{7,5},{8,10},{9,11},{10,... | collective-permute-start | bytes 983048 | tf_op jit(solution)/shard_map/ppermute | solution.py:206
  96.1 15.8 %collective-permute-start.9 = (f32[4,1,8,2,1280]{4,3,2,1,0:T(2,128)}, f32[4,1,8,2,1280]{4,3,2,1,0:T(2,128)S(1)}, u32[]{:S(2)}, u32[]{:S(2)}) collective-permute-start(f32[4,1,8,2,1280]{4,3,2,1,0:T(2,128)} %get-tuple-element.24), channel_id=1, source_target_pairs={{0,3},{1,0},{2,1},{3,2},{4,7},{5,4},{6,5},{7,6},{8,11},{9,8},{10,9... | collective-permute-start | bytes 983048 | tf_op jit(solution)/shard_map/ppermute | solution.py:206
  97.6 14.3 %copy-start.3 = (f32[4,1,8,2,1280]{4,3,2,1,0:T(2,128)S(1)}, f32[4,1,8,2,1280]{4,3,2,1,0:T(2,128)}, u32[]{:S(2)}) copy-start(f32[4,1,8,2,1280]{4,3,2,1,0:T(2,128)} %get-tuple-element.21) | copy-start | bytes 983044
  106.8 33.8 %collective-permute-start.13 = (f32[4,1,8,2,1280]{4,3,2,1,0:T(2,128)}, f32[4,1,8,2,1280]{4,3,2,1,0:T(2,128)S(1)}, u32[]{:S(2)}, u32[]{:S(2)}) collective-permute-start(f32[4,1,8,2,1280]{4,3,2,1,0:T(2,128)} %get-tuple-element.26), channel_id=1, source_target_pairs={{0,1},{1,2},{2,3},{3,0},{4,5},{5,6},{6,7},{7,4},{8,9},{9,10},{10,1... | collective-permute-start | bytes 983048 | tf_op jit(solution)/shard_map/ppermute | solution.py:206
  107.5 36.1 %collective-permute-start.14 = (f32[4,1,8,2,1280]{4,3,2,1,0:T(2,128)}, f32[4,1,8,2,1280]{4,3,2,1,0:T(2,128)S(1)}, u32[]{:S(2)}, u32[]{:S(2)}) collective-permute-start(f32[4,1,8,2,1280]{4,3,2,1,0:T(2,128)} %get-tuple-element.27), channel_id=1, source_target_pairs={{0,2},{1,3},{2,0},{3,1},{4,6},{5,7},{6,4},{7,5},{8,10},{9,11},{10,... | collective-permute-start | bytes 983048 | tf_op jit(solution)/shard_map/ppermute | solution.py:206
  108.2 36.6 %collective-permute-start.15 = (f32[4,1,8,2,1280]{4,3,2,1,0:T(2,128)}, f32[4,1,8,2,1280]{4,3,2,1,0:T(2,128)S(1)}, u32[]{:S(2)}, u32[]{:S(2)}) collective-permute-start(f32[4,1,8,2,1280]{4,3,2,1,0:T(2,128)} %get-tuple-element.28), channel_id=1, source_target_pairs={{0,3},{1,0},{2,1},{3,2},{4,7},{5,4},{6,5},{7,6},{8,11},{9,8},{10,9... | collective-permute-start | bytes 983048 | tf_op jit(solution)/shard_map/ppermute | solution.py:206
  112.1 36.3 %copy-start.2 = (f32[4,1,8,2,1280]{4,3,2,1,0:T(2,128)S(1)}, f32[4,1,8,2,1280]{4,3,2,1,0:T(2,128)}, u32[]{:S(2)}) copy-start(f32[4,1,8,2,1280]{4,3,2,1,0:T(2,128)} %get-tuple-element.25) | copy-start | bytes 983044
  112.1 35.2 %collective-permute-start.10 = (f32[1,8,2,1280]{3,2,1,0:T(2,128)S(1)}, f32[1,8,2,1280]{3,2,1,0:T(2,128)S(1)}, u32[]{:S(2)}, u32[]{:S(2)}) collective-permute-start(f32[1,8,2,1280]{3,2,1,0:T(2,128)S(1)} %get-tuple-element.34), channel_id=1, source_target_pairs={{0,8},{8,16},{16,24},{24,0},{1,9},{9,17},{17,25},{25,1},{2,10},{10... | collective-permute-start | bytes 245768 | tf_op jit(solution)/shard_map/ppermute | solution.py:206
  139.0 17.9 %collective-permute-start.1 = (f32[4,2,8,2,1280]{4,3,2,1,0:T(2,128)}, f32[4,2,8,2,1280]{4,3,2,1,0:T(2,128)S(1)}, u32[]{:S(2)}, u32[]{:S(2)}) collective-permute-start(f32[4,2,8,2,1280]{4,3,2,1,0:T(2,128)} %get-tuple-element.18), channel_id=1, source_target_pairs={{0,1},{1,2},{2,3},{3,0},{4,5},{5,6},{6,7},{7,4},{8,9},{9,10},{10,1... | collective-permute-start | bytes 1966088 | tf_op jit(solution)/shard_map/ppermute | solution.py:206
  140.6 30.5 %collective-permute-start.2 = (f32[4,2,8,2,1280]{4,3,2,1,0:T(2,128)}, f32[4,2,8,2,1280]{4,3,2,1,0:T(2,128)S(1)}, u32[]{:S(2)}, u32[]{:S(2)}) collective-permute-start(f32[4,2,8,2,1280]{4,3,2,1,0:T(2,128)} %get-tuple-element.19), channel_id=1, source_target_pairs={{0,2},{1,3},{2,0},{3,1},{4,6},{5,7},{6,4},{7,5},{8,10},{9,11},{10,... | collective-permute-start | bytes 1966088 | tf_op jit(solution)/shard_map/ppermute | solution.py:206
  143.5 27.6 %collective-permute-start.3 = (f32[4,2,8,2,1280]{4,3,2,1,0:T(2,128)}, f32[4,2,8,2,1280]{4,3,2,1,0:T(2,128)S(1)}, u32[]{:S(2)}, u32[]{:S(2)}) collective-permute-start(f32[4,2,8,2,1280]{4,3,2,1,0:T(2,128)} %get-tuple-element.20), channel_id=1, source_target_pairs={{0,3},{1,0},{2,1},{3,2},{4,7},{5,4},{6,5},{7,6},{8,11},{9,8},{10,9... | collective-permute-start | bytes 1966088 | tf_op jit(solution)/shard_map/ppermute | solution.py:206
  144.9 5.9 %collective-permute-start.11 = (f32[1,8,2,1280]{3,2,1,0:T(2,128)S(1)}, f32[1,8,2,1280]{3,2,1,0:T(2,128)S(1)}, u32[]{:S(2)}, u32[]{:S(2)}) collective-permute-start(f32[1,8,2,1280]{3,2,1,0:T(2,128)S(1)} %get-tuple-element.36), channel_id=1, source_target_pairs={{0,16},{8,24},{16,0},{24,8},{1,17},{9,25},{17,1},{25,9},{2,18},{10... | collective-permute-start | bytes 245768 | tf_op jit(solution)/shard_map/ppermute | solution.py:206
  147.3 5.2 %collective-permute-start.12 = (f32[1,8,2,1280]{3,2,1,0:T(2,128)S(1)}, f32[1,8,2,1280]{3,2,1,0:T(2,128)S(1)}, u32[]{:S(2)}, u32[]{:S(2)}) collective-permute-start(f32[1,8,2,1280]{3,2,1,0:T(2,128)S(1)} %get-tuple-element.35), channel_id=1, source_target_pairs={{0,24},{8,0},{16,8},{24,16},{1,25},{9,1},{17,9},{25,17},{2,26},{10... | collective-permute-start | bytes 245768 | tf_op jit(solution)/shard_map/ppermute | solution.py:206
  148.7 43.0 %copy-start.4 = (f32[48]{0:T(128)S(1)}, f32[48]{0:T(128)}, u32[]{:S(2)}) copy-start(f32[48]{0:T(128)} %param.10) | copy-start | bytes 580
  148.7 61.5 %copy-start.5 = (f32[48]{0:T(128)S(1)}, f32[48]{0:T(128)}, u32[]{:S(2)}) copy-start(f32[48]{0:T(128)} %param.11) | copy-start | bytes 580
  150.8 26.2 %collective-permute-start.16 = (f32[1,8,2,1280]{3,2,1,0:T(2,128)S(1)}, f32[1,8,2,1280]{3,2,1,0:T(2,128)S(1)}, u32[]{:S(2)}, u32[]{:S(2)}) collective-permute-start(f32[1,8,2,1280]{3,2,1,0:T(2,128)S(1)} %get-tuple-element.37), channel_id=1, source_target_pairs={{0,8},{8,16},{16,24},{24,0},{1,9},{9,17},{17,25},{25,1},{2,10},{10... | collective-permute-start | bytes 245768 | tf_op jit(solution)/shard_map/ppermute | solution.py:206
  152.5 24.7 %collective-permute-start.17 = (f32[1,8,2,1280]{3,2,1,0:T(2,128)S(1)}, f32[1,8,2,1280]{3,2,1,0:T(2,128)S(1)}, u32[]{:S(2)}, u32[]{:S(2)}) collective-permute-start(f32[1,8,2,1280]{3,2,1,0:T(2,128)S(1)} %get-tuple-element.39), channel_id=1, source_target_pairs={{0,16},{8,24},{16,0},{24,8},{1,17},{9,25},{17,1},{25,9},{2,18},{10... | collective-permute-start | bytes 245768 | tf_op jit(solution)/shard_map/ppermute | solution.py:206
  156.9 20.3 %collective-permute-start.18 = (f32[1,8,2,1280]{3,2,1,0:T(2,128)S(1)}, f32[1,8,2,1280]{3,2,1,0:T(2,128)S(1)}, u32[]{:S(2)}, u32[]{:S(2)}) collective-permute-start(f32[1,8,2,1280]{3,2,1,0:T(2,128)S(1)} %get-tuple-element.38), channel_id=1, source_target_pairs={{0,24},{8,0},{16,8},{24,16},{1,25},{9,1},{17,9},{25,17},{2,26},{10... | collective-permute-start | bytes 245768 | tf_op jit(solution)/shard_map/ppermute | solution.py:206
  172.6 7.1 %collective-permute-start.4 = (f32[2,8,2,1280]{3,2,1,0:T(2,128)S(1)}, f32[2,8,2,1280]{3,2,1,0:T(2,128)S(1)}, u32[]{:S(2)}, u32[]{:S(2)}) collective-permute-start(f32[2,8,2,1280]{3,2,1,0:T(2,128)S(1)} %get-tuple-element.31), channel_id=1, source_target_pairs={{0,8},{8,16},{16,24},{24,0},{1,9},{9,17},{17,25},{25,1},{2,10},{10... | collective-permute-start | bytes 491528 | tf_op jit(solution)/shard_map/ppermute | solution.py:206
  173.7 7.9 %collective-permute-start.5 = (f32[2,8,2,1280]{3,2,1,0:T(2,128)S(1)}, f32[2,8,2,1280]{3,2,1,0:T(2,128)S(1)}, u32[]{:S(2)}, u32[]{:S(2)}) collective-permute-start(f32[2,8,2,1280]{3,2,1,0:T(2,128)S(1)} %get-tuple-element.33), channel_id=1, source_target_pairs={{0,16},{8,24},{16,0},{24,8},{1,17},{9,25},{17,1},{25,9},{2,18},{10... | collective-permute-start | bytes 491528 | tf_op jit(solution)/shard_map/ppermute | solution.py:206
  177.1 6.2 %collective-permute-start.6 = (f32[2,8,2,1280]{3,2,1,0:T(2,128)S(1)}, f32[2,8,2,1280]{3,2,1,0:T(2,128)S(1)}, u32[]{:S(2)}, u32[]{:S(2)}) collective-permute-start(f32[2,8,2,1280]{3,2,1,0:T(2,128)S(1)} %get-tuple-element.32), channel_id=1, source_target_pairs={{0,24},{8,0},{16,8},{24,16},{1,25},{9,1},{17,9},{25,17},{2,26},{10... | collective-permute-start | bytes 491528 | tf_op jit(solution)/shard_map/ppermute | solution.py:206
  185.4 18.8 %all-to-all-start.3 = ((f32[8,8,1280]{2,1,0:T(8,128)}), f32[8,8,1280]{2,1,0:T(8,128)S(1)}, u32[]{:S(2)}, u32[]{:S(2)}) async-start(f32[8,8,1280]{2,1,0:T(8,128)} %copy.18), calls=%async_computation.3 | async-start | bytes 655360 | tf_op jit(solution)/shard_map/all_to_all | solution.py:250
  204.2 8.1 %collective-permute-start.19 = (f32[8,1280]{1,0:T(8,128)S(1)}, f32[8,1280]{1,0:T(8,128)S(1)}, u32[]{:S(2)}, u32[]{:S(2)}) collective-permute-start(f32[8,1280]{1,0:T(8,128)S(1)} %reduce_sum.45), channel_id=1, source_target_pairs={{0,1},{1,2},{2,3},{3,0},{4,5},{5,6},{6,7},{7,4},{8,9},{9,10},{10,1... | collective-permute-start | bytes 122888 | tf_op jit(solution)/shard_map/ppermute | solution.py:206
  206.3 6.1 %collective-permute-start.20 = (f32[8,1280]{1,0:T(8,128)S(1)}, f32[8,1280]{1,0:T(8,128)S(1)}, u32[]{:S(2)}, u32[]{:S(2)}) collective-permute-start(f32[8,1280]{1,0:T(8,128)S(1)} %reduce_sum.45), channel_id=1, source_target_pairs={{0,2},{1,3},{2,0},{3,1},{4,6},{5,7},{6,4},{7,5},{8,10},{9,11},{10,... | collective-permute-start | bytes 122888 | tf_op jit(solution)/shard_map/ppermute | solution.py:206
  209.5 4.0 %collective-permute-start.21 = (f32[8,1280]{1,0:T(8,128)S(1)}, f32[8,1280]{1,0:T(8,128)S(1)}, u32[]{:S(2)}, u32[]{:S(2)}) collective-permute-start(f32[8,1280]{1,0:T(8,128)S(1)} %reduce_sum.45), channel_id=1, source_target_pairs={{0,3},{1,0},{2,1},{3,2},{4,7},{5,4},{6,5},{7,6},{8,11},{9,8},{10,9... | collective-permute-start | bytes 122888 | tf_op jit(solution)/shard_map/ppermute | solution.py:206

commit v3 on v2

--- a/solution.py
+++ b/solution.py
@@ -14,7 +14,7 @@
 F32 = jnp.float32
 
 
-def params(mib=60):
+def params(mib=40):
     return pltpu.CompilerParams(vmem_limit_bytes=mib * 1024 * 1024)
 
 
@@ -48,7 +48,6 @@
 
 def flatten_kernel(xs, zs, width, where_ref, x_ref, o_ref, rows, flat):
     parts, count, inner = x_ref.shape[0], x_ref.shape[3], x_ref.shape[4]
-    core = where_ref[0]
     for k in range(0, inner, LANES):
         part = min(LANES, inner - k)
         for s in range(ROWS):
@@ -69,15 +68,12 @@
             base = (z * xs + x) * 2 * width
             q = x * zs + z
             for half in range(2):
-                place = lax.bitwise_xor(core, half) * whole
                 for t in range(whole):
                     at = base + half * width + t * LANES
-                    o_ref[q, 0, place + t] = flat[:, at : at + LANES].astype(BF)
-            low, high = base + main, base + width + main
-            own = jnp.where(core == 0, flat[:, low : low + LANES], flat[:, high : high + LANES])
-            low, high = low - LEFT, high - LEFT
-            other = jnp.where(core == 0, flat[:, high : high + LANES], flat[:, low : low + LANES])
-            o_ref[q, 0, 2 * whole] = jnp.where(lane < LEFT, own, other).astype(BF)
+                    o_ref[q, 0, half * whole + t] = flat[:, at : at + LANES].astype(BF)
+            low, high = base + main, base + width + main - LEFT
+            edge = jnp.where(lane < LEFT, flat[:, low : low + LANES], flat[:, high : high + LANES])
+            o_ref[q, 0, 2 * whole] = edge.astype(BF)
 
 
 def flatten(amps, start, size, where, xs, zs):
@@ -139,55 +135,62 @@
     )(one, two, columns)
 
 
-def ladder_kernel(xs, where_ref, x_ref, own_ref, other_ref, *o_refs):
+def ladder_kernel(xs, where_ref, x_ref, own_ref, other_ref, *refs):
+    o_refs, lhs = refs[:-1], refs[-1]
     chips, tiles = x_ref.shape[0], x_ref.shape[2]
     zs = chips // xs
     whole = tiles // 2
     main = whole * LANES
-    start = where_ref[2]
-
-    def rows_of(t):
-        pieces = []
-        for r in range(xs):
-            at = pl.ds(lax.rem(start + r, xs) * zs, zs)
-            pieces.append(x_ref[at, 0, t].astype(F32).reshape(zs * ROWS, LANES))
-        return jnp.concatenate(pieces, axis=0).astype(BF)
-
-    left = jnp.concatenate([rows_of(t) for t in range(whole)], axis=1)
-    right = jnp.concatenate([rows_of(whole + t) for t in range(whole)], axis=1)
-    rest = rows_of(2 * whole)[:, : 2 * LEFT]
-    count, block = own_ref.shape[2], 256
-    for n in range(0, count, block):
-        at = slice(n, n + block)
-        total = jnp.zeros((chips * ROWS, block), F32)
-        for part in range(2):
-            total += jnp.dot(left, own_ref[part, :main, at], preferred_element_type=F32)
-            total += jnp.dot(right, other_ref[part, :main, at], preferred_element_type=F32)
-            edge = jnp.concatenate([own_ref[part, main:, at], other_ref[part, main:, at]], axis=0)
-            total += jnp.dot(rest, edge, preferred_element_type=F32)
-        total = total.reshape(xs, zs, ROWS, block)
-        for k, o_ref in enumerate(o_refs):
-            o_ref[:, 0, :, :, at] = total[:, :, k * COPIES : (k + 1) * COPIES, :]
+    core, start = where_ref[0], where_ref[2]
+    slab = pl.program_id(1)
+
+    @pl.when(pl.program_id(0) == 0)
+    def _():
+        for t in range(tiles):
+            if t < whole:
+                tile = core * whole + t
+            elif t < 2 * whole:
+                tile = (1 - core) * whole + t - whole
+            else:
+                tile = t
+            for r in range(xs):
+                at = pl.ds(lax.rem(start + r, xs) * zs, zs)
+                piece = x_ref[at, 0, tile].astype(F32).reshape(zs * ROWS, LANES)
+                lhs[slab, r * zs * ROWS : (r + 1) * zs * ROWS, t * LANES : (t + 1) * LANES] = piece.astype(BF)
+
+    total = jnp.zeros((chips * ROWS, own_ref.shape[2]), F32)
+    for part in range(2):
+        total += jnp.dot(lhs[slab, :, :main], own_ref[part, :main, :], preferred_element_type=F32)
+        total += jnp.dot(lhs[slab, :, main : 2 * main], other_ref[part, :main, :], preferred_element_type=F32)
+        own, other = own_ref[part, main:, :], other_ref[part, main:, :]
+        edge = jnp.where(core == 0, jnp.concatenate([own, other], axis=0), jnp.concatenate([other, own], axis=0))
+        total += jnp.dot(lhs[slab, :, 2 * main : 2 * main + 2 * LEFT], edge, preferred_element_type=F32)
+    total = total.reshape(xs, zs, ROWS, own_ref.shape[2])
+    for k, o_ref in enumerate(o_refs):
+        o_ref[:, 0] = total[:, :, k * COPIES : (k + 1) * COPIES, :]
 
 
 def ladder(panels, own, other, where, xs, ys):
     chips, size, tiles = panels.shape[:3]
     zs = chips // xs
-    count = own.shape[2]
-    once = pl.Buffered(1)
+    count, block = own.shape[2], 256
     return pl.pallas_call(
         lambda *refs: ladder_kernel(xs, *refs),
         grid_spec=pltpu.PrefetchScalarGridSpec(
             num_scalar_prefetch=1,
-            grid=(size,),
+            grid=(count // block, size),
             in_specs=[
-                pl.BlockSpec((chips, 1, tiles, ROWS, LANES), lambda i, where: (0, i, 0, 0, 0)),
-                pl.BlockSpec(own.shape, lambda i, where: (0, 0, 0), pipeline_mode=once),
-                pl.BlockSpec(own.shape, lambda i, where: (0, 0, 0), pipeline_mode=once),
+                pl.BlockSpec(
+                    (chips, 1, tiles, ROWS, LANES),
+                    lambda n, i, where: (0, jnp.where(n == 0, i, size - 1), 0, 0, 0),
+                ),
+                pl.BlockSpec((2, own.shape[1], block), lambda n, i, where: (0, 0, n)),
+                pl.BlockSpec((2, own.shape[1], block), lambda n, i, where: (0, 0, n)),
             ],
             out_specs=[
-                pl.BlockSpec((xs, 1, zs, COPIES, count), lambda i, where: (0, i, 0, 0, 0))
+                pl.BlockSpec((xs, 1, zs, COPIES, block), lambda n, i, where: (0, i, 0, 0, n))
             ] * ys,
+            scratch_shapes=[pltpu.VMEM((size, chips * ROWS, tiles * LANES), BF)],
         ),
         out_shape=[jax.ShapeDtypeStruct((xs, size, zs, COPIES, count), F32)] * ys,
         compiler_params=params(),

time: 219 us -> 213 us (0.973)
  Pallas kernels: 63.4 us -> 46.1 us
  waiting for transfers between devices: 72.1 us -> 82.2 us
  local copies, waits for them, and re-layouts: 5.62 us -> 9.54 us
    pallas_call x3, Pallas kernels: 21 us -> 9.17 us  [flatten(): pl.pallas_call(lambda *refs: flatten_kernel(xs, zs, width, *refs), grid_s...]
    all_to_all x3, waiting for transfers between devices: 37.2 us -> 44.4 us  [body(): panels = lax.all_to_all(flat, ('x', 'z'), 0, 0, tiled=True)]
    unnamed x14 -> x24, local copies, waits for them, and re-layouts: 0.03 us -> 7.19 us
    ppermute x21, waiting for transfers between devices: 22.5 us -> 25.5 us  [further(): lax.ppermute(block, axis, [(i, (i + hops) % size) for i in range(size)])]
    pallas_call x1, Pallas kernels: 9.98 us -> 7.67 us  [fold(): pl.pallas_call(fold_kernel, grid=(count // block,), in_specs=[pl.BlockSpe...]
  transfers between devices with their start and end apart: 26 -> 26, of which waited for: 12 -> 13; matrix products, arithmetic and copies ran while one was open for 3% -> 2% of each run, Pallas kernels for 25% -> 20%
where the time goes in v3:
time: 213 us; the launch traced here: 212 us
  waiting for transfers between devices  82.2 us (39%)
  starting transfers between devices  70.9 us (33%)
  Pallas kernels  46.1 us (22%)
  local copies, waits for them, and re-layouts  9.54 us (4%)
  other arithmetic  3.37 us (2%)
    all_to_all x3, waiting for transfers between devices, body(): panels = lax.all_to_all(flat, ('x', 'z'), 0, 0, tiled=True)  44.4 us
    ppermute x21, starting transfers between devices, further(): lax.ppermute(block, axis, [(i, (i + hops) % size) for i in range(size)])  38.1 us
    pallas_call x3, Pallas kernels, ladder(): pl.pallas_call(lambda *refs: ladder_kernel(xs, *refs), grid_spec=pltpu.Pr...  28.9 us
    all_to_all x3, starting transfers between devices, body(): panels = lax.all_to_all(flat, ('x', 'z'), 0, 0, tiled=True)  26.6 us
    ppermute x21, waiting for transfers between devices, further(): lax.ppermute(block, axis, [(i, (i + hops) % size) for i in range(size)])  25.5 us
    all_to_all x1, waiting for transfers between devices, body(): mine = jnp.sum(lax.all_to_all(mine, 'z', 0, 0, tiled=True), axis=0)  12.3 us
    pallas_call x3, Pallas kernels, flatten(): pl.pallas_call(lambda *refs: flatten_kernel(xs, zs, width, *refs), grid_s...  9.17 us
    pallas_call x1, Pallas kernels, fold(): pl.pallas_call(fold_kernel, grid=(count // block,), in_specs=[pl.BlockSpe...  7.67 us
  transfers between devices with their start and end apart: 26, of which 13 were waited for; matrix products, arithmetic and copies ran while one was open for 2% of the time, Pallas kernels for 20%

profile of v3, /device:TPU:2, one launch (start us, length us, event | category | flops | bytes accessed | tf_op | source)
XLA Modules:
  0.0 212.5 jit_solution(13698420248099112483)
XLA Ops:
  0.1 2.1 copy-done
  2.2 2.6 %shard_map.76 = bf16[32,1,15,8,128]{4,3,2,1,0:T(8,128)(2,1)} custom-call(s32[3]{0:T(128)S(1)} %pad_add_fusion.refs_0_, bf16[4,4,2,120,480]{4,3,2,1,0:T(8,128)(2,1)S(1)} %bitcast.57), custom_call_target="tpu_custom_call" | custom-call | bytes 8000000 | tf_op jit(solution)/shard_map/pallas_call | solution.py:85
  4.8 11.6 %all-to-all-start.1 = ((bf16[32,1,15,8,128]{4,3,2,1,0:T(8,128)(2,1)}), bf16[32,1,15,8,128]{4,3,2,1,0:T(8,128)(2,1)S(1)}, u32[]{:S(2)}, u32[]{:S(2)}) async-start(bf16[32,1,15,8,128]{4,3,2,1,0:T(8,128)(2,1)} %shard_map.76), calls=%async_computation.1 | async-start | bytes 1966080 | tf_op jit(solution)/shard_map/all_to_all | solution.py:246
  16.5 2.2 %copy-done.3 = bf16[2304,900]{0,1:T(8,128)(2,1)S(1)} copy-done((bf16[2304,900]{0,1:T(8,128)(2,1)S(1)}, bf16[2304,900]{0,1:T(8,128)(2,1)}, u32[]{:S(2)}) %copy-start.3) | copy-done | bytes 4147224
  18.7 7.7 %shard_map.74.refs_2_ = bf16[2,912,1280]{2,1,0:T(8,128)(2,1)} custom-call(s32[1,1280]{1,0:T(1,128)S(1)} %copy-done.4, s32[1,1280]{1,0:T(1,128)S(1)} %copy-done.5, bf16[900,2304]{1,0:T(8,128)(2,1)S(1)} %bitcast.61), custom_call_target="tpu_custom_call" | custom-call | flops 5308416000 | bytes 10000000 | tf_op jit(solution)/shard_map/pallas_call | solution.py:121
  26.3 2.6 %shard_map.78 = bf16[32,1,15,8,128]{4,3,2,1,0:T(8,128)(2,1)} custom-call(s32[3]{0:T(128)S(1)} %pad_add_fusion.refs_0_, bf16[4,4,2,120,480]{4,3,2,1,0:T(8,128)(2,1)S(1)} %bitcast.58), custom_call_target="tpu_custom_call" | custom-call | bytes 8000000 | tf_op jit(solution)/shard_map/pallas_call | solution.py:85
  29.0 12.2 %all-to-all-done.1.refs_1_ = bf16[32,1,15,8,128]{4,3,2,1,0:T(8,128)(2,1)S(1)} async-done(((bf16[32,1,15,8,128]{4,3,2,1,0:T(8,128)(2,1)}), bf16[32,1,15,8,128]{4,3,2,1,0:T(8,128)(2,1)S(1)}, u32[]{:S(2)}, u32[]{:S(2)}) %all-to-all-start.1) | async-done | bytes 983072 | tf_op jit(solution)/shard_map/all_to_all | solution.py:246
  41.2 7.6 %all-to-all-start.2 = ((bf16[32,1,15,8,128]{4,3,2,1,0:T(8,128)(2,1)}), bf16[32,1,15,8,128]{4,3,2,1,0:T(8,128)(2,1)S(1)}, u32[]{:S(2)}, u32[]{:S(2)}) async-start(bf16[32,1,15,8,128]{4,3,2,1,0:T(8,128)(2,1)} %shard_map.78), calls=%async_computation.2 | async-start | bytes 1966080 | tf_op jit(solution)/shard_map/all_to_all | solution.py:246
  48.8 2.1 copy-done.2
  50.9 3.9 %shard_map.73 = bf16[32,2,15,8,128]{4,3,2,1,0:T(8,128)(2,1)} custom-call(s32[3]{0:T(128)S(1)} %pad_add_fusion.refs_0_, bf16[4,4,2,120,480]{4,3,2,1,0:T(8,128)(2,1)S(1)} %bitcast.59), custom_call_target="tpu_custom_call" | custom-call | bytes 8000000 | tf_op jit(solution)/shard_map/pallas_call | solution.py:85
  54.8 18.4 %all-to-all-done.2.refs_1_ = bf16[32,1,15,8,128]{4,3,2,1,0:T(8,128)(2,1)S(1)} async-done(((bf16[32,1,15,8,128]{4,3,2,1,0:T(8,128)(2,1)}), bf16[32,1,15,8,128]{4,3,2,1,0:T(8,128)(2,1)S(1)}, u32[]{:S(2)}, u32[]{:S(2)}) %all-to-all-start.2) | async-done | bytes 983072 | tf_op jit(solution)/shard_map/all_to_all | solution.py:246
  73.2 7.4 %all-to-all-start = ((bf16[32,2,15,8,128]{4,3,2,1,0:T(8,128)(2,1)}), bf16[32,2,15,8,128]{4,3,2,1,0:T(8,128)(2,1)}, u32[]{:S(2)}, u32[]{:S(2)}) async-start(bf16[32,2,15,8,128]{4,3,2,1,0:T(8,128)(2,1)} %shard_map.73), calls=%async_computation | async-start | bytes 3932160 | tf_op jit(solution)/shard_map/all_to_all | solution.py:246
  80.7 0.2 convert_reduce_fusion
  81.0 7.7 %shard_map.77 = (f32[4,1,8,2,1280]{4,3,2,1,0:T(2,128)S(1)}, f32[4,1,8,2,1280]{4,3,2,1,0:T(2,128)S(1)}, f32[4,1,8,2,1280]{4,3,2,1,0:T(2,128)S(1)}, f32[4,1,8,2,1280]{4,3,2,1,0:T(2,128)S(1)}) custom-call(s32[3]{0:T(128)S(1)} %pad_add_fusion.refs_0_, bf16[32,1,15,8,128]{4,3,2,1,0:T(8,128)(2,1)S(1)} %all-to-all-done.1.refs_1_, ...), custom_call_target="tpu_custom_call" | custom-call | flops 2516582400 | bytes 12000000 | tf_op jit(solution)/shard_map/pallas_call | solution.py:177
  88.7 1.7 collective-permute-start.7
  90.3 2.9 %collective-permute-start.8 = (f32[4,1,8,2,1280]{4,3,2,1,0:T(2,128)S(1)}, f32[4,1,8,2,1280]{4,3,2,1,0:T(2,128)S(1)}, u32[]{:S(2)}, u32[]{:S(2)}) collective-permute-start(f32[4,1,8,2,1280]{4,3,2,1,0:T(2,128)S(1)} %get-tuple-element.23), channel_id=1, source_target_pairs={{0,2},{1,3},{2,0},{3,1},{4,6},{5,7},{6,4},{7,5},{8,10},{9,11},{10,... | collective-permute-start | bytes 983048 | tf_op jit(solution)/shard_map/ppermute | solution.py:209
  93.2 1.3 collective-permute-start.9
  94.6 0.2 select_reduce_fusion.1
  94.7 7.7 %shard_map.79 = (f32[4,1,8,2,1280]{4,3,2,1,0:T(2,128)S(1)}, f32[4,1,8,2,1280]{4,3,2,1,0:T(2,128)S(1)}, f32[4,1,8,2,1280]{4,3,2,1,0:T(2,128)S(1)}, f32[4,1,8,2,1280]{4,3,2,1,0:T(2,128)S(1)}) custom-call(s32[3]{0:T(128)S(1)} %pad_add_fusion.refs_0_, bf16[32,1,15,8,128]{4,3,2,1,0:T(8,128)(2,1)S(1)} %all-to-all-done.2.refs_1_, ...), custom_call_target="tpu_custom_call" | custom-call | flops 2516582400 | bytes 12000000 | tf_op jit(solution)/shard_map/pallas_call | solution.py:177
  102.4 0.8 collective-permute-start.13
  103.2 0.8 collective-permute-start.14
  104.0 2.2 %collective-permute-start.15 = (f32[4,1,8,2,1280]{4,3,2,1,0:T(2,128)S(1)}, f32[4,1,8,2,1280]{4,3,2,1,0:T(2,128)S(1)}, u32[]{:S(2)}, u32[]{:S(2)}) collective-permute-start(f32[4,1,8,2,1280]{4,3,2,1,0:T(2,128)S(1)} %get-tuple-element.28), channel_id=1, source_target_pairs={{0,3},{1,0},{2,1},{3,2},{4,7},{5,4},{6,5},{7,6},{8,11},{9,8},{10,9... | collective-permute-start | bytes 983048 | tf_op jit(solution)/shard_map/ppermute | solution.py:209
  106.1 2.7 %collective-permute-done.8 = f32[4,1,8,2,1280]{4,3,2,1,0:T(2,128)S(1)} collective-permute-done((f32[4,1,8,2,1280]{4,3,2,1,0:T(2,128)S(1)}, f32[4,1,8,2,1280]{4,3,2,1,0:T(2,128)S(1)}, u32[]{:S(2)}, u32[]{:S(2)}) %collective-permute-start.8) | collective-permute-done | bytes 327712 | tf_op jit(solution)/shard_map/ppermute | solution.py:209
  108.8 0.8 copy-done.8
  109.6 0.2 fusion.16
  109.8 1.5 collective-permute-start.10
  111.3 13.8 %all-to-all-done.refs_1_ = bf16[32,2,15,8,128]{4,3,2,1,0:T(8,128)(2,1)} async-done(((bf16[32,2,15,8,128]{4,3,2,1,0:T(8,128)(2,1)}), bf16[32,2,15,8,128]{4,3,2,1,0:T(8,128)(2,1)}, u32[]{:S(2)}, u32[]{:S(2)}) %all-to-all-start) | async-done | bytes 1966112 | tf_op jit(solution)/shard_map/all_to_all | solution.py:246
  125.1 13.5 %shard_map.75 = (f32[4,2,8,2,1280]{4,3,2,1,0:T(2,128)S(1)}, f32[4,2,8,2,1280]{4,3,2,1,0:T(2,128)S(1)}, f32[4,2,8,2,1280]{4,3,2,1,0:T(2,128)S(1)}, f32[4,2,8,2,1280]{4,3,2,1,0:T(2,128)S(1)}) custom-call(s32[3]{0:T(128)S(1)} %pad_add_fusion.refs_0_, bf16[32,2,15,8,128]{4,3,2,1,0:T(8,128)(2,1)} %all-to-all-done.refs_1_, ...), custom_call_target="tpu_custom_call" | custom-call | flops 5033164800 | bytes 15000000 | tf_op jit(solution)/shard_map/pallas_call | solution.py:177
  138.6 1.7 collective-permute-start.1
  140.3 2.9 %collective-permute-start.2 = (f32[4,2,8,2,1280]{4,3,2,1,0:T(2,128)S(1)}, f32[4,2,8,2,1280]{4,3,2,1,0:T(2,128)S(1)}, u32[]{:S(2)}, u32[]{:S(2)}) collective-permute-start(f32[4,2,8,2,1280]{4,3,2,1,0:T(2,128)S(1)} %get-tuple-element.19), channel_id=1, source_target_pairs={{0,2},{1,3},{2,0},{3,1},{4,6},{5,7},{6,4},{7,5},{8,10},{9,11},{10,... | collective-permute-start | bytes 1966088 | tf_op jit(solution)/shard_map/ppermute | solution.py:209
  143.2 1.4 collective-permute-start.3
  144.5 2.4 %collective-permute-start.11 = (f32[1,8,2,1280]{3,2,1,0:T(2,128)S(1)}, f32[1,8,2,1280]{3,2,1,0:T(2,128)S(1)}, u32[]{:S(2)}, u32[]{:S(2)}) collective-permute-start(f32[1,8,2,1280]{3,2,1,0:T(2,128)S(1)} %get-tuple-element.36), channel_id=1, source_target_pairs={{0,16},{8,24},{16,0},{24,8},{1,17},{9,25},{17,1},{25,9},{2,18},{10... | collective-permute-start | bytes 245768 | tf_op jit(solution)/shard_map/ppermute | solution.py:209
  147.0 1.2 collective-permute-start.12
  148.1 0.2 fusion.9
  148.4 2.1 collective-permute-done.11
  150.5 1.7 collective-permute-start.16
  152.2 4.2 %collective-permute-start.17 = (f32[1,8,2,1280]{3,2,1,0:T(2,128)S(1)}, f32[1,8,2,1280]{3,2,1,0:T(2,128)S(1)}, u32[]{:S(2)}, u32[]{:S(2)}) collective-permute-start(f32[1,8,2,1280]{3,2,1,0:T(2,128)S(1)} %get-tuple-element.39), channel_id=1, source_target_pairs={{0,16},{8,24},{16,0},{24,8},{1,17},{9,25},{17,1},{25,9},{2,18},{10... | collective-permute-start | bytes 245768 | tf_op jit(solution)/shard_map/ppermute | solution.py:209
  156.3 1.1 fusion.20
  157.5 1.7 collective-permute-start.18
  159.2 11.4 %collective-permute-done.2 = f32[4,2,8,2,1280]{4,3,2,1,0:T(2,128)S(1)} collective-permute-done((f32[4,2,8,2,1280]{4,3,2,1,0:T(2,128)S(1)}, f32[4,2,8,2,1280]{4,3,2,1,0:T(2,128)S(1)}, u32[]{:S(2)}, u32[]{:S(2)}) %collective-permute-start.2) | collective-permute-done | bytes 655392 | tf_op jit(solution)/shard_map/ppermute | solution.py:209
  170.6 0.4 fusion.2
  171.0 1.1 collective-permute-start.4
  172.1 3.4 %collective-permute-start.5 = (f32[2,8,2,1280]{3,2,1,0:T(2,128)S(1)}, f32[2,8,2,1280]{3,2,1,0:T(2,128)S(1)}, u32[]{:S(2)}, u32[]{:S(2)}) collective-permute-start(f32[2,8,2,1280]{3,2,1,0:T(2,128)S(1)} %get-tuple-element.33), channel_id=1, source_target_pairs={{0,16},{8,24},{16,0},{24,8},{1,17},{9,25},{17,1},{25,9},{2,18},{10... | collective-permute-start | bytes 491528 | tf_op jit(solution)/shard_map/ppermute | solution.py:209
  175.5 0.2 collective-permute-start.6
  175.6 0.1 fusion.13
  175.8 2.2 %collective-permute-done.4 = f32[2,8,2,1280]{3,2,1,0:T(2,128)S(1)} collective-permute-done((f32[2,8,2,1280]{3,2,1,0:T(2,128)S(1)}, f32[2,8,2,1280]{3,2,1,0:T(2,128)S(1)}, u32[]{:S(2)}, u32[]{:S(2)}) %collective-permute-start.4) | collective-permute-done | bytes 163872 | tf_op jit(solution)/shard_map/ppermute | solution.py:209
  178.0 1.9 collective-permute-done.5
  179.9 1.7 collective-permute-done.6
  181.5 0.2 fusion.6
  181.8 0.2 maximum_bitcast_fusion
  182.0 0.8 copy.18
  182.8 6.2 %all-to-all-start.3 = ((f32[8,8,1280]{2,1,0:T(8,128)}), f32[8,8,1280]{2,1,0:T(8,128)S(1)}, u32[]{:S(2)}, u32[]{:S(2)}) async-start(f32[8,8,1280]{2,1,0:T(8,128)} %copy.18), calls=%async_computation.3 | async-start | bytes 655360 | tf_op jit(solution)/shard_map/all_to_all | solution.py:253
  189.1 0.2 select_reduce_fusion
  189.4 12.3 %all-to-all-done.3 = f32[8,8,1280]{2,1,0:T(8,128)S(1)} async-done(((f32[8,8,1280]{2,1,0:T(8,128)}), f32[8,8,1280]{2,1,0:T(8,128)S(1)}, u32[]{:S(2)}, u32[]{:S(2)}) %all-to-all-start.3) | async-done | bytes 327712 | tf_op jit(solution)/shard_map/all_to_all | solution.py:253
  201.7 2.1 collective-permute-start.19
  203.8 3.2 %collective-permute-start.20 = (f32[8,1280]{1,0:T(8,128)S(1)}, f32[8,1280]{1,0:T(8,128)S(1)}, u32[]{:S(2)}, u32[]{:S(2)}) collective-permute-start(f32[8,1280]{1,0:T(8,128)S(1)} %reduce_sum.45), channel_id=1, source_target_pairs={{0,2},{1,3},{2,0},{3,1},{4,6},{5,7},{6,4},{7,5},{8,10},{9,11},{10,... | collective-permute-start | bytes 122888 | tf_op jit(solution)/shard_map/ppermute | solution.py:209
  207.0 0.1 copy.19.pair_ref
  207.5 0.5 collective-permute-done.19
  208.0 1.5 collective-permute-done.20
  209.4 1.6 collective-permute-done.21
  211.0 0.4 shard_map.80
  211.5 0.1 reshape.451
  211.6 0.1 broadcast_select_fusion
  211.7 0.7 copy.20
  (60 shorter events, 0.9 us)
Async XLA Ops:
  0.0 16.5 %copy-start.4 = (s32[1,1280]{1,0:T(1,128)S(1)}, s32[1,1280]{1,0:T(1,128)}, u32[]{:S(2)}) copy-start(s32[1,1280]{1,0:T(1,128)} %constant.57.clone.one_ref) | copy-start | bytes 15364
  0.0 16.5 %copy-start.5 = (s32[1,1280]{1,0:T(1,128)S(1)}, s32[1,1280]{1,0:T(1,128)}, u32[]{:S(2)}) copy-start(s32[1,1280]{1,0:T(1,128)} %constant.58.clone.two_ref) | copy-start | bytes 15364
  0.1 2.1 copy-start
  4.8 36.4 %all-to-all-start.1 = ((bf16[32,1,15,8,128]{4,3,2,1,0:T(8,128)(2,1)}), bf16[32,1,15,8,128]{4,3,2,1,0:T(8,128)(2,1)S(1)}, u32[]{:S(2)}, u32[]{:S(2)}) async-start(bf16[32,1,15,8,128]{4,3,2,1,0:T(8,128)(2,1)} %shard_map.76), calls=%async_computation.1 | async-start | bytes 1966080 | tf_op jit(solution)/shard_map/all_to_all | solution.py:246
  16.5 2.2 %copy-start.3 = (bf16[2304,900]{0,1:T(8,128)(2,1)S(1)}, bf16[2304,900]{0,1:T(8,128)(2,1)}, u32[]{:S(2)}) copy-start(bf16[2304,900]{0,1:T(8,128)(2,1)} %param.8) | copy-start | bytes 12441604
  18.7 7.7 %copy-start.1 = (bf16[32,120,480]{2,1,0:T(8,128)(2,1)S(1)}, bf16[32,120,480]{2,1,0:T(8,128)(2,1)}, u32[]{:S(2)}) copy-start(bf16[32,120,480]{2,1,0:T(8,128)(2,1)} %param.7) | copy-start | bytes 11059204
  26.3 54.7 %collective-permute-start = (bf16[2,912,1280]{2,1,0:T(8,128)(2,1)}, bf16[2,912,1280]{2,1,0:T(8,128)(2,1)}, u32[]{:S(2)}, u32[]{:S(2)}) collective-permute-start(bf16[2,912,1280]{2,1,0:T(8,128)(2,1)} %shard_map.74.refs_2_), channel_id=1, source_target_pairs={{0,4},{4,0},{1,5},{5,1},{2,6},{6,2},{3,7},{7,3},{8,12},{12,8},{9,1... | collective-permute-start | bytes 14008328 | tf_op jit(solution)/shard_map/ppermute | solution.py:240
  41.2 32.0 %all-to-all-start.2 = ((bf16[32,1,15,8,128]{4,3,2,1,0:T(8,128)(2,1)}), bf16[32,1,15,8,128]{4,3,2,1,0:T(8,128)(2,1)S(1)}, u32[]{:S(2)}, u32[]{:S(2)}) async-start(bf16[32,1,15,8,128]{4,3,2,1,0:T(8,128)(2,1)} %shard_map.78), calls=%async_computation.2 | async-start | bytes 1966080 | tf_op jit(solution)/shard_map/all_to_all | solution.py:246
  48.8 2.1 copy-start.2
  50.9 29.8 %copy-start.11 = (s32[32]{0:T(128)S(1)}, s32[32]{0:T(128)}, u32[]{:S(2)}) copy-start(s32[32]{0:T(128)} %param.9) | copy-start | bytes 388
  73.2 51.9 %all-to-all-start = ((bf16[32,2,15,8,128]{4,3,2,1,0:T(8,128)(2,1)}), bf16[32,2,15,8,128]{4,3,2,1,0:T(8,128)(2,1)}, u32[]{:S(2)}, u32[]{:S(2)}) async-start(bf16[32,2,15,8,128]{4,3,2,1,0:T(8,128)(2,1)} %shard_map.73), calls=%async_computation | async-start | bytes 3932160 | tf_op jit(solution)/shard_map/all_to_all | solution.py:246
  88.7 15.3 %collective-permute-start.7 = (f32[4,1,8,2,1280]{4,3,2,1,0:T(2,128)S(1)}, f32[4,1,8,2,1280]{4,3,2,1,0:T(2,128)S(1)}, u32[]{:S(2)}, u32[]{:S(2)}) collective-permute-start(f32[4,1,8,2,1280]{4,3,2,1,0:T(2,128)S(1)} %get-tuple-element.22), channel_id=1, source_target_pairs={{0,1},{1,2},{2,3},{3,0},{4,5},{5,6},{6,7},{7,4},{8,9},{9,10},{10,1... | collective-permute-start | bytes 983048 | tf_op jit(solution)/shard_map/ppermute | solution.py:209
  90.3 18.5 %collective-permute-start.8 = (f32[4,1,8,2,1280]{4,3,2,1,0:T(2,128)S(1)}, f32[4,1,8,2,1280]{4,3,2,1,0:T(2,128)S(1)}, u32[]{:S(2)}, u32[]{:S(2)}) collective-permute-start(f32[4,1,8,2,1280]{4,3,2,1,0:T(2,128)S(1)} %get-tuple-element.23), channel_id=1, source_target_pairs={{0,2},{1,3},{2,0},{3,1},{4,6},{5,7},{6,4},{7,5},{8,10},{9,11},{10,... | collective-permute-start | bytes 983048 | tf_op jit(solution)/shard_map/ppermute | solution.py:209
  93.2 15.6 %collective-permute-start.9 = (f32[4,1,8,2,1280]{4,3,2,1,0:T(2,128)S(1)}, f32[4,1,8,2,1280]{4,3,2,1,0:T(2,128)S(1)}, u32[]{:S(2)}, u32[]{:S(2)}) collective-permute-start(f32[4,1,8,2,1280]{4,3,2,1,0:T(2,128)S(1)} %get-tuple-element.24), channel_id=1, source_target_pairs={{0,3},{1,0},{2,1},{3,2},{4,7},{5,4},{6,5},{7,6},{8,11},{9,8},{10,9... | collective-permute-start | bytes 983048 | tf_op jit(solution)/shard_map/ppermute | solution.py:209
  102.4 37.9 %collective-permute-start.13 = (f32[4,1,8,2,1280]{4,3,2,1,0:T(2,128)S(1)}, f32[4,1,8,2,1280]{4,3,2,1,0:T(2,128)S(1)}, u32[]{:S(2)}, u32[]{:S(2)}) collective-permute-start(f32[4,1,8,2,1280]{4,3,2,1,0:T(2,128)S(1)} %get-tuple-element.26), channel_id=1, source_target_pairs={{0,1},{1,2},{2,3},{3,0},{4,5},{5,6},{6,7},{7,4},{8,9},{9,10},{10,1... | collective-permute-start | bytes 983048 | tf_op jit(solution)/shard_map/ppermute | solution.py:209
  103.2 40.0 %collective-permute-start.14 = (f32[4,1,8,2,1280]{4,3,2,1,0:T(2,128)S(1)}, f32[4,1,8,2,1280]{4,3,2,1,0:T(2,128)S(1)}, u32[]{:S(2)}, u32[]{:S(2)}) collective-permute-start(f32[4,1,8,2,1280]{4,3,2,1,0:T(2,128)S(1)} %get-tuple-element.27), channel_id=1, source_target_pairs={{0,2},{1,3},{2,0},{3,1},{4,6},{5,7},{6,4},{7,5},{8,10},{9,11},{10,... | collective-permute-start | bytes 983048 | tf_op jit(solution)/shard_map/ppermute | solution.py:209
  104.0 7.4 %copy-start.6 = (f32[4,1,8,2,1280]{4,3,2,1,0:T(2,128)}, f32[4,1,8,2,1280]{4,3,2,1,0:T(2,128)S(1)}, u32[]{:S(2)}) copy-start(f32[4,1,8,2,1280]{4,3,2,1,0:T(2,128)S(1)} %collective-permute-done.7) | copy-start | bytes 983044
  104.0 40.6 %collective-permute-start.15 = (f32[4,1,8,2,1280]{4,3,2,1,0:T(2,128)S(1)}, f32[4,1,8,2,1280]{4,3,2,1,0:T(2,128)S(1)}, u32[]{:S(2)}, u32[]{:S(2)}) collective-permute-start(f32[4,1,8,2,1280]{4,3,2,1,0:T(2,128)S(1)} %get-tuple-element.28), channel_id=1, source_target_pairs={{0,3},{1,0},{2,1},{3,2},{4,7},{5,4},{6,5},{7,6},{8,11},{9,8},{10,9... | collective-permute-start | bytes 983048 | tf_op jit(solution)/shard_map/ppermute | solution.py:209
  108.8 2.5 %copy-start.7 = (f32[4,1,8,2,1280]{4,3,2,1,0:T(2,128)}, f32[4,1,8,2,1280]{4,3,2,1,0:T(2,128)S(1)}, u32[]{:S(2)}) copy-start(f32[4,1,8,2,1280]{4,3,2,1,0:T(2,128)S(1)} %collective-permute-done.8) | copy-start | bytes 983044
  108.8 0.8 copy-start.8
  109.8 37.2 %collective-permute-start.10 = (f32[1,8,2,1280]{3,2,1,0:T(2,128)S(1)}, f32[1,8,2,1280]{3,2,1,0:T(2,128)}, u32[]{:S(2)}, u32[]{:S(2)}) collective-permute-start(f32[1,8,2,1280]{3,2,1,0:T(2,128)S(1)} %get-tuple-element.34), channel_id=1, source_target_pairs={{0,8},{8,16},{16,24},{24,0},{1,9},{9,17},{17,25},{25,1},{2,10},{10... | collective-permute-start | bytes 245768 | tf_op jit(solution)/shard_map/ppermute | solution.py:209
  138.6 18.8 %collective-permute-start.1 = (f32[4,2,8,2,1280]{4,3,2,1,0:T(2,128)S(1)}, f32[4,2,8,2,1280]{4,3,2,1,0:T(2,128)S(1)}, u32[]{:S(2)}, u32[]{:S(2)}) collective-permute-start(f32[4,2,8,2,1280]{4,3,2,1,0:T(2,128)S(1)} %get-tuple-element.18), channel_id=1, source_target_pairs={{0,1},{1,2},{2,3},{3,0},{4,5},{5,6},{6,7},{7,4},{8,9},{9,10},{10,1... | collective-permute-start | bytes 1966088 | tf_op jit(solution)/shard_map/ppermute | solution.py:209
  140.3 30.3 %collective-permute-start.2 = (f32[4,2,8,2,1280]{4,3,2,1,0:T(2,128)S(1)}, f32[4,2,8,2,1280]{4,3,2,1,0:T(2,128)S(1)}, u32[]{:S(2)}, u32[]{:S(2)}) collective-permute-start(f32[4,2,8,2,1280]{4,3,2,1,0:T(2,128)S(1)} %get-tuple-element.19), channel_id=1, source_target_pairs={{0,2},{1,3},{2,0},{3,1},{4,6},{5,7},{6,4},{7,5},{8,10},{9,11},{10,... | collective-permute-start | bytes 1966088 | tf_op jit(solution)/shard_map/ppermute | solution.py:209
  143.2 27.4 %collective-permute-start.3 = (f32[4,2,8,2,1280]{4,3,2,1,0:T(2,128)S(1)}, f32[4,2,8,2,1280]{4,3,2,1,0:T(2,128)S(1)}, u32[]{:S(2)}, u32[]{:S(2)}) collective-permute-start(f32[4,2,8,2,1280]{4,3,2,1,0:T(2,128)S(1)} %get-tuple-element.20), channel_id=1, source_target_pairs={{0,3},{1,0},{2,1},{3,2},{4,7},{5,4},{6,5},{7,6},{8,11},{9,8},{10,9... | collective-permute-start | bytes 1966088 | tf_op jit(solution)/shard_map/ppermute | solution.py:209
  144.5 5.9 %collective-permute-start.11 = (f32[1,8,2,1280]{3,2,1,0:T(2,128)S(1)}, f32[1,8,2,1280]{3,2,1,0:T(2,128)S(1)}, u32[]{:S(2)}, u32[]{:S(2)}) collective-permute-start(f32[1,8,2,1280]{3,2,1,0:T(2,128)S(1)} %get-tuple-element.36), channel_id=1, source_target_pairs={{0,16},{8,24},{16,0},{24,8},{1,17},{9,25},{17,1},{25,9},{2,18},{10... | collective-permute-start | bytes 245768 | tf_op jit(solution)/shard_map/ppermute | solution.py:209
  147.0 5.2 %collective-permute-start.12 = (f32[1,8,2,1280]{3,2,1,0:T(2,128)S(1)}, f32[1,8,2,1280]{3,2,1,0:T(2,128)S(1)}, u32[]{:S(2)}, u32[]{:S(2)}) collective-permute-start(f32[1,8,2,1280]{3,2,1,0:T(2,128)S(1)} %get-tuple-element.35), channel_id=1, source_target_pairs={{0,24},{8,0},{16,8},{24,16},{1,25},{9,1},{17,9},{25,17},{2,26},{10... | collective-permute-start | bytes 245768 | tf_op jit(solution)/shard_map/ppermute | solution.py:209
  148.4 40.8 %copy-start.9 = (f32[48]{0:T(128)S(1)}, f32[48]{0:T(128)}, u32[]{:S(2)}) copy-start(f32[48]{0:T(128)} %param.10) | copy-start | bytes 580
  148.4 58.8 %copy-start.10 = (f32[48]{0:T(128)S(1)}, f32[48]{0:T(128)}, u32[]{:S(2)}) copy-start(f32[48]{0:T(128)} %param.11) | copy-start | bytes 580
  150.5 25.0 %collective-permute-start.16 = (f32[1,8,2,1280]{3,2,1,0:T(2,128)S(1)}, f32[1,8,2,1280]{3,2,1,0:T(2,128)S(1)}, u32[]{:S(2)}, u32[]{:S(2)}) collective-permute-start(f32[1,8,2,1280]{3,2,1,0:T(2,128)S(1)} %get-tuple-element.37), channel_id=1, source_target_pairs={{0,8},{8,16},{16,24},{24,0},{1,9},{9,17},{17,25},{25,1},{2,10},{10... | collective-permute-start | bytes 245768 | tf_op jit(solution)/shard_map/ppermute | solution.py:209
  152.2 23.5 %collective-permute-start.17 = (f32[1,8,2,1280]{3,2,1,0:T(2,128)S(1)}, f32[1,8,2,1280]{3,2,1,0:T(2,128)S(1)}, u32[]{:S(2)}, u32[]{:S(2)}) collective-permute-start(f32[1,8,2,1280]{3,2,1,0:T(2,128)S(1)} %get-tuple-element.39), channel_id=1, source_target_pairs={{0,16},{8,24},{16,0},{24,8},{1,17},{9,25},{17,1},{25,9},{2,18},{10... | collective-permute-start | bytes 245768 | tf_op jit(solution)/shard_map/ppermute | solution.py:209
  157.5 18.2 %collective-permute-start.18 = (f32[1,8,2,1280]{3,2,1,0:T(2,128)S(1)}, f32[1,8,2,1280]{3,2,1,0:T(2,128)S(1)}, u32[]{:S(2)}, u32[]{:S(2)}) collective-permute-start(f32[1,8,2,1280]{3,2,1,0:T(2,128)S(1)} %get-tuple-element.38), channel_id=1, source_target_pairs={{0,24},{8,0},{16,8},{24,16},{1,25},{9,1},{17,9},{25,17},{2,26},{10... | collective-permute-start | bytes 245768 | tf_op jit(solution)/shard_map/ppermute | solution.py:209
  171.0 7.0 %collective-permute-start.4 = (f32[2,8,2,1280]{3,2,1,0:T(2,128)S(1)}, f32[2,8,2,1280]{3,2,1,0:T(2,128)S(1)}, u32[]{:S(2)}, u32[]{:S(2)}) collective-permute-start(f32[2,8,2,1280]{3,2,1,0:T(2,128)S(1)} %get-tuple-element.31), channel_id=1, source_target_pairs={{0,8},{8,16},{16,24},{24,0},{1,9},{9,17},{17,25},{25,1},{2,10},{10... | collective-permute-start | bytes 491528 | tf_op jit(solution)/shard_map/ppermute | solution.py:209
  172.1 7.8 %collective-permute-start.5 = (f32[2,8,2,1280]{3,2,1,0:T(2,128)S(1)}, f32[2,8,2,1280]{3,2,1,0:T(2,128)S(1)}, u32[]{:S(2)}, u32[]{:S(2)}) collective-permute-start(f32[2,8,2,1280]{3,2,1,0:T(2,128)S(1)} %get-tuple-element.33), channel_id=1, source_target_pairs={{0,16},{8,24},{16,0},{24,8},{1,17},{9,25},{17,1},{25,9},{2,18},{10... | collective-permute-start | bytes 491528 | tf_op jit(solution)/shard_map/ppermute | solution.py:209
  175.5 6.1 %collective-permute-start.6 = (f32[2,8,2,1280]{3,2,1,0:T(2,128)S(1)}, f32[2,8,2,1280]{3,2,1,0:T(2,128)S(1)}, u32[]{:S(2)}, u32[]{:S(2)}) collective-permute-start(f32[2,8,2,1280]{3,2,1,0:T(2,128)S(1)} %get-tuple-element.32), channel_id=1, source_target_pairs={{0,24},{8,0},{16,8},{24,16},{1,25},{9,1},{17,9},{25,17},{2,26},{10... | collective-permute-start | bytes 491528 | tf_op jit(solution)/shard_map/ppermute | solution.py:209
  182.8 18.9 %all-to-all-start.3 = ((f32[8,8,1280]{2,1,0:T(8,128)}), f32[8,8,1280]{2,1,0:T(8,128)S(1)}, u32[]{:S(2)}, u32[]{:S(2)}) async-start(f32[8,8,1280]{2,1,0:T(8,128)} %copy.18), calls=%async_computation.3 | async-start | bytes 655360 | tf_op jit(solution)/shard_map/all_to_all | solution.py:253
  201.7 6.3 %collective-permute-start.19 = (f32[8,1280]{1,0:T(8,128)S(1)}, f32[8,1280]{1,0:T(8,128)S(1)}, u32[]{:S(2)}, u32[]{:S(2)}) collective-permute-start(f32[8,1280]{1,0:T(8,128)S(1)} %reduce_sum.45), channel_id=1, source_target_pairs={{0,1},{1,2},{2,3},{3,0},{4,5},{5,6},{6,7},{7,4},{8,9},{9,10},{10,1... | collective-permute-start | bytes 122888 | tf_op jit(solution)/shard_map/ppermute | solution.py:209
  203.8 5.6 %collective-permute-start.20 = (f32[8,1280]{1,0:T(8,128)S(1)}, f32[8,1280]{1,0:T(8,128)S(1)}, u32[]{:S(2)}, u32[]{:S(2)}) collective-permute-start(f32[8,1280]{1,0:T(8,128)S(1)} %reduce_sum.45), channel_id=1, source_target_pairs={{0,2},{1,3},{2,0},{3,1},{4,6},{5,7},{6,4},{7,5},{8,10},{9,11},{10,... | collective-permute-start | bytes 122888 | tf_op jit(solution)/shard_map/ppermute | solution.py:209
  207.0 4.0 %collective-permute-start.21 = (f32[8,1280]{1,0:T(8,128)S(1)}, f32[8,1280]{1,0:T(8,128)S(1)}, u32[]{:S(2)}, u32[]{:S(2)}) collective-permute-start(f32[8,1280]{1,0:T(8,128)S(1)} %reduce_sum.45), channel_id=1, source_target_pairs={{0,3},{1,0},{2,1},{3,2},{4,7},{5,4},{6,5},{7,6},{8,11},{9,8},{10,9... | collective-permute-start | bytes 122888 | tf_op jit(solution)/shard_map/ppermute | solution.py:209

commit v4 on v3

--- a/solution.py
+++ b/solution.py
@@ -107,11 +107,11 @@
     row = lax.broadcasted_iota(jnp.int32, (full, one_ref.shape[1]), 0)
     pick = (row == one_ref[...]).astype(F32) + (row == two_ref[...]).astype(F32)
     both = jnp.dot(b_ref[...], pick.astype(BF), preferred_element_type=F32)
-    rest = o_ref.shape[1] - width
+    rest = o_ref.shape[2] - width
     both = jnp.concatenate([both, jnp.zeros((rest, both.shape[1]), F32)], axis=0)
     hi = both.astype(BF)
-    o_ref[0] = hi
-    o_ref[1] = (both - hi.astype(F32)).astype(BF)
+    o_ref[0, 0] = hi
+    o_ref[0, 1] = (both - hi.astype(F32)).astype(BF)
 
 
 def fold(columns, one, two):
@@ -126,8 +126,8 @@
             pl.BlockSpec((1, block), lambda i: (0, i)),
             pl.BlockSpec((width, full), lambda i: (0, 0), pipeline_mode=pl.Buffered(1)),
         ],
-        out_specs=pl.BlockSpec((2, padded, block), lambda i: (0, 0, i)),
-        out_shape=jax.ShapeDtypeStruct((2, padded, count), BF),
+        out_specs=pl.BlockSpec((1, 2, padded, block), lambda i: (i, 0, 0, 0)),
+        out_shape=jax.ShapeDtypeStruct((count // block, 2, padded, block), BF),
         compiler_params=params(),
         cost_estimate=pl.CostEstimate(
             flops=2 * width * full * count, bytes_accessed=10_000_000, transcendentals=0
@@ -135,64 +135,117 @@
     )(one, two, columns)
 
 
-def ladder_kernel(xs, where_ref, x_ref, own_ref, other_ref, *refs):
-    o_refs, lhs = refs[:-1], refs[-1]
-    chips, tiles = x_ref.shape[0], x_ref.shape[2]
+def ladder_block(xs, where_ref, x_ref, own_ref, other_ref, lhs):
+    chips, size, tiles = x_ref.shape[:3]
     zs = chips // xs
     whole = tiles // 2
     main = whole * LANES
-    core, start = where_ref[0], where_ref[2]
-    slab = pl.program_id(1)
+    core = where_ref[0]
 
     @pl.when(pl.program_id(0) == 0)
     def _():
-        for t in range(tiles):
-            if t < whole:
-                tile = core * whole + t
-            elif t < 2 * whole:
-                tile = (1 - core) * whole + t - whole
-            else:
-                tile = t
-            for r in range(xs):
-                at = pl.ds(lax.rem(start + r, xs) * zs, zs)
-                piece = x_ref[at, 0, tile].astype(F32).reshape(zs * ROWS, LANES)
-                lhs[slab, r * zs * ROWS : (r + 1) * zs * ROWS, t * LANES : (t + 1) * LANES] = piece.astype(BF)
-
-    total = jnp.zeros((chips * ROWS, own_ref.shape[2]), F32)
+        for r in range(xs):
+            for s in range(zs // 2):
+                pick = [
+                    lax.rem(where_ref[2] + r, xs) * zs + lax.bitwise_xor(where_ref[3], 2 * s + odd)
+                    for odd in range(2)
+                ]
+                for i in range(size):
+                    at = ((i * xs + r) * zs + 2 * s) * ROWS
+                    for t in range(tiles):
+                        if t < whole:
+                            tile = core * whole + t
+                        elif t < 2 * whole:
+                            tile = (1 - core) * whole + t - whole
+                        else:
+                            tile = t
+                        pair = jnp.concatenate([x_ref[q, i, tile].astype(F32) for q in pick], axis=0)
+                        lhs[at : at + 2 * ROWS, t * LANES : (t + 1) * LANES] = pair.astype(BF)
+
+    total = jnp.zeros((lhs.shape[0], own_ref.shape[3]), F32)
     for part in range(2):
-        total += jnp.dot(lhs[slab, :, :main], own_ref[part, :main, :], preferred_element_type=F32)
-        total += jnp.dot(lhs[slab, :, main : 2 * main], other_ref[part, :main, :], preferred_element_type=F32)
-        own, other = own_ref[part, main:, :], other_ref[part, main:, :]
+        total += jnp.dot(lhs[:, :main], own_ref[0, part, :main], preferred_element_type=F32)
+        total += jnp.dot(lhs[:, main : 2 * main], other_ref[0, part, :main], preferred_element_type=F32)
+        own, other = own_ref[0, part, main:], other_ref[0, part, main:]
         edge = jnp.where(core == 0, jnp.concatenate([own, other], axis=0), jnp.concatenate([other, own], axis=0))
-        total += jnp.dot(lhs[slab, :, 2 * main : 2 * main + 2 * LEFT], edge, preferred_element_type=F32)
-    total = total.reshape(xs, zs, ROWS, own_ref.shape[2])
+        total += jnp.dot(lhs[:, 2 * main : 2 * main + 2 * LEFT], edge, preferred_element_type=F32)
+    return total
+
+
+def ladder_kernel(xs, where_ref, x_ref, own_ref, other_ref, *refs):
+    o_refs, lhs = refs[:-1], refs[-1]
+    total = ladder_block(xs, where_ref, x_ref, own_ref, other_ref, lhs)
+    size, zs, block = x_ref.shape[1], x_ref.shape[0] // xs, total.shape[1]
+    total = total.reshape(size, xs, zs, ROWS, block)
+    at = pl.ds(pl.multiple_of(pl.program_id(0) * block, block), block)
     for k, o_ref in enumerate(o_refs):
-        o_ref[:, 0] = total[:, :, k * COPIES : (k + 1) * COPIES, :]
-
-
-def ladder(panels, own, other, where, xs, ys):
+        for i in range(size):
+            o_ref[:, i, :, :, at] = total[i, :, :, k * COPIES : (k + 1) * COPIES, :]
+
+
+def whole_kernel(xs, where_ref, x_ref, own_ref, other_ref, o_ref, f_ref, lhs, most):
+    total = ladder_block(xs, where_ref, x_ref, own_ref, other_ref, lhs)
+    block = total.shape[1]
+    total = total.reshape(o_ref.shape[0], ROWS, block)
+    step = pl.program_id(0)
+    at = pl.ds(pl.multiple_of(step * block, block), block)
+    o_ref[:, :, at] = total
+    top = jnp.max(jnp.abs(total), axis=0)
+
+    @pl.when(step == 0)
+    def _():
+        most[...] = top
+
+    @pl.when(step > 0)
+    def _():
+        most[...] = jnp.maximum(most[...], top)
+
+    @pl.when(step == pl.num_programs(0) - 1)
+    def _():
+        left = jnp.max(most[...])
+        factors, inverses = [], []
+        for _ in range(3):
+            factor, inverse = jnp.float32(1), jnp.float32(1)
+            for power in (7, 4, 2, 1):
+                small = left * float(2**power) <= 16384.0
+                grow = jnp.where(small, float(2**power), 1.0)
+                left, factor = left * grow, factor * grow
+                inverse = inverse * jnp.where(small, 2.0**-power, 1.0)
+            factors.append(factor)
+            inverses.append(inverse)
+        lane = lax.broadcasted_iota(jnp.int32, f_ref.shape, 1)
+        out = jnp.zeros(f_ref.shape, F32)
+        for n, value in enumerate(factors + inverses):
+            out = jnp.where(lane == n, value, out)
+        f_ref[...] = out
+
+
+def ladder(panels, own, other, where, xs, ys, whole=False):
     chips, size, tiles = panels.shape[:3]
     zs = chips // xs
-    count, block = own.shape[2], 256
+    blocks, _, padded, block = own.shape
+    count = blocks * block
+    scratch = [pltpu.VMEM((size * chips * ROWS, tiles * LANES), BF)]
+    if whole:
+        shapes = [(chips, ROWS, count), (8, LANES)]
+        scratch.append(pltpu.VMEM((ROWS, block), F32))
+    else:
+        shapes = [(xs, size, zs, COPIES, count)] * ys
+    kernel = whole_kernel if whole else ladder_kernel
     return pl.pallas_call(
-        lambda *refs: ladder_kernel(xs, *refs),
+        lambda *refs: kernel(xs, *refs),
         grid_spec=pltpu.PrefetchScalarGridSpec(
             num_scalar_prefetch=1,
-            grid=(count // block, size),
+            grid=(blocks,),
             in_specs=[
-                pl.BlockSpec(
-                    (chips, 1, tiles, ROWS, LANES),
-                    lambda n, i, where: (0, jnp.where(n == 0, i, size - 1), 0, 0, 0),
-                ),
-                pl.BlockSpec((2, own.shape[1], block), lambda n, i, where: (0, 0, n)),
-                pl.BlockSpec((2, own.shape[1], block), lambda n, i, where: (0, 0, n)),
+                pl.BlockSpec(panels.shape, lambda n, where: (0, 0, 0, 0, 0), pipeline_mode=pl.Buffered(1)),
+                pl.BlockSpec((1, 2, padded, block), lambda n, where: (n, 0, 0, 0)),
+                pl.BlockSpec((1, 2, padded, block), lambda n, where: (n, 0, 0, 0)),
             ],
-            out_specs=[
-                pl.BlockSpec((xs, 1, zs, COPIES, block), lambda n, i, where: (0, i, 0, 0, n))
-            ] * ys,
-            scratch_shapes=[pltpu.VMEM((size, chips * ROWS, tiles * LANES), BF)],
+            out_specs=[pl.BlockSpec(shape, lambda n, where, rank=len(shape): (0,) * rank) for shape in shapes],
+            scratch_shapes=scratch,
         ),
-        out_shape=[jax.ShapeDtypeStruct((xs, size, zs, COPIES, count), F32)] * ys,
+        out_shape=[jax.ShapeDtypeStruct(shape, F32) for shape in shapes],
         compiler_params=params(),
         cost_estimate=pl.CostEstimate(
             flops=4 * size * chips * ROWS * tiles * LANES * count,
@@ -202,6 +255,22 @@
     )(where, panels, own, other)
 
 
+def encode(partial, factors):
+    count = partial.shape[2]
+    lane = lax.broadcasted_iota(jnp.int32, partial.shape, 2)
+    coded = partial * (factors[0, 0] * factors[0, 1] * factors[0, 2])
+    for n in range(3):
+        coded = jnp.where(lane == count - 1 - n, factors[0, 3 + n], coded)
+    return coded.astype(jnp.float16)
+
+
+def decode(coded):
+    wide = coded.astype(F32)
+    count = wide.shape[2]
+    inverse = wide[:, :1, count - 1 :] * wide[:, :1, count - 2 : count - 1] * wide[:, :1, count - 3 : count - 2]
+    return jnp.sum(wide * inverse, axis=0)
+
+
 def further(block, axis, hops):
     if hops == 0:
         return block
@@ -210,9 +279,15 @@
 
 
 def update_kernel(place_ref, g_ref, col_ref, pair_ref, ea_ref, eb_ref, o_ref, slots_of):
-    parts, rows, count = g_ref.shape
+    parts, rows, count = slots_of.shape
+    done = rows - COPIES
     for k in range(parts):
-        slots_of[lax.rem(place_ref[0] + parts - k, parts)] = g_ref[k]
+        slots_of[lax.rem(place_ref[0] + parts - k, parts), :done] = g_ref[k, :done]
+    last = g_ref[0, rows:]
+    for k in range(1, parts):
+        last = last + g_ref[k, rows:]
+    for k in range(parts):
+        slots_of[k, done:] = last[k * COPIES : (k + 1) * COPIES]
     total = slots_of[...].reshape(parts * rows, count)
     slots = parts * rows
     hi = total.astype(BF).astype(F32)
@@ -234,23 +309,36 @@
     local_rows = window // ys
     one, two = unique_pairs(window)
     count = one.shape[1]
-    where = jnp.stack([lax.axis_index(axis).astype(jnp.int32) for axis in ("c", "y", "x")])
+    where = jnp.stack([lax.axis_index(axis).astype(jnp.int32) for axis in ("c", "y", "x", "z")])
+    plain = where * jnp.asarray([1, 0, 0, 0], jnp.int32)
     place = lax.axis_index("y").astype(jnp.int32)
     own = fold(integrals.T, jnp.asarray(one), jnp.asarray(two))
     other = lax.ppermute(own, "c", [(0, 1), (1, 0)])
-    reduced = []
+    done = []
     start = 0
-    for size in SIZES:
-        flat = flatten(amps, start, size, where, xs, zs)
+    for chunk, size in enumerate(SIZES):
+        final = chunk == len(SIZES) - 1
+        flat = flatten(amps, start, size, plain if final else where, xs, zs)
         start += size
         panels = lax.all_to_all(flat, ("x", "z"), 0, 0, tiled=True)
-        partial = ladder(panels, own, other, where, xs, ys)
+        partial = ladder(panels, own, other, plain if final else where, xs, ys, final)
+        if final:
+            coded = encode(*partial)
+            coded = lax.all_to_all(coded, ("x", "z"), 0, 0, tiled=True)
+            last = decode(coded)
+            continue
         partial = [further(block, "y", k) for k, block in enumerate(partial)]
         partial = [sum((block[r] for block in partial[1:]), partial[0][r]) for r in range(xs)]
         partial = [further(block, "x", r) for r, block in enumerate(partial)]
-        reduced.append(sum(partial[1:], partial[0]))
-    mine = jnp.swapaxes(jnp.concatenate(reduced, axis=0), 0, 1).reshape(zs, slots // ys, count)
-    mine = jnp.sum(lax.all_to_all(mine, "z", 0, 0, tiled=True), axis=0)
+        done.append(sum(partial[1:], partial[0]))
+    mine = jnp.concatenate(done, axis=0)
+    half = zs
+    while half > 1:
+        half //= 2
+        swap = [(i, i ^ half) for i in range(zs)]
+        mine = mine[:, :half] + lax.ppermute(mine[:, half:], "z", swap)
+    mine = mine.reshape(-1, count)
+    mine = jnp.concatenate([jnp.pad(mine, ((0, COPIES), (0, 0))), last], axis=0)
     everyone = jnp.stack([further(mine, "y", k) for k in range(ys)])
 
     pair_sum, filled = pair_energy(slot_pair, occ_energy)
@@ -269,7 +357,7 @@
         update_kernel,
         in_specs=[pl.BlockSpec(memory_space=pltpu.SMEM)] + [pl.BlockSpec(memory_space=pltpu.VMEM)] * 5,
         out_shape=jax.ShapeDtypeStruct((slots, full), F32),
-        scratch_shapes=[pltpu.VMEM(everyone.shape, F32)],
+        scratch_shapes=[pltpu.VMEM((ys, slots // ys, count), F32)],
         compiler_params=params(),
     )(place[None], everyone, column, pair_sum[:, None], ea, eb)
     update = update[:, :wide].reshape(slots, local_rows, window)

time: 213 us -> 239 us (1.12)
  waiting for transfers between devices: 82.2 us -> 104 us
  other arithmetic: 3.37 us -> 11.3 us
  starting transfers between devices: 70.9 us -> 67.7 us
    ppermute x0 -> x3, waiting for transfers between devices: none -> 17 us  [body(): mine = mine[:, :half] + lax.ppermute(mine[:, half:], 'z', swap)]
    ppermute x21 -> x15, starting transfers between devices: 38.1 us -> 25.8 us  [further(): lax.ppermute(block, axis, [(i, (i + hops) % size) for i in range(size)])]
    all_to_all x1, waiting for transfers between devices: 12.3 us -> 0.01 us  [body(): coded = lax.all_to_all(coded, ('x', 'z'), 0, 0, tiled=True)]
    ppermute x21 -> x15, waiting for transfers between devices: 25.5 us -> 35.8 us  [further(): lax.ppermute(block, axis, [(i, (i + hops) % size) for i in range(size)])]
    ppermute x0 -> x3, starting transfers between devices: none -> 8.46 us  [body(): mine = mine[:, :half] + lax.ppermute(mine[:, half:], 'z', swap)]
    all_to_all x3, waiting for transfers between devices: 44.4 us -> 50.7 us  [body(): panels = lax.all_to_all(flat, ('x', 'z'), 0, 0, tiled=True)]
    convert_element_type x0 -> x2, other arithmetic: none -> 3.06 us  [the longest x1 2.97 us: encode(): return coded.astype(jnp.float16)]
    unnamed x24 -> x18, local copies, waits for them, and re-layouts: 7.19 us -> 6.42 us
  transfers between devices with their start and end apart: 26 -> 23, of which waited for: 13 -> 12; matrix products, arithmetic and copies ran while one was open for 2% -> 4% of each run, Pallas kernels for 20% -> 17%
where the time goes in v4:
time: 239 us; the launch traced here: 238 us
  waiting for transfers between devices  104 us (44%)
  starting transfers between devices  67.7 us (28%)
  Pallas kernels  44.4 us (19%)
  other arithmetic  11.3 us (5%)
  local copies, waits for them, and re-layouts  8.64 us (4%)
    all_to_all x3, waiting for transfers between devices, body(): panels = lax.all_to_all(flat, ('x', 'z'), 0, 0, tiled=True)  50.7 us
    ppermute x15, waiting for transfers between devices, further(): lax.ppermute(block, axis, [(i, (i + hops) % size) for i in range(size)])  35.8 us
    all_to_all x3, starting transfers between devices, body(): panels = lax.all_to_all(flat, ('x', 'z'), 0, 0, tiled=True)  27.7 us
    pallas_call x3, Pallas kernels, ladder(): pl.pallas_call(lambda *refs: kernel(xs, *refs), grid_spec=pltpu.PrefetchS...  27.3 us
    ppermute x15, starting transfers between devices, further(): lax.ppermute(block, axis, [(i, (i + hops) % size) for i in range(size)])  25.8 us
    ppermute x3, waiting for transfers between devices, body(): mine = mine[:, :half] + lax.ppermute(mine[:, half:], 'z', swap)  17 us
    pallas_call x3, Pallas kernels, flatten(): pl.pallas_call(lambda *refs: flatten_kernel(xs, zs, width, *refs), grid_s...  9.09 us
    ppermute x3, starting transfers between devices, body(): mine = mine[:, :half] + lax.ppermute(mine[:, half:], 'z', swap)  8.46 us
  transfers between devices with their start and end apart: 23, of which 12 were waited for; matrix products, arithmetic and copies ran while one was open for 4% of the time, Pallas kernels for 17%

profile of v4, /device:TPU:2, one launch (start us, length us, event | category | flops | bytes accessed | tf_op | source)
XLA Modules:
  0.0 237.8 jit_solution(14322056214840378700)
XLA Ops:
  0.0 0.7 fusion.24
  0.7 2.1 copy-done
  2.8 2.6 %shard_map.85 = bf16[32,1,15,8,128]{4,3,2,1,0:T(8,128)(2,1)} custom-call(s32[4]{0:T(128)S(1)} %get-tuple-element.28.refs_0_, bf16[4,4,2,120,480]{4,3,2,1,0:T(8,128)(2,1)S(1)} %bitcast.46), custom_call_target="tpu_custom_call" | custom-call | bytes 8000000 | tf_op jit(solution)/shard_map/pallas_call | solution.py:85
  5.5 11.6 %all-to-all-start.1 = ((bf16[32,1,15,8,128]{4,3,2,1,0:T(8,128)(2,1)}), bf16[32,1,15,8,128]{4,3,2,1,0:T(8,128)(2,1)S(1)}, u32[]{:S(2)}, u32[]{:S(2)}) async-start(bf16[32,1,15,8,128]{4,3,2,1,0:T(8,128)(2,1)} %shard_map.85), calls=%async_computation.1 | async-start | bytes 1966080 | tf_op jit(solution)/shard_map/all_to_all | solution.py:323
  17.1 2.1 copy-done.1
  19.2 3.8 %shard_map.82 = bf16[32,2,15,8,128]{4,3,2,1,0:T(8,128)(2,1)} custom-call(s32[4]{0:T(128)S(1)} %get-tuple-element.28.refs_0_, bf16[4,4,2,120,480]{4,3,2,1,0:T(8,128)(2,1)S(1)} %bitcast.47), custom_call_target="tpu_custom_call" | custom-call | bytes 8000000 | tf_op jit(solution)/shard_map/pallas_call | solution.py:85
  23.1 18.8 %all-to-all-done.1.refs_1_ = bf16[32,1,15,8,128]{4,3,2,1,0:T(8,128)(2,1)S(1)} async-done(((bf16[32,1,15,8,128]{4,3,2,1,0:T(8,128)(2,1)}), bf16[32,1,15,8,128]{4,3,2,1,0:T(8,128)(2,1)S(1)}, u32[]{:S(2)}, u32[]{:S(2)}) %all-to-all-start.1) | async-done | bytes 983072 | tf_op jit(solution)/shard_map/all_to_all | solution.py:323
  41.9 7.6 %all-to-all-start = ((bf16[32,2,15,8,128]{4,3,2,1,0:T(8,128)(2,1)}), bf16[32,2,15,8,128]{4,3,2,1,0:T(8,128)(2,1)}, u32[]{:S(2)}, u32[]{:S(2)}) async-start(bf16[32,2,15,8,128]{4,3,2,1,0:T(8,128)(2,1)} %shard_map.82), calls=%async_computation | async-start | bytes 3932160 | tf_op jit(solution)/shard_map/all_to_all | solution.py:323
  49.5 2.2 copy-done.3
  51.7 7.6 %shard_map.83.refs_2_ = bf16[5,2,912,256]{3,2,1,0:T(8,128)(2,1)} custom-call(s32[1,1280]{1,0:T(1,128)S(1)} %copy-done.4, s32[1,1280]{1,0:T(1,128)S(1)} %copy-done.5, bf16[900,2304]{1,0:T(8,128)(2,1)S(1)} %bitcast.50), custom_call_target="tpu_custom_call" | custom-call | flops 5308416000 | bytes 10000000 | tf_op jit(solution)/shard_map/pallas_call | solution.py:121
  59.3 2.6 %shard_map.87 = bf16[32,1,15,8,128]{4,3,2,1,0:T(8,128)(2,1)} custom-call(s32[4]{0:T(128)S(1)} %get-tuple-element.27.refs_0_, bf16[4,4,2,120,480]{4,3,2,1,0:T(8,128)(2,1)S(1)} %bitcast.48), custom_call_target="tpu_custom_call" | custom-call | bytes 8000000 | tf_op jit(solution)/shard_map/pallas_call | solution.py:85
  62.0 0.1 slice.194
  62.0 31.9 %all-to-all-done.refs_1_ = bf16[32,2,15,8,128]{4,3,2,1,0:T(8,128)(2,1)} async-done(((bf16[32,2,15,8,128]{4,3,2,1,0:T(8,128)(2,1)}), bf16[32,2,15,8,128]{4,3,2,1,0:T(8,128)(2,1)}, u32[]{:S(2)}, u32[]{:S(2)}) %all-to-all-start) | async-done | bytes 1966112 | tf_op jit(solution)/shard_map/all_to_all | solution.py:323
  93.9 8.5 %all-to-all-start.2 = ((bf16[32,1,15,8,128]{4,3,2,1,0:T(8,128)(2,1)}), bf16[32,1,15,8,128]{4,3,2,1,0:T(8,128)(2,1)S(1)}, u32[]{:S(2)}, u32[]{:S(2)}) async-start(bf16[32,1,15,8,128]{4,3,2,1,0:T(8,128)(2,1)} %shard_map.87), calls=%async_computation.2 | async-start | bytes 1966080 | tf_op jit(solution)/shard_map/all_to_all | solution.py:323
  102.5 0.1 max.7
  102.7 0.2 convert_reduce_fusion
  102.9 0.2 select_reduce_fusion.1
  103.1 8.3 %shard_map.86 = (f32[4,1,8,2,1280]{4,3,2,1,0:T(2,128)S(1)}, f32[4,1,8,2,1280]{4,3,2,1,0:T(2,128)S(1)}, f32[4,1,8,2,1280]{4,3,2,1,0:T(2,128)}, f32[4,1,8,2,1280]{4,3,2,1,0:T(2,128)S(1)}) custom-call(s32[4]{0:T(128)S(1)} %get-tuple-element.28.refs_0_, bf16[32,1,15,8,128]{4,3,2,1,0:T(8,128)(2,1)S(1)} %all-to-all-done.1.refs_1_, ...), custom_call_target="tpu_custom_call" | custom-call | flops 2516582400 | bytes 12000000 | tf_op jit(solution)/shard_map/pallas_call | solution.py:235
  111.4 1.6 collective-permute-start.7
  113.0 11.2 %shard_map.84 = (f32[4,2,8,2,1280]{4,3,2,1,0:T(2,128)S(1)}, f32[4,2,8,2,1280]{4,3,2,1,0:T(2,128)}, f32[4,2,8,2,1280]{4,3,2,1,0:T(2,128)}, f32[4,2,8,2,1280]{4,3,2,1,0:T(2,128)S(1)}) custom-call(s32[4]{0:T(128)S(1)} %get-tuple-element.28.refs_0_, bf16[32,2,15,8,128]{4,3,2,1,0:T(8,128)(2,1)} %all-to-all-done.refs_1_, ...), custom_call_target="tpu_custom_call" | custom-call | flops 5033164800 | bytes 15000000 | tf_op jit(solution)/shard_map/pallas_call | solution.py:235
  124.2 1.6 collective-permute-start.1
  125.8 1.5 collective-permute-start.2
  127.3 2.4 %collective-permute-start.3 = (f32[4,2,8,2,1280]{4,3,2,1,0:T(2,128)S(1)}, f32[4,2,8,2,1280]{4,3,2,1,0:T(2,128)}, u32[]{:S(2)}, u32[]{:S(2)}) collective-permute-start(f32[4,2,8,2,1280]{4,3,2,1,0:T(2,128)S(1)} %get-tuple-element.18), channel_id=1, source_target_pairs={{0,3},{1,0},{2,1},{3,2},{4,7},{5,4},{6,5},{7,6},{8,11},{9,8},{10,9... | collective-permute-start | bytes 1966088 | tf_op jit(solution)/shard_map/ppermute | solution.py:278
  129.7 0.6 collective-permute-start.8
  130.4 1.7 collective-permute-start.9
  132.0 7.8 %shard_map.88 = (f32[32,8,1280]{2,1,0:T(8,128)S(1)}, f32[8,128]{1,0:T(8,128)S(1)}) custom-call(s32[4]{0:T(128)S(1)} %get-tuple-element.27.refs_0_, bf16[32,1,15,8,128]{4,3,2,1,0:T(8,128)(2,1)S(1)} %all-to-all-done.2.refs_1_, bf16[5,2,912,256]{3,2,1,0:T(8,128)(2,1)} %shard_map.83.refs_2_, bf16[5,2,912,256]{3,2,1,0:T(8,128)(2,1)} %collective-permute-done.refs_3_), custom_call_target="tpu_custom_call" | custom-call | flops 2516582400 | bytes 12000000 | tf_op jit(solution)/shard_map/pallas_call | solution.py:235
  139.8 0.7 fusion.25
  142.3 19.6 %collective-permute-done.8 = f32[4,1,8,2,1280]{4,3,2,1,0:T(2,128)} collective-permute-done((f32[4,1,8,2,1280]{4,3,2,1,0:T(2,128)}, f32[4,1,8,2,1280]{4,3,2,1,0:T(2,128)}, u32[]{:S(2)}, u32[]{:S(2)}) %collective-permute-start.8) | collective-permute-done | bytes 327712 | tf_op jit(solution)/shard_map/ppermute | solution.py:278
  161.9 7.7 %collective-permute-done.9 = f32[4,1,8,2,1280]{4,3,2,1,0:T(2,128)} collective-permute-done((f32[4,1,8,2,1280]{4,3,2,1,0:T(2,128)S(1)}, f32[4,1,8,2,1280]{4,3,2,1,0:T(2,128)}, u32[]{:S(2)}, u32[]{:S(2)}) %collective-permute-start.9) | collective-permute-done | bytes 327712 | tf_op jit(solution)/shard_map/ppermute | solution.py:278
  169.6 1.3 fusion.11
  170.9 1.5 collective-permute-start.10
  172.5 1.1 collective-permute-start.11
  173.6 2.2 collective-permute-start.12
  175.8 1.9 fusion.2
  177.6 0.1 collective-permute-start.4
  177.7 3.5 %collective-permute-start.5 = (f32[2,8,2,1280]{3,2,1,0:T(2,128)S(1)}, f32[2,8,2,1280]{3,2,1,0:T(2,128)S(1)}, u32[]{:S(2)}, u32[]{:S(2)}) collective-permute-start(f32[2,8,2,1280]{3,2,1,0:T(2,128)S(1)} %get-tuple-element.31), channel_id=1, source_target_pairs={{0,16},{8,24},{16,0},{24,8},{1,17},{9,25},{17,1},{25,9},{2,18},{10... | collective-permute-start | bytes 491528 | tf_op jit(solution)/shard_map/ppermute | solution.py:278
  181.2 1.1 fusion.15
  182.3 1.3 collective-permute-done.4
  183.6 1.6 collective-permute-done.5
  185.2 1.7 collective-permute-done.6
  186.9 1.4 fusion.6
  188.4 5.5 %collective-permute-start.13 = (f32[3,4,2,1280]{3,2,1,0:T(2,128)S(1)}, f32[3,4,2,1280]{3,2,1,0:T(2,128)S(1)}, u32[]{:S(2)}, u32[]{:S(2)}) collective-permute-start(f32[3,4,2,1280]{3,2,1,0:T(2,128)S(1)} %pad_maximum_fusion.1), channel_id=1, source_target_pairs={{0,128},{32,160},{64,192},{96,224},{128,0},{160,32},{192,64},{224,... | collective-permute-start | bytes 368648 | tf_op jit(solution)/shard_map/ppermute | solution.py:339
  193.8 3.0 %select_convert_fusion = f16[32,8,1280]{2,1,0:T(8,128)(2,1)} fusion(f32[32,8,1280]{2,1,0:T(8,128)S(1)} %get-tuple-element.24, f32[]{:T(128)} %bitcast.17, f32[]{:T(128)} %bitcast.16, f32[]{:T(128)} %bitcast.15, f32[]{:T(128)} %bitcast.14, pred[1280]{0:T(1024)(128)(4,1)S(1)} %get-tuple-element.45, pred[1280]{0:T(1024)(128)(4,1)S(1)} %get-tuple-element.46, ...), kind=kLoop, calls=%fused_computation.1 | loop fusion | flops 1638400 | bytes 1969936 | tf_op jit(solution)/shard_map/convert_element_type | solution.py:264
  196.8 5.7 %all-to-all-start.3 = ((f16[32,8,1280]{2,1,0:T(8,128)(2,1)}), f16[32,8,1280]{2,1,0:T(8,128)(2,1)S(1)}, u32[]{:S(2)}, u32[]{:S(2)}) async-start(f16[32,8,1280]{2,1,0:T(8,128)(2,1)} %select_convert_fusion), calls=%async_computation.3 | async-start | bytes 1310720 | tf_op jit(solution)/shard_map/all_to_all | solution.py:327
  202.6 0.1 fusion.8
  202.7 2.4 %collective-permute-start.14 = (f32[3,2,2,1280]{3,2,1,0:T(2,128)S(1)}, f32[3,2,2,1280]{3,2,1,0:T(2,128)S(1)}, u32[]{:S(2)}, u32[]{:S(2)}) collective-permute-start(f32[3,2,2,1280]{3,2,1,0:T(2,128)S(1)} %slice.223), channel_id=1, source_target_pairs={{0,64},{32,96},{64,0},{96,32},{128,192},{160,224},{192,128},{224,1... | collective-permute-start | bytes 184328 | tf_op jit(solution)/shard_map/ppermute | solution.py:339
  205.1 0.2 select_reduce_fusion
  205.3 13.6 %collective-permute-done.14 = f32[3,2,2,1280]{3,2,1,0:T(2,128)S(1)} collective-permute-done((f32[3,2,2,1280]{3,2,1,0:T(2,128)S(1)}, f32[3,2,2,1280]{3,2,1,0:T(2,128)S(1)}, u32[]{:S(2)}, u32[]{:S(2)}) %collective-permute-start.14) | collective-permute-done | bytes 61472 | tf_op jit(solution)/shard_map/ppermute | solution.py:339
  218.9 0.5 collective-permute-start.15
  219.5 3.4 %collective-permute-done.15 = f32[3,1,2,1280]{3,2,1,0:T(2,128)S(1)} collective-permute-done((f32[3,1,2,1280]{3,2,1,0:T(2,128)S(1)}, f32[3,1,2,1280]{3,2,1,0:T(2,128)S(1)}, u32[]{:S(2)}, u32[]{:S(2)}) %collective-permute-start.15) | collective-permute-done | bytes 30752 | tf_op jit(solution)/shard_map/ppermute | solution.py:339
  223.0 0.1 convert_element_type.15
  223.1 0.6 fusion.16
  223.7 0.2 multiply_reduce_fusion
  223.9 3.9 %collective-permute-start.16 = (f32[16,1280]{1,0:T(8,128)S(1)}, f32[16,1280]{1,0:T(8,128)S(1)}, u32[]{:S(2)}, u32[]{:S(2)}) collective-permute-start(f32[16,1280]{1,0:T(8,128)S(1)} %get-tuple-element.36), channel_id=1, source_target_pairs={{0,1},{1,2},{2,3},{3,0},{4,5},{5,6},{6,7},{7,4},{8,9},{9,10},{10,1... | collective-permute-start | bytes 245768 | tf_op jit(solution)/shard_map/ppermute | solution.py:278
  227.8 4.1 %collective-permute-start.17 = (f32[16,1280]{1,0:T(8,128)S(1)}, f32[16,1280]{1,0:T(8,128)S(1)}, u32[]{:S(2)}, u32[]{:S(2)}) collective-permute-start(f32[16,1280]{1,0:T(8,128)S(1)} %get-tuple-element.36), channel_id=1, source_target_pairs={{0,2},{1,3},{2,0},{3,1},{4,6},{5,7},{6,4},{7,5},{8,10},{9,11},{10,... | collective-permute-start | bytes 245768 | tf_op jit(solution)/shard_map/ppermute | solution.py:278
  231.9 0.1 copy.13.pair_ref
  232.2 0.1 reshape.264
  232.4 0.5 collective-permute-done.16
  232.9 2.3 collective-permute-done.17
  235.2 1.1 collective-permute-done.18
  236.4 0.4 shard_map.89
  236.8 0.1 reshape.265
  237.0 0.1 broadcast_select_fusion
  237.1 0.7 copy.14
  (57 shorter events, 0.7 us)
Async XLA Ops:
  0.7 2.1 copy-start
  5.5 36.4 %all-to-all-start.1 = ((bf16[32,1,15,8,128]{4,3,2,1,0:T(8,128)(2,1)}), bf16[32,1,15,8,128]{4,3,2,1,0:T(8,128)(2,1)S(1)}, u32[]{:S(2)}, u32[]{:S(2)}) async-start(bf16[32,1,15,8,128]{4,3,2,1,0:T(8,128)(2,1)} %shard_map.85), calls=%async_computation.1 | async-start | bytes 1966080 | tf_op jit(solution)/shard_map/all_to_all | solution.py:323
  17.1 2.1 copy-start.1
  23.1 26.4 %copy-start.4 = (s32[1,1280]{1,0:T(1,128)S(1)}, s32[1,1280]{1,0:T(1,128)}, u32[]{:S(2)}) copy-start(s32[1,1280]{1,0:T(1,128)} %constant.71.clone.one_ref) | copy-start | bytes 15364
  23.1 26.4 %copy-start.5 = (s32[1,1280]{1,0:T(1,128)S(1)}, s32[1,1280]{1,0:T(1,128)}, u32[]{:S(2)}) copy-start(s32[1,1280]{1,0:T(1,128)} %constant.72.clone.two_ref) | copy-start | bytes 15364
  41.9 52.1 %all-to-all-start = ((bf16[32,2,15,8,128]{4,3,2,1,0:T(8,128)(2,1)}), bf16[32,2,15,8,128]{4,3,2,1,0:T(8,128)(2,1)}, u32[]{:S(2)}, u32[]{:S(2)}) async-start(bf16[32,2,15,8,128]{4,3,2,1,0:T(8,128)(2,1)} %shard_map.82), calls=%async_computation | async-start | bytes 3932160 | tf_op jit(solution)/shard_map/all_to_all | solution.py:323
  49.5 2.2 copy-start.3
  51.7 7.6 %copy-start.2 = (bf16[32,120,480]{2,1,0:T(8,128)(2,1)S(1)}, bf16[32,120,480]{2,1,0:T(8,128)(2,1)}, u32[]{:S(2)}) copy-start(bf16[32,120,480]{2,1,0:T(8,128)(2,1)} %param.8) | copy-start | bytes 11059204
  59.3 43.8 %collective-permute-start = (bf16[5,2,912,256]{3,2,1,0:T(8,128)(2,1)}, bf16[5,2,912,256]{3,2,1,0:T(8,128)(2,1)}, u32[]{:S(2)}, u32[]{:S(2)}) collective-permute-start(bf16[5,2,912,256]{3,2,1,0:T(8,128)(2,1)} %shard_map.83.refs_2_), channel_id=1, source_target_pairs={{0,4},{4,0},{1,5},{5,1},{2,6},{6,2},{3,7},{7,3},{8,12},{12,8},{9,1... | collective-permute-start | bytes 14008328 | tf_op jit(solution)/shard_map/ppermute | solution.py:316
  61.9 40.7 %copy-start.8 = (s32[32]{0:T(128)S(1)}, s32[32]{0:T(128)}, u32[]{:S(2)}) copy-start(s32[32]{0:T(128)} %param.10) | copy-start | bytes 388
  93.9 38.1 %all-to-all-start.2 = ((bf16[32,1,15,8,128]{4,3,2,1,0:T(8,128)(2,1)}), bf16[32,1,15,8,128]{4,3,2,1,0:T(8,128)(2,1)S(1)}, u32[]{:S(2)}, u32[]{:S(2)}) async-start(bf16[32,1,15,8,128]{4,3,2,1,0:T(8,128)(2,1)} %shard_map.87), calls=%async_computation.2 | async-start | bytes 1966080 | tf_op jit(solution)/shard_map/all_to_all | solution.py:323
  111.4 19.0 %collective-permute-start.7 = (f32[4,1,8,2,1280]{4,3,2,1,0:T(2,128)S(1)}, f32[4,1,8,2,1280]{4,3,2,1,0:T(2,128)S(1)}, u32[]{:S(2)}, u32[]{:S(2)}) collective-permute-start(f32[4,1,8,2,1280]{4,3,2,1,0:T(2,128)S(1)} %get-tuple-element.20), channel_id=1, source_target_pairs={{0,1},{1,2},{2,3},{3,0},{4,5},{5,6},{6,7},{7,4},{8,9},{9,10},{10,1... | collective-permute-start | bytes 983048 | tf_op jit(solution)/shard_map/ppermute | solution.py:278
  124.2 49.4 %collective-permute-start.1 = (f32[4,2,8,2,1280]{4,3,2,1,0:T(2,128)}, f32[4,2,8,2,1280]{4,3,2,1,0:T(2,128)}, u32[]{:S(2)}, u32[]{:S(2)}) collective-permute-start(f32[4,2,8,2,1280]{4,3,2,1,0:T(2,128)} %get-tuple-element.16), channel_id=1, source_target_pairs={{0,1},{1,2},{2,3},{3,0},{4,5},{5,6},{6,7},{7,4},{8,9},{9,10},{10,1... | collective-permute-start | bytes 1966088 | tf_op jit(solution)/shard_map/ppermute | solution.py:278
  125.8 50.0 %collective-permute-start.2 = (f32[4,2,8,2,1280]{4,3,2,1,0:T(2,128)}, f32[4,2,8,2,1280]{4,3,2,1,0:T(2,128)}, u32[]{:S(2)}, u32[]{:S(2)}) collective-permute-start(f32[4,2,8,2,1280]{4,3,2,1,0:T(2,128)} %get-tuple-element.17), channel_id=1, source_target_pairs={{0,2},{1,3},{2,0},{3,1},{4,6},{5,7},{6,4},{7,5},{8,10},{9,11},{10,... | collective-permute-start | bytes 1966088 | tf_op jit(solution)/shard_map/ppermute | solution.py:278
  127.3 48.4 %collective-permute-start.3 = (f32[4,2,8,2,1280]{4,3,2,1,0:T(2,128)S(1)}, f32[4,2,8,2,1280]{4,3,2,1,0:T(2,128)}, u32[]{:S(2)}, u32[]{:S(2)}) collective-permute-start(f32[4,2,8,2,1280]{4,3,2,1,0:T(2,128)S(1)} %get-tuple-element.18), channel_id=1, source_target_pairs={{0,3},{1,0},{2,1},{3,2},{4,7},{5,4},{6,5},{7,6},{8,11},{9,8},{10,9... | collective-permute-start | bytes 1966088 | tf_op jit(solution)/shard_map/ppermute | solution.py:278
  129.7 32.2 %collective-permute-start.8 = (f32[4,1,8,2,1280]{4,3,2,1,0:T(2,128)}, f32[4,1,8,2,1280]{4,3,2,1,0:T(2,128)}, u32[]{:S(2)}, u32[]{:S(2)}) collective-permute-start(f32[4,1,8,2,1280]{4,3,2,1,0:T(2,128)} %get-tuple-element.21), channel_id=1, source_target_pairs={{0,2},{1,3},{2,0},{3,1},{4,6},{5,7},{6,4},{7,5},{8,10},{9,11},{10,... | collective-permute-start | bytes 983048 | tf_op jit(solution)/shard_map/ppermute | solution.py:278
  130.4 39.3 %collective-permute-start.9 = (f32[4,1,8,2,1280]{4,3,2,1,0:T(2,128)S(1)}, f32[4,1,8,2,1280]{4,3,2,1,0:T(2,128)}, u32[]{:S(2)}, u32[]{:S(2)}) collective-permute-start(f32[4,1,8,2,1280]{4,3,2,1,0:T(2,128)S(1)} %get-tuple-element.22), channel_id=1, source_target_pairs={{0,3},{1,0},{2,1},{3,2},{4,7},{5,4},{6,5},{7,6},{8,11},{9,8},{10,9... | collective-permute-start | bytes 983048 | tf_op jit(solution)/shard_map/ppermute | solution.py:278
  170.9 10.3 %collective-permute-start.10 = (f32[1,8,2,1280]{3,2,1,0:T(2,128)S(1)}, f32[1,8,2,1280]{3,2,1,0:T(2,128)S(1)}, u32[]{:S(2)}, u32[]{:S(2)}) collective-permute-start(f32[1,8,2,1280]{3,2,1,0:T(2,128)S(1)} %get-tuple-element.32), channel_id=1, source_target_pairs={{0,8},{8,16},{16,24},{24,0},{1,9},{9,17},{17,25},{25,1},{2,10},{10... | collective-permute-start | bytes 245768 | tf_op jit(solution)/shard_map/ppermute | solution.py:278
  172.5 8.7 %collective-permute-start.11 = (f32[1,8,2,1280]{3,2,1,0:T(2,128)S(1)}, f32[1,8,2,1280]{3,2,1,0:T(2,128)S(1)}, u32[]{:S(2)}, u32[]{:S(2)}) collective-permute-start(f32[1,8,2,1280]{3,2,1,0:T(2,128)S(1)} %get-tuple-element.34), channel_id=1, source_target_pairs={{0,16},{8,24},{16,0},{24,8},{1,17},{9,25},{17,1},{25,9},{2,18},{10... | collective-permute-start | bytes 245768 | tf_op jit(solution)/shard_map/ppermute | solution.py:278
  173.6 7.6 %collective-permute-start.12 = (f32[1,8,2,1280]{3,2,1,0:T(2,128)S(1)}, f32[1,8,2,1280]{3,2,1,0:T(2,128)S(1)}, u32[]{:S(2)}, u32[]{:S(2)}) collective-permute-start(f32[1,8,2,1280]{3,2,1,0:T(2,128)S(1)} %get-tuple-element.33), channel_id=1, source_target_pairs={{0,24},{8,0},{16,8},{24,16},{1,25},{9,1},{17,9},{25,17},{2,26},{10... | collective-permute-start | bytes 245768 | tf_op jit(solution)/shard_map/ppermute | solution.py:278
  177.6 5.9 %collective-permute-start.4 = (f32[2,8,2,1280]{3,2,1,0:T(2,128)S(1)}, f32[2,8,2,1280]{3,2,1,0:T(2,128)S(1)}, u32[]{:S(2)}, u32[]{:S(2)}) collective-permute-start(f32[2,8,2,1280]{3,2,1,0:T(2,128)S(1)} %get-tuple-element.29), channel_id=1, source_target_pairs={{0,8},{8,16},{16,24},{24,0},{1,9},{9,17},{17,25},{25,1},{2,10},{10... | collective-permute-start | bytes 491528 | tf_op jit(solution)/shard_map/ppermute | solution.py:278
  177.7 7.5 %collective-permute-start.5 = (f32[2,8,2,1280]{3,2,1,0:T(2,128)S(1)}, f32[2,8,2,1280]{3,2,1,0:T(2,128)S(1)}, u32[]{:S(2)}, u32[]{:S(2)}) collective-permute-start(f32[2,8,2,1280]{3,2,1,0:T(2,128)S(1)} %get-tuple-element.31), channel_id=1, source_target_pairs={{0,16},{8,24},{16,0},{24,8},{1,17},{9,25},{17,1},{25,9},{2,18},{10... | collective-permute-start | bytes 491528 | tf_op jit(solution)/shard_map/ppermute | solution.py:278
  181.2 5.7 %collective-permute-start.6 = (f32[2,8,2,1280]{3,2,1,0:T(2,128)S(1)}, f32[2,8,2,1280]{3,2,1,0:T(2,128)S(1)}, u32[]{:S(2)}, u32[]{:S(2)}) collective-permute-start(f32[2,8,2,1280]{3,2,1,0:T(2,128)S(1)} %get-tuple-element.30), channel_id=1, source_target_pairs={{0,24},{8,0},{16,8},{24,16},{1,25},{9,1},{17,9},{25,17},{2,26},{10... | collective-permute-start | bytes 491528 | tf_op jit(solution)/shard_map/ppermute | solution.py:278
  188.4 14.2 %collective-permute-start.13 = (f32[3,4,2,1280]{3,2,1,0:T(2,128)S(1)}, f32[3,4,2,1280]{3,2,1,0:T(2,128)S(1)}, u32[]{:S(2)}, u32[]{:S(2)}) collective-permute-start(f32[3,4,2,1280]{3,2,1,0:T(2,128)S(1)} %pad_maximum_fusion.1), channel_id=1, source_target_pairs={{0,128},{32,160},{64,192},{96,224},{128,0},{160,32},{192,64},{224,... | collective-permute-start | bytes 368648 | tf_op jit(solution)/shard_map/ppermute | solution.py:339
  196.8 8.3 %copy-start.6 = (f32[48]{0:T(128)S(1)}, f32[48]{0:T(128)}, u32[]{:S(2)}) copy-start(f32[48]{0:T(128)} %param.11) | copy-start | bytes 580
  196.8 26.2 %all-to-all-start.3 = ((f16[32,8,1280]{2,1,0:T(8,128)(2,1)}), f16[32,8,1280]{2,1,0:T(8,128)(2,1)S(1)}, u32[]{:S(2)}, u32[]{:S(2)}) async-start(f16[32,8,1280]{2,1,0:T(8,128)(2,1)} %select_convert_fusion), calls=%async_computation.3 | async-start | bytes 1310720 | tf_op jit(solution)/shard_map/all_to_all | solution.py:327
  202.7 16.2 %collective-permute-start.14 = (f32[3,2,2,1280]{3,2,1,0:T(2,128)S(1)}, f32[3,2,2,1280]{3,2,1,0:T(2,128)S(1)}, u32[]{:S(2)}, u32[]{:S(2)}) collective-permute-start(f32[3,2,2,1280]{3,2,1,0:T(2,128)S(1)} %slice.223), channel_id=1, source_target_pairs={{0,64},{32,96},{64,0},{96,32},{128,192},{160,224},{192,128},{224,1... | collective-permute-start | bytes 184328 | tf_op jit(solution)/shard_map/ppermute | solution.py:339
  218.9 4.0 %collective-permute-start.15 = (f32[3,1,2,1280]{3,2,1,0:T(2,128)S(1)}, f32[3,1,2,1280]{3,2,1,0:T(2,128)S(1)}, u32[]{:S(2)}, u32[]{:S(2)}) collective-permute-start(f32[3,1,2,1280]{3,2,1,0:T(2,128)S(1)} %slice.225), channel_id=1, source_target_pairs={{0,32},{32,0},{64,96},{96,64},{128,160},{160,128},{192,224},{224,1... | collective-permute-start | bytes 92168 | tf_op jit(solution)/shard_map/ppermute | solution.py:339
  223.0 9.1 %copy-start.7 = (f32[48]{0:T(128)S(1)}, f32[48]{0:T(128)}, u32[]{:S(2)}) copy-start(f32[48]{0:T(128)} %param.12) | copy-start | bytes 580
  223.9 9.0 %collective-permute-start.16 = (f32[16,1280]{1,0:T(8,128)S(1)}, f32[16,1280]{1,0:T(8,128)S(1)}, u32[]{:S(2)}, u32[]{:S(2)}) collective-permute-start(f32[16,1280]{1,0:T(8,128)S(1)} %get-tuple-element.36), channel_id=1, source_target_pairs={{0,1},{1,2},{2,3},{3,0},{4,5},{5,6},{6,7},{7,4},{8,9},{9,10},{10,1... | collective-permute-start | bytes 245768 | tf_op jit(solution)/shard_map/ppermute | solution.py:278
  227.8 7.4 %collective-permute-start.17 = (f32[16,1280]{1,0:T(8,128)S(1)}, f32[16,1280]{1,0:T(8,128)S(1)}, u32[]{:S(2)}, u32[]{:S(2)}) collective-permute-start(f32[16,1280]{1,0:T(8,128)S(1)} %get-tuple-element.36), channel_id=1, source_target_pairs={{0,2},{1,3},{2,0},{3,1},{4,6},{5,7},{6,4},{7,5},{8,10},{9,11},{10,... | collective-permute-start | bytes 245768 | tf_op jit(solution)/shard_map/ppermute | solution.py:278
  231.9 4.4 %collective-permute-start.18 = (f32[16,1280]{1,0:T(8,128)S(1)}, f32[16,1280]{1,0:T(8,128)S(1)}, u32[]{:S(2)}, u32[]{:S(2)}) collective-permute-start(f32[16,1280]{1,0:T(8,128)S(1)} %get-tuple-element.36), channel_id=1, source_target_pairs={{0,3},{1,0},{2,1},{3,2},{4,7},{5,4},{6,5},{7,6},{8,11},{9,8},{10,9... | collective-permute-start | bytes 245768 | tf_op jit(solution)/shard_map/ppermute | solution.py:278

commit v5 on v4

--- a/solution.py
+++ b/solution.py
@@ -9,12 +9,13 @@
 ROWS = 8
 LEFT = 16
 COPIES = 2
+LADDER_MIB = 60
 LANES = 128
 BF = jnp.bfloat16
 F32 = jnp.float32
 
 
-def params(mib=40):
+def params(mib):
     return pltpu.CompilerParams(vmem_limit_bytes=mib * 1024 * 1024)
 
 
@@ -97,7 +98,7 @@
             ],
         ),
         out_shape=jax.ShapeDtypeStruct((xs * zs, size, tiles, ROWS, LANES), BF),
-        compiler_params=params(),
+        compiler_params=params(60),
         cost_estimate=pl.CostEstimate(flops=0, bytes_accessed=8_000_000, transcendentals=0),
     )(where, view)
 
@@ -128,7 +129,7 @@
         ],
         out_specs=pl.BlockSpec((1, 2, padded, block), lambda i: (i, 0, 0, 0)),
         out_shape=jax.ShapeDtypeStruct((count // block, 2, padded, block), BF),
-        compiler_params=params(),
+        compiler_params=params(60),
         cost_estimate=pl.CostEstimate(
             flops=2 * width * full * count, bytes_accessed=10_000_000, transcendentals=0
         ),
@@ -159,8 +160,8 @@
                             tile = (1 - core) * whole + t - whole
                         else:
                             tile = t
-                        pair = jnp.concatenate([x_ref[q, i, tile].astype(F32) for q in pick], axis=0)
-                        lhs[at : at + 2 * ROWS, t * LANES : (t + 1) * LANES] = pair.astype(BF)
+                        pair = jnp.concatenate([x_ref[q, i, tile] for q in pick], axis=0)
+                        lhs[at : at + 2 * ROWS, t * LANES : (t + 1) * LANES] = pair
 
     total = jnp.zeros((lhs.shape[0], own_ref.shape[3]), F32)
     for part in range(2):
@@ -215,7 +216,7 @@
             inverses.append(inverse)
         lane = lax.broadcasted_iota(jnp.int32, f_ref.shape, 1)
         out = jnp.zeros(f_ref.shape, F32)
-        for n, value in enumerate(factors + inverses):
+        for n, value in enumerate([factors[0] * factors[1] * factors[2]] + inverses):
             out = jnp.where(lane == n, value, out)
         f_ref[...] = out
 
@@ -246,7 +247,7 @@
             scratch_shapes=scratch,
         ),
         out_shape=[jax.ShapeDtypeStruct(shape, F32) for shape in shapes],
-        compiler_params=params(),
+        compiler_params=params(LADDER_MIB),
         cost_estimate=pl.CostEstimate(
             flops=4 * size * chips * ROWS * tiles * LANES * count,
             bytes_accessed=size * 3_000_000 + 9_000_000,
@@ -258,9 +259,9 @@
 def encode(partial, factors):
     count = partial.shape[2]
     lane = lax.broadcasted_iota(jnp.int32, partial.shape, 2)
-    coded = partial * (factors[0, 0] * factors[0, 1] * factors[0, 2])
+    coded = partial * factors[0, 0]
     for n in range(3):
-        coded = jnp.where(lane == count - 1 - n, factors[0, 3 + n], coded)
+        coded = jnp.where(lane == count - 1 - n, factors[0, 1 + n], coded)
     return coded.astype(jnp.float16)
 
 
@@ -332,11 +333,11 @@
         partial = [further(block, "x", r) for r, block in enumerate(partial)]
         done.append(sum(partial[1:], partial[0]))
     mine = jnp.concatenate(done, axis=0)
-    half = zs
-    while half > 1:
-        half //= 2
-        swap = [(i, i ^ half) for i in range(zs)]
-        mine = mine[:, :half] + lax.ppermute(mine[:, half:], "z", swap)
+    apart = [mine[:, s] for s in range(zs)]
+    apart = [apart[0]] + [
+        lax.ppermute(apart[s], "z", [(i, i ^ s) for i in range(zs)]) for s in range(1, zs)
+    ]
+    mine = sum(apart[1:], apart[0])
     mine = mine.reshape(-1, count)
     mine = jnp.concatenate([jnp.pad(mine, ((0, COPIES), (0, 0))), last], axis=0)
     everyone = jnp.stack([further(mine, "y", k) for k in range(ys)])
@@ -358,7 +359,7 @@
         in_specs=[pl.BlockSpec(memory_space=pltpu.SMEM)] + [pl.BlockSpec(memory_space=pltpu.VMEM)] * 5,
         out_shape=jax.ShapeDtypeStruct((slots, full), F32),
         scratch_shapes=[pltpu.VMEM((ys, slots // ys, count), F32)],
-        compiler_params=params(),
+        compiler_params=params(24),
     )(place[None], everyone, column, pair_sum[:, None], ea, eb)
     update = update[:, :wide].reshape(slots, local_rows, window)
     return jnp.where(filled[:, None, None], update, jnp.zeros_like(update))

time: 239 us -> 221 us (0.925)
  waiting for transfers between devices: 104 us -> 75.4 us
  Pallas kernels: 44.4 us -> 53.2 us
  starting transfers between devices: 67.7 us -> 73.7 us
  local copies, waits for them, and re-layouts: 8.64 us -> 4.96 us
    ppermute x15, waiting for transfers between devices: 35.8 us -> 21.3 us  [further(): lax.ppermute(block, axis, [(i, (i + hops) % size) for i in range(size)])]
    ppermute x3 -> x7, waiting for transfers between devices: 17 us -> 3.9 us  [body(): lax.ppermute(apart[s], 'z', [(i, i ^ s) for i in range(zs)])]
    ppermute x3 -> x7, starting transfers between devices: 8.46 us -> 13.7 us  [body(): lax.ppermute(apart[s], 'z', [(i, i ^ s) for i in range(zs)])]
    unnamed x18 -> x16, local copies, waits for them, and re-layouts: 6.42 us -> 1.93 us
    all_to_all x1, starting transfers between devices: 5.71 us -> 9.91 us  [body(): coded = lax.all_to_all(coded, ('x', 'z'), 0, 0, tiled=True)]
    pallas_call x3, Pallas kernels: 9.09 us -> 12.8 us  [flatten(): pl.pallas_call(lambda *refs: flatten_kernel(xs, zs, width, *refs), grid_s...]
    ppermute x15, starting transfers between devices: 25.8 us -> 22.4 us  [further(): lax.ppermute(block, axis, [(i, (i + hops) % size) for i in range(size)])]
    pallas_call x3, Pallas kernels: 27.3 us -> 30 us  [ladder(): pl.pallas_call(lambda *refs: kernel(xs, *refs), grid_spec=pltpu.PrefetchS...]
  transfers between devices with their start and end apart: 23 -> 27, of which waited for: 12 -> 12; matrix products, arithmetic and copies ran while one was open for 4% -> 5% of each run, Pallas kernels for 17% -> 22%
where the time goes in v5:
time: 221 us; the launch traced here: 219 us
  waiting for transfers between devices  75.4 us (34%)
  starting transfers between devices  73.7 us (33%)
  Pallas kernels  53.2 us (24%)
  other arithmetic  11.5 us (5%)
  local copies, waits for them, and re-layouts  4.96 us (2%)
    all_to_all x3, waiting for transfers between devices, body(): panels = lax.all_to_all(flat, ('x', 'z'), 0, 0, tiled=True)  50.2 us
    pallas_call x3, Pallas kernels, ladder(): pl.pallas_call(lambda *refs: kernel(xs, *refs), grid_spec=pltpu.PrefetchS...  30 us
    all_to_all x3, starting transfers between devices, body(): panels = lax.all_to_all(flat, ('x', 'z'), 0, 0, tiled=True)  27.6 us
    ppermute x15, starting transfers between devices, further(): lax.ppermute(block, axis, [(i, (i + hops) % size) for i in range(size)])  22.4 us
    ppermute x15, waiting for transfers between devices, further(): lax.ppermute(block, axis, [(i, (i + hops) % size) for i in range(size)])  21.3 us
    ppermute x7, starting transfers between devices, body(): lax.ppermute(apart[s], 'z', [(i, i ^ s) for i in range(zs)])  13.7 us
    pallas_call x3, Pallas kernels, flatten(): pl.pallas_call(lambda *refs: flatten_kernel(xs, zs, width, *refs), grid_s...  12.8 us
    pallas_call x1, Pallas kernels, fold(): pl.pallas_call(fold_kernel, grid=(count // block,), in_specs=[pl.BlockSpe...  9.93 us
  transfers between devices with their start and end apart: 27, of which 12 were waited for; matrix products, arithmetic and copies ran while one was open for 5% of the time, Pallas kernels for 22%

profile of v5, /device:TPU:2, one launch (start us, length us, event | category | flops | bytes accessed | tf_op | source)
XLA Modules:
  0.0 219.0 jit_solution(15702701197962167027)
XLA Ops:
  0.0 1.3 fusion.42
  1.3 3.9 %shard_map.85 = bf16[32,1,15,8,128]{4,3,2,1,0:T(8,128)(2,1)} custom-call(s32[4]{0:T(128)} %get-tuple-element.28.refs_0_, bf16[4,4,2,120,480]{4,3,2,1,0:T(8,128)(2,1)} %bitcast.89), custom_call_target="tpu_custom_call" | custom-call | bytes 8000000 | tf_op jit(solution)/shard_map/pallas_call | solution.py:86
  5.2 11.6 %all-to-all-start.1 = ((bf16[32,1,15,8,128]{4,3,2,1,0:T(8,128)(2,1)}), bf16[32,1,15,8,128]{4,3,2,1,0:T(8,128)(2,1)S(1)}, u32[]{:S(2)}, u32[]{:S(2)}) async-start(bf16[32,1,15,8,128]{4,3,2,1,0:T(8,128)(2,1)} %shard_map.85), calls=%async_computation.1 | async-start | bytes 1966080 | tf_op jit(solution)/shard_map/all_to_all | solution.py:324
  16.8 5.0 %shard_map.82 = bf16[32,2,15,8,128]{4,3,2,1,0:T(8,128)(2,1)} custom-call(s32[4]{0:T(128)} %get-tuple-element.28.refs_0_, bf16[4,4,2,120,480]{4,3,2,1,0:T(8,128)(2,1)} %bitcast.90), custom_call_target="tpu_custom_call" | custom-call | bytes 8000000 | tf_op jit(solution)/shard_map/pallas_call | solution.py:86
  21.8 19.8 %all-to-all-done.1.refs_1_ = bf16[32,1,15,8,128]{4,3,2,1,0:T(8,128)(2,1)S(1)} async-done(((bf16[32,1,15,8,128]{4,3,2,1,0:T(8,128)(2,1)}), bf16[32,1,15,8,128]{4,3,2,1,0:T(8,128)(2,1)S(1)}, u32[]{:S(2)}, u32[]{:S(2)}) %all-to-all-start.1) | async-done | bytes 983072 | tf_op jit(solution)/shard_map/all_to_all | solution.py:324
  41.6 1.0 copy-done
  42.6 7.6 %all-to-all-start = ((bf16[32,2,15,8,128]{4,3,2,1,0:T(8,128)(2,1)}), bf16[32,2,15,8,128]{4,3,2,1,0:T(8,128)(2,1)S(1)}, u32[]{:S(2)}, u32[]{:S(2)}) async-start(bf16[32,2,15,8,128]{4,3,2,1,0:T(8,128)(2,1)} %shard_map.82), calls=%async_computation | async-start | bytes 3932160 | tf_op jit(solution)/shard_map/all_to_all | solution.py:324
  50.1 9.9 %shard_map.83.refs_2_ = bf16[5,2,912,256]{3,2,1,0:T(8,128)(2,1)} custom-call(s32[1,1280]{1,0:T(1,128)} %constant.71.clone.one_ref, s32[1,1280]{1,0:T(1,128)} %constant.72.clone.two_ref, bf16[900,2304]{1,0:T(8,128)(2,1)} %bitcast.95), custom_call_target="tpu_custom_call" | custom-call | flops 5308416000 | bytes 10000000 | tf_op jit(solution)/shard_map/pallas_call | solution.py:122
  60.1 3.9 %shard_map.87 = bf16[32,1,15,8,128]{4,3,2,1,0:T(8,128)(2,1)} custom-call(s32[4]{0:T(128)} %get-tuple-element.27.refs_0_, bf16[4,4,2,120,480]{4,3,2,1,0:T(8,128)(2,1)} %bitcast.91), custom_call_target="tpu_custom_call" | custom-call | bytes 8000000 | tf_op jit(solution)/shard_map/pallas_call | solution.py:86
  64.1 30.4 %all-to-all-done.refs_1_ = bf16[32,2,15,8,128]{4,3,2,1,0:T(8,128)(2,1)S(1)} async-done(((bf16[32,2,15,8,128]{4,3,2,1,0:T(8,128)(2,1)}), bf16[32,2,15,8,128]{4,3,2,1,0:T(8,128)(2,1)S(1)}, u32[]{:S(2)}, u32[]{:S(2)}) %all-to-all-start) | async-done | bytes 1966112 | tf_op jit(solution)/shard_map/all_to_all | solution.py:324
  94.5 8.5 %all-to-all-start.2 = ((bf16[32,1,15,8,128]{4,3,2,1,0:T(8,128)(2,1)}), bf16[32,1,15,8,128]{4,3,2,1,0:T(8,128)(2,1)S(1)}, u32[]{:S(2)}, u32[]{:S(2)}) async-start(bf16[32,1,15,8,128]{4,3,2,1,0:T(8,128)(2,1)} %shard_map.87), calls=%async_computation.2 | async-start | bytes 1966080 | tf_op jit(solution)/shard_map/all_to_all | solution.py:324
  103.3 0.2 convert_reduce_fusion
  103.4 0.2 select_reduce_fusion.1
  103.7 11.8 %shard_map.84 = (f32[4,2,8,2,1280]{4,3,2,1,0:T(2,128)}, f32[4,2,8,2,1280]{4,3,2,1,0:T(2,128)}, f32[4,2,8,2,1280]{4,3,2,1,0:T(2,128)}, f32[4,2,8,2,1280]{4,3,2,1,0:T(2,128)}) custom-call(s32[4]{0:T(128)} %get-tuple-element.28.refs_0_, bf16[32,2,15,8,128]{4,3,2,1,0:T(8,128)(2,1)} %copy-done.2, bf16[5,2,912,256]{3,2,1,0:T(8,128)(2,1)} %shard_map.83.refs_2_, ...), custom_call_target="tpu_custom_call" | custom-call | flops 5033164800 | bytes 15000000 | tf_op jit(solution)/shard_map/pallas_call | solution.py:236
  115.4 1.6 collective-permute-start.1
  117.0 2.9 %collective-permute-start.2 = (f32[4,2,8,2,1280]{4,3,2,1,0:T(2,128)}, f32[4,2,8,2,1280]{4,3,2,1,0:T(2,128)S(1)}, u32[]{:S(2)}, u32[]{:S(2)}) collective-permute-start(f32[4,2,8,2,1280]{4,3,2,1,0:T(2,128)} %get-tuple-element.17), channel_id=1, source_target_pairs={{0,2},{1,3},{2,0},{3,1},{4,6},{5,7},{6,4},{7,5},{8,10},{9,11},{10,... | collective-permute-start | bytes 1966088 | tf_op jit(solution)/shard_map/ppermute | solution.py:279
  119.9 1.3 collective-permute-start.3
  121.3 9.0 %shard_map.86 = (f32[4,1,8,2,1280]{4,3,2,1,0:T(2,128)}, f32[4,1,8,2,1280]{4,3,2,1,0:T(2,128)}, f32[4,1,8,2,1280]{4,3,2,1,0:T(2,128)}, f32[4,1,8,2,1280]{4,3,2,1,0:T(2,128)}) custom-call(s32[4]{0:T(128)} %get-tuple-element.28.refs_0_, bf16[32,1,15,8,128]{4,3,2,1,0:T(8,128)(2,1)} %copy-done, bf16[5,2,912,256]{3,2,1,0:T(8,128)(2,1)} %shard_map.83.refs_2_, ...), custom_call_target="tpu_custom_call" | custom-call | flops 2516582400 | bytes 12000000 | tf_op jit(solution)/shard_map/pallas_call | solution.py:236
  130.3 0.7 collective-permute-start.7
  131.0 0.8 collective-permute-start.8
  131.8 0.9 copy-done.1
  132.7 9.2 %shard_map.88 = (f32[32,8,1280]{2,1,0:T(8,128)}, f32[8,128]{1,0:T(8,128)}) custom-call(s32[4]{0:T(128)} %get-tuple-element.27.refs_0_, bf16[32,1,15,8,128]{4,3,2,1,0:T(8,128)(2,1)} %copy-done.1, bf16[5,2,912,256]{3,2,1,0:T(8,128)(2,1)} %shard_map.83.refs_2_, bf16[5,2,912,256]{3,2,1,0:T(8,128)(2,1)} %collective-permute-done.refs_3_), custom_call_target="tpu_custom_call" | custom-call | flops 2516582400 | bytes 12000000 | tf_op jit(solution)/shard_map/pallas_call | solution.py:236
  141.9 1.5 fusion.43
  143.4 11.0 %collective-permute-done.7 = f32[4,1,8,2,1280]{4,3,2,1,0:T(2,128)S(1)} collective-permute-done((f32[4,1,8,2,1280]{4,3,2,1,0:T(2,128)}, f32[4,1,8,2,1280]{4,3,2,1,0:T(2,128)S(1)}, u32[]{:S(2)}, u32[]{:S(2)}) %collective-permute-start.7) | collective-permute-done | bytes 327712 | tf_op jit(solution)/shard_map/ppermute | solution.py:279
  154.4 3.0 %collective-permute-start.9 = (f32[4,1,8,2,1280]{4,3,2,1,0:T(2,128)}, f32[4,1,8,2,1280]{4,3,2,1,0:T(2,128)}, u32[]{:S(2)}, u32[]{:S(2)}) collective-permute-start(f32[4,1,8,2,1280]{4,3,2,1,0:T(2,128)} %get-tuple-element.22), channel_id=1, source_target_pairs={{0,3},{1,0},{2,1},{3,2},{4,7},{5,4},{6,5},{7,6},{8,11},{9,8},{10,9... | collective-permute-start | bytes 983048 | tf_op jit(solution)/shard_map/ppermute | solution.py:279
  157.4 5.0 %select_convert_fusion = f16[32,8,1280]{2,1,0:T(8,128)(2,1)} fusion(f32[32,8,1280]{2,1,0:T(8,128)} %get-tuple-element.24, f32[]{:T(128)} %bitcast.25, f32[]{:T(128)} %bitcast.24, f32[]{:T(128)} %bitcast.23, f32[]{:T(128)} %bitcast.22, pred[1280]{0:T(1024)(128)(4,1)S(1)} %get-tuple-element.50, pred[1280]{0:T(1024)(128)(4,1)S(1)} %get-tuple-element.51, ...), kind=kLoop, calls=%fused_computation.1 | loop fusion | flops 1638400 | bytes 1969936 | tf_op jit(solution)/shard_map/convert_element_type | solution.py:265
  162.4 9.9 %all-to-all-start.3 = ((f16[32,8,1280]{2,1,0:T(8,128)(2,1)}), f16[32,8,1280]{2,1,0:T(8,128)(2,1)S(1)}, u32[]{:S(2)}, u32[]{:S(2)}) async-start(f16[32,8,1280]{2,1,0:T(8,128)(2,1)} %select_convert_fusion), calls=%async_computation.3 | async-start | bytes 1310720 | tf_op jit(solution)/shard_map/all_to_all | solution.py:328
  172.4 1.5 fusion.9
  173.9 1.5 collective-permute-start.10
  175.4 0.8 collective-permute-start.11
  176.2 2.4 %collective-permute-start.12 = (f32[1,8,2,1280]{3,2,1,0:T(2,128)S(1)}, f32[1,8,2,1280]{3,2,1,0:T(2,128)S(1)}, u32[]{:S(2)}, u32[]{:S(2)}) collective-permute-start(f32[1,8,2,1280]{3,2,1,0:T(2,128)S(1)} %get-tuple-element.33), channel_id=1, source_target_pairs={{0,24},{8,0},{16,8},{24,16},{1,25},{9,1},{17,9},{25,17},{2,26},{10... | collective-permute-start | bytes 245768 | tf_op jit(solution)/shard_map/ppermute | solution.py:279
  178.7 0.4 fusion.2
  179.1 0.1 collective-permute-start.4
  179.2 3.5 %collective-permute-start.5 = (f32[2,8,2,1280]{3,2,1,0:T(2,128)S(1)}, f32[2,8,2,1280]{3,2,1,0:T(2,128)S(1)}, u32[]{:S(2)}, u32[]{:S(2)}) collective-permute-start(f32[2,8,2,1280]{3,2,1,0:T(2,128)S(1)} %get-tuple-element.31), channel_id=1, source_target_pairs={{0,16},{8,24},{16,0},{24,8},{1,17},{9,25},{17,1},{25,9},{2,18},{10... | collective-permute-start | bytes 491528 | tf_op jit(solution)/shard_map/ppermute | solution.py:279
  182.7 1.2 collective-permute-done.11
  183.9 2.6 %collective-permute-done.12 = f32[1,8,2,1280]{3,2,1,0:T(2,128)S(1)} collective-permute-done((f32[1,8,2,1280]{3,2,1,0:T(2,128)S(1)}, f32[1,8,2,1280]{3,2,1,0:T(2,128)S(1)}, u32[]{:S(2)}, u32[]{:S(2)}) %collective-permute-start.12) | collective-permute-done | bytes 81952 | tf_op jit(solution)/shard_map/ppermute | solution.py:279
  186.6 1.1 fusion.13
  187.7 1.7 collective-permute-done.5
  189.4 1.5 collective-permute-done.6
  190.9 0.2 fusion.6
  191.1 0.1 fusion.32
  191.2 1.1 collective-permute-start.13
  192.4 2.9 %collective-permute-start.14 = (f32[3,2,1280]{2,1,0:T(2,128)S(1)}, f32[3,2,1280]{2,1,0:T(2,128)S(1)}, u32[]{:S(2)}, u32[]{:S(2)}) collective-permute-start(f32[3,2,1280]{2,1,0:T(2,128)S(1)} %get-tuple-element.36), channel_id=1, source_target_pairs={{0,64},{32,96},{64,0},{96,32},{128,192},{160,224},{192,128},{224,1... | collective-permute-start | bytes 92168 | tf_op jit(solution)/shard_map/ppermute | solution.py:338
  195.2 0.2 select_reduce_fusion
  195.4 0.6 collective-permute-start.15
  196.0 4.7 %collective-permute-start.16 = (f32[3,2,1280]{2,1,0:T(2,128)S(1)}, f32[3,2,1280]{2,1,0:T(2,128)S(1)}, u32[]{:S(2)}, u32[]{:S(2)}) collective-permute-start(f32[3,2,1280]{2,1,0:T(2,128)S(1)} %get-tuple-element.38), channel_id=1, source_target_pairs={{0,128},{32,160},{64,192},{96,224},{128,0},{160,32},{192,64},{224,... | collective-permute-start | bytes 92168 | tf_op jit(solution)/shard_map/ppermute | solution.py:338
  200.7 3.3 %collective-permute-start.18 = (f32[3,2,1280]{2,1,0:T(2,128)S(1)}, f32[3,2,1280]{2,1,0:T(2,128)S(1)}, u32[]{:S(2)}, u32[]{:S(2)}) collective-permute-start(f32[3,2,1280]{2,1,0:T(2,128)S(1)} %get-tuple-element.41), channel_id=1, source_target_pairs={{0,192},{32,224},{64,128},{96,160},{128,64},{160,96},{192,0},{224,... | collective-permute-start | bytes 92168 | tf_op jit(solution)/shard_map/ppermute | solution.py:338
  204.0 1.2 collective-permute-start.19
  205.2 2.4 %collective-permute-done.17 = f32[3,2,1280]{2,1,0:T(2,128)S(1)} collective-permute-done((f32[3,2,1280]{2,1,0:T(2,128)S(1)}, f32[3,2,1280]{2,1,0:T(2,128)S(1)}, u32[]{:S(2)}, u32[]{:S(2)}) %collective-permute-start.17) | collective-permute-done | bytes 30752 | tf_op jit(solution)/shard_map/ppermute | solution.py:338
  207.6 1.5 collective-permute-done.19
  209.2 0.1 convert_element_type.15
  209.3 0.6 fusion.34
  209.9 0.2 multiply_reduce_fusion
  210.1 0.9 collective-permute-start.20
  211.0 1.3 collective-permute-start.21
  212.3 1.5 collective-permute-start.22
  213.8 0.1 copy.34.pair_ref
  214.3 1.5 collective-permute-done.20
  215.8 1.2 collective-permute-done.21
  217.0 0.6 collective-permute-done.22
  217.6 0.4 shard_map.89
  218.0 0.1 reshape.263
  218.2 0.1 broadcast_select_fusion
  218.3 0.7 copy.35
  (59 shorter events, 0.9 us)
Async XLA Ops:
  5.2 36.4 %all-to-all-start.1 = ((bf16[32,1,15,8,128]{4,3,2,1,0:T(8,128)(2,1)}), bf16[32,1,15,8,128]{4,3,2,1,0:T(8,128)(2,1)S(1)}, u32[]{:S(2)}, u32[]{:S(2)}) async-start(bf16[32,1,15,8,128]{4,3,2,1,0:T(8,128)(2,1)} %shard_map.85), calls=%async_computation.1 | async-start | bytes 1966080 | tf_op jit(solution)/shard_map/all_to_all | solution.py:324
  41.6 1.0 copy-start
  42.6 52.0 %all-to-all-start = ((bf16[32,2,15,8,128]{4,3,2,1,0:T(8,128)(2,1)}), bf16[32,2,15,8,128]{4,3,2,1,0:T(8,128)(2,1)S(1)}, u32[]{:S(2)}, u32[]{:S(2)}) async-start(bf16[32,2,15,8,128]{4,3,2,1,0:T(8,128)(2,1)} %shard_map.82), calls=%async_computation | async-start | bytes 3932160 | tf_op jit(solution)/shard_map/all_to_all | solution.py:324
  60.0 43.6 %collective-permute-start = (bf16[5,2,912,256]{3,2,1,0:T(8,128)(2,1)}, bf16[5,2,912,256]{3,2,1,0:T(8,128)(2,1)}, u32[]{:S(2)}, u32[]{:S(2)}) collective-permute-start(bf16[5,2,912,256]{3,2,1,0:T(8,128)(2,1)} %shard_map.83.refs_2_), channel_id=1, source_target_pairs={{0,4},{4,0},{1,5},{5,1},{2,6},{6,2},{3,7},{7,3},{8,12},{12,8},{9,1... | collective-permute-start | bytes 14008328 | tf_op jit(solution)/shard_map/ppermute | solution.py:317
  64.0 39.3 %copy-start.7 = (s32[32]{0:T(128)S(1)}, s32[32]{0:T(128)}, u32[]{:S(2)}) copy-start(s32[32]{0:T(128)} %param.10) | copy-start | bytes 388
  94.5 9.2 %copy-start.2 = (bf16[32,2,15,8,128]{4,3,2,1,0:T(8,128)(2,1)}, bf16[32,2,15,8,128]{4,3,2,1,0:T(8,128)(2,1)S(1)}, u32[]{:S(2)}) copy-start(bf16[32,2,15,8,128]{4,3,2,1,0:T(8,128)(2,1)S(1)} %all-to-all-done.refs_1_) | copy-start | bytes 5898244
  94.5 37.2 %all-to-all-start.2 = ((bf16[32,1,15,8,128]{4,3,2,1,0:T(8,128)(2,1)}), bf16[32,1,15,8,128]{4,3,2,1,0:T(8,128)(2,1)S(1)}, u32[]{:S(2)}, u32[]{:S(2)}) async-start(bf16[32,1,15,8,128]{4,3,2,1,0:T(8,128)(2,1)} %shard_map.87), calls=%async_computation.2 | async-start | bytes 1966080 | tf_op jit(solution)/shard_map/all_to_all | solution.py:324
  115.4 60.8 %collective-permute-start.1 = (f32[4,2,8,2,1280]{4,3,2,1,0:T(2,128)}, f32[4,2,8,2,1280]{4,3,2,1,0:T(2,128)S(1)}, u32[]{:S(2)}, u32[]{:S(2)}) collective-permute-start(f32[4,2,8,2,1280]{4,3,2,1,0:T(2,128)} %get-tuple-element.16), channel_id=1, source_target_pairs={{0,1},{1,2},{2,3},{3,0},{4,5},{5,6},{6,7},{7,4},{8,9},{9,10},{10,1... | collective-permute-start | bytes 1966088 | tf_op jit(solution)/shard_map/ppermute | solution.py:279
  117.0 61.7 %collective-permute-start.2 = (f32[4,2,8,2,1280]{4,3,2,1,0:T(2,128)}, f32[4,2,8,2,1280]{4,3,2,1,0:T(2,128)S(1)}, u32[]{:S(2)}, u32[]{:S(2)}) collective-permute-start(f32[4,2,8,2,1280]{4,3,2,1,0:T(2,128)} %get-tuple-element.17), channel_id=1, source_target_pairs={{0,2},{1,3},{2,0},{3,1},{4,6},{5,7},{6,4},{7,5},{8,10},{9,11},{10,... | collective-permute-start | bytes 1966088 | tf_op jit(solution)/shard_map/ppermute | solution.py:279
  119.9 58.8 %collective-permute-start.3 = (f32[4,2,8,2,1280]{4,3,2,1,0:T(2,128)}, f32[4,2,8,2,1280]{4,3,2,1,0:T(2,128)S(1)}, u32[]{:S(2)}, u32[]{:S(2)}) collective-permute-start(f32[4,2,8,2,1280]{4,3,2,1,0:T(2,128)} %get-tuple-element.18), channel_id=1, source_target_pairs={{0,3},{1,0},{2,1},{3,2},{4,7},{5,4},{6,5},{7,6},{8,11},{9,8},{10,9... | collective-permute-start | bytes 1966088 | tf_op jit(solution)/shard_map/ppermute | solution.py:279
  130.3 24.1 %collective-permute-start.7 = (f32[4,1,8,2,1280]{4,3,2,1,0:T(2,128)}, f32[4,1,8,2,1280]{4,3,2,1,0:T(2,128)S(1)}, u32[]{:S(2)}, u32[]{:S(2)}) collective-permute-start(f32[4,1,8,2,1280]{4,3,2,1,0:T(2,128)} %get-tuple-element.20), channel_id=1, source_target_pairs={{0,1},{1,2},{2,3},{3,0},{4,5},{5,6},{6,7},{7,4},{8,9},{9,10},{10,1... | collective-permute-start | bytes 983048 | tf_op jit(solution)/shard_map/ppermute | solution.py:279
  131.0 41.4 %collective-permute-start.8 = (f32[4,1,8,2,1280]{4,3,2,1,0:T(2,128)}, f32[4,1,8,2,1280]{4,3,2,1,0:T(2,128)}, u32[]{:S(2)}, u32[]{:S(2)}) collective-permute-start(f32[4,1,8,2,1280]{4,3,2,1,0:T(2,128)} %get-tuple-element.21), channel_id=1, source_target_pairs={{0,2},{1,3},{2,0},{3,1},{4,6},{5,7},{6,4},{7,5},{8,10},{9,11},{10,... | collective-permute-start | bytes 983048 | tf_op jit(solution)/shard_map/ppermute | solution.py:279
  131.8 0.9 copy-start.1
  154.4 3.0 %copy-start.4 = (f32[4,1,8,2,1280]{4,3,2,1,0:T(2,128)}, f32[4,1,8,2,1280]{4,3,2,1,0:T(2,128)S(1)}, u32[]{:S(2)}) copy-start(f32[4,1,8,2,1280]{4,3,2,1,0:T(2,128)S(1)} %collective-permute-done.7) | copy-start | bytes 983044
  154.4 18.0 %collective-permute-start.9 = (f32[4,1,8,2,1280]{4,3,2,1,0:T(2,128)}, f32[4,1,8,2,1280]{4,3,2,1,0:T(2,128)}, u32[]{:S(2)}, u32[]{:S(2)}) collective-permute-start(f32[4,1,8,2,1280]{4,3,2,1,0:T(2,128)} %get-tuple-element.22), channel_id=1, source_target_pairs={{0,3},{1,0},{2,1},{3,2},{4,7},{5,4},{6,5},{7,6},{8,11},{9,8},{10,9... | collective-permute-start | bytes 983048 | tf_op jit(solution)/shard_map/ppermute | solution.py:279
  162.4 16.3 %copy-start.3 = (f32[4,2,8,2,1280]{4,3,2,1,0:T(2,128)S(1)}, f32[4,2,8,2,1280]{4,3,2,1,0:T(2,128)}, u32[]{:S(2)}) copy-start(f32[4,2,8,2,1280]{4,3,2,1,0:T(2,128)} %get-tuple-element.15) | copy-start | bytes 1966084
  162.4 46.8 %all-to-all-start.3 = ((f16[32,8,1280]{2,1,0:T(8,128)(2,1)}), f16[32,8,1280]{2,1,0:T(8,128)(2,1)S(1)}, u32[]{:S(2)}, u32[]{:S(2)}) async-start(f16[32,8,1280]{2,1,0:T(8,128)(2,1)} %select_convert_fusion), calls=%async_computation.3 | async-start | bytes 1310720 | tf_op jit(solution)/shard_map/all_to_all | solution.py:328
  173.9 8.9 %collective-permute-start.10 = (f32[1,8,2,1280]{3,2,1,0:T(2,128)S(1)}, f32[1,8,2,1280]{3,2,1,0:T(2,128)S(1)}, u32[]{:S(2)}, u32[]{:S(2)}) collective-permute-start(f32[1,8,2,1280]{3,2,1,0:T(2,128)S(1)} %get-tuple-element.32), channel_id=1, source_target_pairs={{0,8},{8,16},{16,24},{24,0},{1,9},{9,17},{17,25},{25,1},{2,10},{10... | collective-permute-start | bytes 245768 | tf_op jit(solution)/shard_map/ppermute | solution.py:279
  175.4 8.5 %collective-permute-start.11 = (f32[1,8,2,1280]{3,2,1,0:T(2,128)S(1)}, f32[1,8,2,1280]{3,2,1,0:T(2,128)S(1)}, u32[]{:S(2)}, u32[]{:S(2)}) collective-permute-start(f32[1,8,2,1280]{3,2,1,0:T(2,128)S(1)} %get-tuple-element.34), channel_id=1, source_target_pairs={{0,16},{8,24},{16,0},{24,8},{1,17},{9,25},{17,1},{25,9},{2,18},{10... | collective-permute-start | bytes 245768 | tf_op jit(solution)/shard_map/ppermute | solution.py:279
  176.2 10.3 %collective-permute-start.12 = (f32[1,8,2,1280]{3,2,1,0:T(2,128)S(1)}, f32[1,8,2,1280]{3,2,1,0:T(2,128)S(1)}, u32[]{:S(2)}, u32[]{:S(2)}) collective-permute-start(f32[1,8,2,1280]{3,2,1,0:T(2,128)S(1)} %get-tuple-element.33), channel_id=1, source_target_pairs={{0,24},{8,0},{16,8},{24,16},{1,25},{9,1},{17,9},{25,17},{2,26},{10... | collective-permute-start | bytes 245768 | tf_op jit(solution)/shard_map/ppermute | solution.py:279
  179.1 16.1 %copy-start.5 = (f32[48]{0:T(128)S(1)}, f32[48]{0:T(128)}, u32[]{:S(2)}) copy-start(f32[48]{0:T(128)} %param.11) | copy-start | bytes 580
  179.1 8.5 %collective-permute-start.4 = (f32[2,8,2,1280]{3,2,1,0:T(2,128)S(1)}, f32[2,8,2,1280]{3,2,1,0:T(2,128)S(1)}, u32[]{:S(2)}, u32[]{:S(2)}) collective-permute-start(f32[2,8,2,1280]{3,2,1,0:T(2,128)S(1)} %get-tuple-element.29), channel_id=1, source_target_pairs={{0,8},{8,16},{16,24},{24,0},{1,9},{9,17},{17,25},{25,1},{2,10},{10... | collective-permute-start | bytes 491528 | tf_op jit(solution)/shard_map/ppermute | solution.py:279
  179.2 10.1 %collective-permute-start.5 = (f32[2,8,2,1280]{3,2,1,0:T(2,128)S(1)}, f32[2,8,2,1280]{3,2,1,0:T(2,128)S(1)}, u32[]{:S(2)}, u32[]{:S(2)}) collective-permute-start(f32[2,8,2,1280]{3,2,1,0:T(2,128)S(1)} %get-tuple-element.31), channel_id=1, source_target_pairs={{0,16},{8,24},{16,0},{24,8},{1,17},{9,25},{17,1},{25,9},{2,18},{10... | collective-permute-start | bytes 491528 | tf_op jit(solution)/shard_map/ppermute | solution.py:279
  182.7 8.2 %collective-permute-start.6 = (f32[2,8,2,1280]{3,2,1,0:T(2,128)S(1)}, f32[2,8,2,1280]{3,2,1,0:T(2,128)S(1)}, u32[]{:S(2)}, u32[]{:S(2)}) collective-permute-start(f32[2,8,2,1280]{3,2,1,0:T(2,128)S(1)} %get-tuple-element.30), channel_id=1, source_target_pairs={{0,24},{8,0},{16,8},{24,16},{1,25},{9,1},{17,9},{25,17},{2,26},{10... | collective-permute-start | bytes 491528 | tf_op jit(solution)/shard_map/ppermute | solution.py:279
  191.2 9.4 %collective-permute-start.13 = (f32[3,2,1280]{2,1,0:T(2,128)S(1)}, f32[3,2,1280]{2,1,0:T(2,128)S(1)}, u32[]{:S(2)}, u32[]{:S(2)}) collective-permute-start(f32[3,2,1280]{2,1,0:T(2,128)S(1)} %get-tuple-element.35), channel_id=1, source_target_pairs={{0,32},{32,0},{64,96},{96,64},{128,160},{160,128},{192,224},{224,1... | collective-permute-start | bytes 92168 | tf_op jit(solution)/shard_map/ppermute | solution.py:338
  192.4 11.6 %collective-permute-start.14 = (f32[3,2,1280]{2,1,0:T(2,128)S(1)}, f32[3,2,1280]{2,1,0:T(2,128)S(1)}, u32[]{:S(2)}, u32[]{:S(2)}) collective-permute-start(f32[3,2,1280]{2,1,0:T(2,128)S(1)} %get-tuple-element.36), channel_id=1, source_target_pairs={{0,64},{32,96},{64,0},{96,32},{128,192},{160,224},{192,128},{224,1... | collective-permute-start | bytes 92168 | tf_op jit(solution)/shard_map/ppermute | solution.py:338
  195.4 9.8 %collective-permute-start.15 = (f32[3,2,1280]{2,1,0:T(2,128)S(1)}, f32[3,2,1280]{2,1,0:T(2,128)S(1)}, u32[]{:S(2)}, u32[]{:S(2)}) collective-permute-start(f32[3,2,1280]{2,1,0:T(2,128)S(1)} %get-tuple-element.37), channel_id=1, source_target_pairs={{0,96},{32,64},{64,32},{96,0},{128,224},{160,192},{192,160},{224,1... | collective-permute-start | bytes 92168 | tf_op jit(solution)/shard_map/ppermute | solution.py:338
  196.0 9.2 %collective-permute-start.16 = (f32[3,2,1280]{2,1,0:T(2,128)S(1)}, f32[3,2,1280]{2,1,0:T(2,128)S(1)}, u32[]{:S(2)}, u32[]{:S(2)}) collective-permute-start(f32[3,2,1280]{2,1,0:T(2,128)S(1)} %get-tuple-element.38), channel_id=1, source_target_pairs={{0,128},{32,160},{64,192},{96,224},{128,0},{160,32},{192,64},{224,... | collective-permute-start | bytes 92168 | tf_op jit(solution)/shard_map/ppermute | solution.py:338
  200.7 6.9 %collective-permute-start.17 = (f32[3,2,1280]{2,1,0:T(2,128)S(1)}, f32[3,2,1280]{2,1,0:T(2,128)S(1)}, u32[]{:S(2)}, u32[]{:S(2)}) collective-permute-start(f32[3,2,1280]{2,1,0:T(2,128)S(1)} %get-tuple-element.39), channel_id=1, source_target_pairs={{0,160},{32,128},{64,224},{96,192},{128,32},{160,0},{192,96},{224,... | collective-permute-start | bytes 92168 | tf_op jit(solution)/shard_map/ppermute | solution.py:338
  200.7 6.9 %collective-permute-start.18 = (f32[3,2,1280]{2,1,0:T(2,128)S(1)}, f32[3,2,1280]{2,1,0:T(2,128)S(1)}, u32[]{:S(2)}, u32[]{:S(2)}) collective-permute-start(f32[3,2,1280]{2,1,0:T(2,128)S(1)} %get-tuple-element.41), channel_id=1, source_target_pairs={{0,192},{32,224},{64,128},{96,160},{128,64},{160,96},{192,0},{224,... | collective-permute-start | bytes 92168 | tf_op jit(solution)/shard_map/ppermute | solution.py:338
  204.0 5.1 %collective-permute-start.19 = (f32[3,2,1280]{2,1,0:T(2,128)S(1)}, f32[3,2,1280]{2,1,0:T(2,128)S(1)}, u32[]{:S(2)}, u32[]{:S(2)}) collective-permute-start(f32[3,2,1280]{2,1,0:T(2,128)S(1)} %get-tuple-element.40), channel_id=1, source_target_pairs={{0,224},{32,192},{64,160},{96,128},{128,96},{160,64},{192,32},{224... | collective-permute-start | bytes 92168 | tf_op jit(solution)/shard_map/ppermute | solution.py:338
  209.2 4.7 %copy-start.6 = (f32[48]{0:T(128)S(1)}, f32[48]{0:T(128)}, u32[]{:S(2)}) copy-start(f32[48]{0:T(128)} %param.12) | copy-start | bytes 580
  210.1 5.7 %collective-permute-start.20 = (f32[16,1280]{1,0:T(8,128)S(1)}, f32[16,1280]{1,0:T(8,128)S(1)}, u32[]{:S(2)}, u32[]{:S(2)}) collective-permute-start(f32[16,1280]{1,0:T(8,128)S(1)} %get-tuple-element.43), channel_id=1, source_target_pairs={{0,1},{1,2},{2,3},{3,0},{4,5},{5,6},{6,7},{7,4},{8,9},{9,10},{10,1... | collective-permute-start | bytes 245768 | tf_op jit(solution)/shard_map/ppermute | solution.py:279
  211.0 5.9 %collective-permute-start.21 = (f32[16,1280]{1,0:T(8,128)S(1)}, f32[16,1280]{1,0:T(8,128)S(1)}, u32[]{:S(2)}, u32[]{:S(2)}) collective-permute-start(f32[16,1280]{1,0:T(8,128)S(1)} %get-tuple-element.43), channel_id=1, source_target_pairs={{0,2},{1,3},{2,0},{3,1},{4,6},{5,7},{6,4},{7,5},{8,10},{9,11},{10,... | collective-permute-start | bytes 245768 | tf_op jit(solution)/shard_map/ppermute | solution.py:279
  212.3 5.3 %collective-permute-start.22 = (f32[16,1280]{1,0:T(8,128)S(1)}, f32[16,1280]{1,0:T(8,128)S(1)}, u32[]{:S(2)}, u32[]{:S(2)}) collective-permute-start(f32[16,1280]{1,0:T(8,128)S(1)} %get-tuple-element.43), channel_id=1, source_target_pairs={{0,3},{1,0},{2,1},{3,2},{4,7},{5,4},{6,5},{7,6},{8,11},{9,8},{10,9... | collective-permute-start | bytes 245768 | tf_op jit(solution)/shard_map/ppermute | solution.py:279

commit v6 on v5

--- a/solution.py
+++ b/solution.py
@@ -9,7 +9,7 @@
 ROWS = 8
 LEFT = 16
 COPIES = 2
-LADDER_MIB = 60
+MIB = 36
 LANES = 128
 BF = jnp.bfloat16
 F32 = jnp.float32
@@ -98,7 +98,7 @@
             ],
         ),
         out_shape=jax.ShapeDtypeStruct((xs * zs, size, tiles, ROWS, LANES), BF),
-        compiler_params=params(60),
+        compiler_params=params(60 if start == 0 else MIB),
         cost_estimate=pl.CostEstimate(flops=0, bytes_accessed=8_000_000, transcendentals=0),
     )(where, view)
 
@@ -129,7 +129,7 @@
         ],
         out_specs=pl.BlockSpec((1, 2, padded, block), lambda i: (i, 0, 0, 0)),
         out_shape=jax.ShapeDtypeStruct((count // block, 2, padded, block), BF),
-        compiler_params=params(60),
+        compiler_params=params(MIB),
         cost_estimate=pl.CostEstimate(
             flops=2 * width * full * count, bytes_accessed=10_000_000, transcendentals=0
         ),
@@ -247,7 +247,7 @@
             scratch_shapes=scratch,
         ),
         out_shape=[jax.ShapeDtypeStruct(shape, F32) for shape in shapes],
-        compiler_params=params(LADDER_MIB),
+        compiler_params=params(MIB),
         cost_estimate=pl.CostEstimate(
             flops=4 * size * chips * ROWS * tiles * LANES * count,
             bytes_accessed=size * 3_000_000 + 9_000_000,
@@ -333,9 +333,11 @@
         partial = [further(block, "x", r) for r, block in enumerate(partial)]
         done.append(sum(partial[1:], partial[0]))
     mine = jnp.concatenate(done, axis=0)
-    apart = [mine[:, s] for s in range(zs)]
-    apart = [apart[0]] + [
-        lax.ppermute(apart[s], "z", [(i, i ^ s) for i in range(zs)]) for s in range(1, zs)
+    mine = mine.reshape(-1, zs // 2, 2, COPIES, count)
+    odd = lax.ppermute(mine[:, :, 1], "z", [(i, i ^ 1) for i in range(zs)])
+    mine = mine[:, :, 0] + odd
+    apart = [mine[:, 0]] + [
+        lax.ppermute(mine[:, s], "z", [(i, i ^ (2 * s)) for i in range(zs)]) for s in range(1, zs // 2)
     ]
     mine = sum(apart[1:], apart[0])
     mine = mine.reshape(-1, count)
@@ -359,7 +361,7 @@
         in_specs=[pl.BlockSpec(memory_space=pltpu.SMEM)] + [pl.BlockSpec(memory_space=pltpu.VMEM)] * 5,
         out_shape=jax.ShapeDtypeStruct((slots, full), F32),
         scratch_shapes=[pltpu.VMEM((ys, slots // ys, count), F32)],
-        compiler_params=params(24),
+        compiler_params=params(MIB),
     )(place[None], everyone, column, pair_sum[:, None], ea, eb)
     update = update[:, :wide].reshape(slots, local_rows, window)
     return jnp.where(filled[:, None, None], update, jnp.zeros_like(update))

time: 221 us -> 238 us (1.077)
  waiting for transfers between devices: 75.4 us -> 102 us
  Pallas kernels: 53.2 us -> 45.6 us
  starting transfers between devices: 73.7 us -> 71.2 us
    ppermute x15, waiting for transfers between devices: 21.3 us -> 37.8 us  [further(): lax.ppermute(block, axis, [(i, (i + hops) % size) for i in range(size)])]
    ppermute x7 -> x4, waiting for transfers between devices: 3.9 us -> 12.6 us  [the longest x3 12.6 us: body(): lax.ppermute(mine[:, s], 'z', [(i, i ^ 2 * s) for i in range(zs)])]
    ppermute x7 -> x4, starting transfers between devices: 13.7 us -> 8.17 us  [the longest x3 6.58 us: body(): lax.ppermute(mine[:, s], 'z', [(i, i ^ 2 * s) for i in range(zs)])]
    ppermute x15, starting transfers between devices: 22.4 us -> 25.8 us  [further(): lax.ppermute(block, axis, [(i, (i + hops) % size) for i in range(size)])]
    pallas_call x3, Pallas kernels: 30 us -> 27.3 us  [ladder(): pl.pallas_call(lambda *refs: kernel(xs, *refs), grid_spec=pltpu.PrefetchS...]
    pallas_call x3, Pallas kernels: 12.8 us -> 10.3 us  [flatten(): pl.pallas_call(lambda *refs: flatten_kernel(xs, zs, width, *refs), grid_s...]
    unnamed x16 -> x21, local copies, waits for them, and re-layouts: 1.93 us -> 4.34 us
  transfers between devices with their start and end apart: 27 -> 24, of which waited for: 12 -> 12; matrix products, arithmetic and copies ran while one was open for 5% -> 4% of each run, Pallas kernels for 22% -> 18%
where the time goes in v6:
time: 238 us; the launch traced here: 237 us
  waiting for transfers between devices  102 us (43%)
  starting transfers between devices  71.2 us (30%)
  Pallas kernels  45.6 us (19%)
  other arithmetic  11.8 us (5%)
  local copies, waits for them, and re-layouts  6.56 us (3%)
    all_to_all x3, waiting for transfers between devices, body(): panels = lax.all_to_all(flat, ('x', 'z'), 0, 0, tiled=True)  51.6 us
    ppermute x15, waiting for transfers between devices, further(): lax.ppermute(block, axis, [(i, (i + hops) % size) for i in range(size)])  37.8 us
    all_to_all x3, starting transfers between devices, body(): panels = lax.all_to_all(flat, ('x', 'z'), 0, 0, tiled=True)  27.7 us
    pallas_call x3, Pallas kernels, ladder(): pl.pallas_call(lambda *refs: kernel(xs, *refs), grid_spec=pltpu.PrefetchS...  27.3 us
    ppermute x15, starting transfers between devices, further(): lax.ppermute(block, axis, [(i, (i + hops) % size) for i in range(size)])  25.8 us
    ppermute x3, waiting for transfers between devices, body(): lax.ppermute(mine[:, s], 'z', [(i, i ^ 2 * s) for i in range(zs)])  12.6 us
    pallas_call x3, Pallas kernels, flatten(): pl.pallas_call(lambda *refs: flatten_kernel(xs, zs, width, *refs), grid_s...  10.3 us
    all_to_all x1, starting transfers between devices, body(): coded = lax.all_to_all(coded, ('x', 'z'), 0, 0, tiled=True)  9.5 us
  transfers between devices with their start and end apart: 24, of which 12 were waited for; matrix products, arithmetic and copies ran while one was open for 4% of the time, Pallas kernels for 18%

profile of v6, /device:TPU:2, one launch (start us, length us, event | category | flops | bytes accessed | tf_op | source)
XLA Modules:
  0.0 237.4 jit_solution(7307897614390725366)
XLA Ops:
  0.0 0.7 fusion.26
  0.7 2.1 copy-done
  2.9 2.6 %shard_map.85 = bf16[32,1,15,8,128]{4,3,2,1,0:T(8,128)(2,1)} custom-call(s32[4]{0:T(128)S(1)} %get-tuple-element.28.refs_0_, bf16[4,4,2,120,480]{4,3,2,1,0:T(8,128)(2,1)S(1)} %bitcast.69), custom_call_target="tpu_custom_call" | custom-call | bytes 8000000 | tf_op jit(solution)/shard_map/pallas_call | solution.py:86
  5.5 11.6 %all-to-all-start.1 = ((bf16[32,1,15,8,128]{4,3,2,1,0:T(8,128)(2,1)}), bf16[32,1,15,8,128]{4,3,2,1,0:T(8,128)(2,1)S(1)}, u32[]{:S(2)}, u32[]{:S(2)}) async-start(bf16[32,1,15,8,128]{4,3,2,1,0:T(8,128)(2,1)} %shard_map.85), calls=%async_computation.1 | async-start | bytes 1966080 | tf_op jit(solution)/shard_map/all_to_all | solution.py:324
  17.1 5.0 %shard_map.82 = bf16[32,2,15,8,128]{4,3,2,1,0:T(8,128)(2,1)} custom-call(s32[4]{0:T(128)} %copy-done.2, bf16[4,4,2,120,480]{4,3,2,1,0:T(8,128)(2,1)} %bitcast.68), custom_call_target="tpu_custom_call" | custom-call | bytes 8000000 | tf_op jit(solution)/shard_map/pallas_call | solution.py:86
  22.1 19.7 %all-to-all-done.1.refs_1_ = bf16[32,1,15,8,128]{4,3,2,1,0:T(8,128)(2,1)S(1)} async-done(((bf16[32,1,15,8,128]{4,3,2,1,0:T(8,128)(2,1)}), bf16[32,1,15,8,128]{4,3,2,1,0:T(8,128)(2,1)S(1)}, u32[]{:S(2)}, u32[]{:S(2)}) %all-to-all-start.1) | async-done | bytes 983072 | tf_op jit(solution)/shard_map/all_to_all | solution.py:324
  41.9 7.6 %all-to-all-start = ((bf16[32,2,15,8,128]{4,3,2,1,0:T(8,128)(2,1)}), bf16[32,2,15,8,128]{4,3,2,1,0:T(8,128)(2,1)}, u32[]{:S(2)}, u32[]{:S(2)}) async-start(bf16[32,2,15,8,128]{4,3,2,1,0:T(8,128)(2,1)} %shard_map.82), calls=%async_computation | async-start | bytes 3932160 | tf_op jit(solution)/shard_map/all_to_all | solution.py:324
  49.5 2.2 copy-done.4
  51.7 7.7 %shard_map.83.refs_2_ = bf16[5,2,912,256]{3,2,1,0:T(8,128)(2,1)} custom-call(s32[1,1280]{1,0:T(1,128)S(1)} %copy-done.5, s32[1,1280]{1,0:T(1,128)S(1)} %copy-done.6, bf16[900,2304]{1,0:T(8,128)(2,1)S(1)} %bitcast.72), custom_call_target="tpu_custom_call" | custom-call | flops 5308416000 | bytes 10000000 | tf_op jit(solution)/shard_map/pallas_call | solution.py:122
  59.3 2.6 %shard_map.87 = bf16[32,1,15,8,128]{4,3,2,1,0:T(8,128)(2,1)} custom-call(s32[4]{0:T(128)S(1)} %get-tuple-element.27.refs_0_, bf16[4,4,2,120,480]{4,3,2,1,0:T(8,128)(2,1)S(1)} %bitcast.70), custom_call_target="tpu_custom_call" | custom-call | bytes 8000000 | tf_op jit(solution)/shard_map/pallas_call | solution.py:86
  62.1 31.8 %all-to-all-done.refs_1_ = bf16[32,2,15,8,128]{4,3,2,1,0:T(8,128)(2,1)} async-done(((bf16[32,2,15,8,128]{4,3,2,1,0:T(8,128)(2,1)}), bf16[32,2,15,8,128]{4,3,2,1,0:T(8,128)(2,1)}, u32[]{:S(2)}, u32[]{:S(2)}) %all-to-all-start) | async-done | bytes 1966112 | tf_op jit(solution)/shard_map/all_to_all | solution.py:324
  93.9 8.5 %all-to-all-start.2 = ((bf16[32,1,15,8,128]{4,3,2,1,0:T(8,128)(2,1)}), bf16[32,1,15,8,128]{4,3,2,1,0:T(8,128)(2,1)S(1)}, u32[]{:S(2)}, u32[]{:S(2)}) async-start(bf16[32,1,15,8,128]{4,3,2,1,0:T(8,128)(2,1)} %shard_map.87), calls=%async_computation.2 | async-start | bytes 1966080 | tf_op jit(solution)/shard_map/all_to_all | solution.py:324
  102.5 0.1 max.7
  102.7 0.2 convert_reduce_fusion
  102.8 0.2 select_reduce_fusion.1
  103.0 0.2 select_reduce_fusion
  103.3 8.3 %shard_map.86 = (f32[4,1,8,2,1280]{4,3,2,1,0:T(2,128)S(1)}, f32[4,1,8,2,1280]{4,3,2,1,0:T(2,128)S(1)}, f32[4,1,8,2,1280]{4,3,2,1,0:T(2,128)}, f32[4,1,8,2,1280]{4,3,2,1,0:T(2,128)S(1)}) custom-call(s32[4]{0:T(128)S(1)} %copy-done.3, bf16[32,1,15,8,128]{4,3,2,1,0:T(8,128)(2,1)S(1)} %all-to-all-done.1.refs_1_, bf16[5,2,912,256]{3,2,1,0:T(8,128)(2,1)} %shard_map.83.refs_2_, ...), custom_call_target="tpu_custom_call" | custom-call | flops 2516582400 | bytes 12000000 | tf_op jit(solution)/shard_map/pallas_call | solution.py:236
  111.5 1.6 collective-permute-start.7
  113.1 11.3 %shard_map.84 = (f32[4,2,8,2,1280]{4,3,2,1,0:T(2,128)S(1)}, f32[4,2,8,2,1280]{4,3,2,1,0:T(2,128)}, f32[4,2,8,2,1280]{4,3,2,1,0:T(2,128)}, f32[4,2,8,2,1280]{4,3,2,1,0:T(2,128)S(1)}) custom-call(s32[4]{0:T(128)S(1)} %copy-done.3, bf16[32,2,15,8,128]{4,3,2,1,0:T(8,128)(2,1)} %all-to-all-done.refs_1_, bf16[5,2,912,256]{3,2,1,0:T(8,128)(2,1)} %shard_map.83.refs_2_, ...), custom_call_target="tpu_custom_call" | custom-call | flops 5033164800 | bytes 15000000 | tf_op jit(solution)/shard_map/pallas_call | solution.py:236
  124.4 1.6 collective-permute-start.1
  126.0 1.6 collective-permute-start.2
  127.5 2.4 %collective-permute-start.3 = (f32[4,2,8,2,1280]{4,3,2,1,0:T(2,128)S(1)}, f32[4,2,8,2,1280]{4,3,2,1,0:T(2,128)}, u32[]{:S(2)}, u32[]{:S(2)}) collective-permute-start(f32[4,2,8,2,1280]{4,3,2,1,0:T(2,128)S(1)} %get-tuple-element.18), channel_id=1, source_target_pairs={{0,3},{1,0},{2,1},{3,2},{4,7},{5,4},{6,5},{7,6},{8,11},{9,8},{10,9... | collective-permute-start | bytes 1966088 | tf_op jit(solution)/shard_map/ppermute | solution.py:279
  129.9 0.6 collective-permute-start.8
  130.5 1.7 collective-permute-start.9
  132.2 7.7 %shard_map.88 = (f32[32,8,1280]{2,1,0:T(8,128)S(1)}, f32[8,128]{1,0:T(8,128)S(1)}) custom-call(s32[4]{0:T(128)S(1)} %get-tuple-element.27.refs_0_, bf16[32,1,15,8,128]{4,3,2,1,0:T(8,128)(2,1)S(1)} %all-to-all-done.2.refs_1_, bf16[5,2,912,256]{3,2,1,0:T(8,128)(2,1)} %shard_map.83.refs_2_, bf16[5,2,912,256]{3,2,1,0:T(8,128)(2,1)} %collective-permute-done.refs_3_), custom_call_target="tpu_custom_call" | custom-call | flops 2516582400 | bytes 12000000 | tf_op jit(solution)/shard_map/pallas_call | solution.py:236
  139.9 0.7 fusion.28
  140.6 21.5 %collective-permute-done.8 = f32[4,1,8,2,1280]{4,3,2,1,0:T(2,128)} collective-permute-done((f32[4,1,8,2,1280]{4,3,2,1,0:T(2,128)}, f32[4,1,8,2,1280]{4,3,2,1,0:T(2,128)}, u32[]{:S(2)}, u32[]{:S(2)}) %collective-permute-start.8) | collective-permute-done | bytes 327712 | tf_op jit(solution)/shard_map/ppermute | solution.py:279
  162.1 7.7 %collective-permute-done.9 = f32[4,1,8,2,1280]{4,3,2,1,0:T(2,128)} collective-permute-done((f32[4,1,8,2,1280]{4,3,2,1,0:T(2,128)S(1)}, f32[4,1,8,2,1280]{4,3,2,1,0:T(2,128)}, u32[]{:S(2)}, u32[]{:S(2)}) %collective-permute-start.9) | collective-permute-done | bytes 327712 | tf_op jit(solution)/shard_map/ppermute | solution.py:279
  169.8 1.3 fusion.10
  171.1 1.5 collective-permute-start.10
  172.6 1.1 collective-permute-start.11
  173.8 2.2 collective-permute-start.12
  175.9 1.9 fusion.2
  177.8 0.1 collective-permute-start.4
  177.9 3.5 %collective-permute-start.5 = (f32[2,8,2,1280]{3,2,1,0:T(2,128)S(1)}, f32[2,8,2,1280]{3,2,1,0:T(2,128)S(1)}, u32[]{:S(2)}, u32[]{:S(2)}) collective-permute-start(f32[2,8,2,1280]{3,2,1,0:T(2,128)S(1)} %get-tuple-element.31), channel_id=1, source_target_pairs={{0,16},{8,24},{16,0},{24,8},{1,17},{9,25},{17,1},{25,9},{2,18},{10... | collective-permute-start | bytes 491528 | tf_op jit(solution)/shard_map/ppermute | solution.py:279
  181.4 1.0 fusion.14
  182.5 1.3 collective-permute-done.4
  183.8 1.6 collective-permute-done.5
  185.4 1.7 collective-permute-done.6
  187.1 1.3 fusion.6
  188.4 0.1 pad_maximum_fusion.1
  188.6 1.6 collective-permute-start.13
  190.2 3.6 %select_convert_fusion = f16[32,8,1280]{2,1,0:T(8,128)(2,1)} fusion(f32[32,8,1280]{2,1,0:T(8,128)S(1)} %get-tuple-element.24, f32[]{:T(128)} %bitcast.24, f32[]{:T(128)} %bitcast.23, f32[]{:T(128)} %bitcast.22, f32[]{:T(128)} %bitcast.21, pred[1280]{0:T(1024)(128)(4,1)S(1)} %get-tuple-element.48, pred[1280]{0:T(1024)(128)(4,1)S(1)} %get-tuple-element.49, ...), kind=kLoop, calls=%fused_computation.1 | loop fusion | flops 1638400 | bytes 1969936 | tf_op jit(solution)/shard_map/convert_element_type | solution.py:265
  193.8 9.5 %all-to-all-start.3 = ((f16[32,8,1280]{2,1,0:T(8,128)(2,1)}), f16[32,8,1280]{2,1,0:T(8,128)(2,1)S(1)}, u32[]{:S(2)}, u32[]{:S(2)}) async-start(f16[32,8,1280]{2,1,0:T(8,128)(2,1)} %select_convert_fusion), calls=%async_computation.3 | async-start | bytes 1310720 | tf_op jit(solution)/shard_map/all_to_all | solution.py:328
  203.3 0.1 fusion.7
  203.4 2.4 %collective-permute-start.14 = (f32[3,2,1280]{2,1,0:T(2,128)S(1)}, f32[3,2,1280]{2,1,0:T(2,128)S(1)}, u32[]{:S(2)}, u32[]{:S(2)}) collective-permute-start(f32[3,2,1280]{2,1,0:T(2,128)S(1)} %get-tuple-element.37), channel_id=1, source_target_pairs={{0,64},{32,96},{64,0},{96,32},{128,192},{160,224},{192,128},{224,1... | collective-permute-start | bytes 92168 | tf_op jit(solution)/shard_map/ppermute | solution.py:340
  205.8 3.6 %collective-permute-start.15 = (f32[3,2,1280]{2,1,0:T(2,128)S(1)}, f32[3,2,1280]{2,1,0:T(2,128)S(1)}, u32[]{:S(2)}, u32[]{:S(2)}) collective-permute-start(f32[3,2,1280]{2,1,0:T(2,128)S(1)} %get-tuple-element.39), channel_id=1, source_target_pairs={{0,128},{32,160},{64,192},{96,224},{128,0},{160,32},{192,64},{224,... | collective-permute-start | bytes 92168 | tf_op jit(solution)/shard_map/ppermute | solution.py:340
  209.4 0.6 collective-permute-start.16
  210.0 8.4 %collective-permute-done.14 = f32[3,2,1280]{2,1,0:T(2,128)S(1)} collective-permute-done((f32[3,2,1280]{2,1,0:T(2,128)S(1)}, f32[3,2,1280]{2,1,0:T(2,128)S(1)}, u32[]{:S(2)}, u32[]{:S(2)}) %collective-permute-start.14) | collective-permute-done | bytes 30752 | tf_op jit(solution)/shard_map/ppermute | solution.py:340
  218.4 4.1 %collective-permute-done.15 = f32[3,2,1280]{2,1,0:T(2,128)S(1)} collective-permute-done((f32[3,2,1280]{2,1,0:T(2,128)S(1)}, f32[3,2,1280]{2,1,0:T(2,128)S(1)}, u32[]{:S(2)}, u32[]{:S(2)}) %collective-permute-start.15) | collective-permute-done | bytes 30752 | tf_op jit(solution)/shard_map/ppermute | solution.py:340
  222.6 0.1 convert_element_type.15
  222.7 0.6 fusion.18
  223.3 0.2 multiply_reduce_fusion
  223.5 3.9 %collective-permute-start.17 = (f32[16,1280]{1,0:T(8,128)S(1)}, f32[16,1280]{1,0:T(8,128)S(1)}, u32[]{:S(2)}, u32[]{:S(2)}) collective-permute-start(f32[16,1280]{1,0:T(8,128)S(1)} %get-tuple-element.41), channel_id=1, source_target_pairs={{0,1},{1,2},{2,3},{3,0},{4,5},{5,6},{6,7},{7,4},{8,9},{9,10},{10,1... | collective-permute-start | bytes 245768 | tf_op jit(solution)/shard_map/ppermute | solution.py:279
  227.4 4.1 %collective-permute-start.18 = (f32[16,1280]{1,0:T(8,128)S(1)}, f32[16,1280]{1,0:T(8,128)S(1)}, u32[]{:S(2)}, u32[]{:S(2)}) collective-permute-start(f32[16,1280]{1,0:T(8,128)S(1)} %get-tuple-element.41), channel_id=1, source_target_pairs={{0,2},{1,3},{2,0},{3,1},{4,6},{5,7},{6,4},{7,5},{8,10},{9,11},{10,... | collective-permute-start | bytes 245768 | tf_op jit(solution)/shard_map/ppermute | solution.py:279
  231.6 0.1 copy.19.pair_ref
  231.8 0.1 reshape.266
  232.0 0.9 collective-permute-done.17
  233.0 1.9 collective-permute-done.18
  234.8 1.1 collective-permute-done.19
  236.0 0.4 shard_map.89
  236.5 0.1 reshape.267
  236.6 0.1 broadcast_select_fusion
  236.7 0.7 copy.20
  (61 shorter events, 0.7 us)
Async XLA Ops:
  0.7 4.7 %copy-start.2 = (s32[4]{0:T(128)}, s32[4]{0:T(128)S(1)}, u32[]{:S(2)}) copy-start(s32[4]{0:T(128)S(1)} %get-tuple-element.28.refs_0_) | copy-start | bytes 52
  0.7 2.1 copy-start
  5.5 36.4 %all-to-all-start.1 = ((bf16[32,1,15,8,128]{4,3,2,1,0:T(8,128)(2,1)}), bf16[32,1,15,8,128]{4,3,2,1,0:T(8,128)(2,1)S(1)}, u32[]{:S(2)}, u32[]{:S(2)}) async-start(bf16[32,1,15,8,128]{4,3,2,1,0:T(8,128)(2,1)} %shard_map.85), calls=%async_computation.1 | async-start | bytes 1966080 | tf_op jit(solution)/shard_map/all_to_all | solution.py:324
  22.1 27.3 %copy-start.5 = (s32[1,1280]{1,0:T(1,128)S(1)}, s32[1,1280]{1,0:T(1,128)}, u32[]{:S(2)}) copy-start(s32[1,1280]{1,0:T(1,128)} %constant.71.clone.one_ref) | copy-start | bytes 15364
  22.1 27.4 %copy-start.6 = (s32[1,1280]{1,0:T(1,128)S(1)}, s32[1,1280]{1,0:T(1,128)}, u32[]{:S(2)}) copy-start(s32[1,1280]{1,0:T(1,128)} %constant.72.clone.two_ref) | copy-start | bytes 15364
  41.9 52.1 %all-to-all-start = ((bf16[32,2,15,8,128]{4,3,2,1,0:T(8,128)(2,1)}), bf16[32,2,15,8,128]{4,3,2,1,0:T(8,128)(2,1)}, u32[]{:S(2)}, u32[]{:S(2)}) async-start(bf16[32,2,15,8,128]{4,3,2,1,0:T(8,128)(2,1)} %shard_map.82), calls=%async_computation | async-start | bytes 3932160 | tf_op jit(solution)/shard_map/all_to_all | solution.py:324
  49.5 2.2 copy-start.4
  51.7 7.7 %copy-start.1 = (bf16[32,120,480]{2,1,0:T(8,128)(2,1)S(1)}, bf16[32,120,480]{2,1,0:T(8,128)(2,1)}, u32[]{:S(2)}) copy-start(bf16[32,120,480]{2,1,0:T(8,128)(2,1)} %param.8) | copy-start | bytes 11059204
  59.3 43.9 %collective-permute-start = (bf16[5,2,912,256]{3,2,1,0:T(8,128)(2,1)}, bf16[5,2,912,256]{3,2,1,0:T(8,128)(2,1)}, u32[]{:S(2)}, u32[]{:S(2)}) collective-permute-start(bf16[5,2,912,256]{3,2,1,0:T(8,128)(2,1)} %shard_map.83.refs_2_), channel_id=1, source_target_pairs={{0,4},{4,0},{1,5},{5,1},{2,6},{6,2},{3,7},{7,3},{8,12},{12,8},{9,1... | collective-permute-start | bytes 14008328 | tf_op jit(solution)/shard_map/ppermute | solution.py:317
  62.0 40.7 %copy-start.9 = (s32[32]{0:T(128)S(1)}, s32[32]{0:T(128)}, u32[]{:S(2)}) copy-start(s32[32]{0:T(128)} %param.10) | copy-start | bytes 388
  62.0 41.1 %copy-start.7 = (f32[48]{0:T(128)S(1)}, f32[48]{0:T(128)}, u32[]{:S(2)}) copy-start(f32[48]{0:T(128)} %param.11) | copy-start | bytes 580
  62.0 41.3 %copy-start.3 = (s32[4]{0:T(128)S(1)}, s32[4]{0:T(128)}, u32[]{:S(2)}) copy-start(s32[4]{0:T(128)} %copy-done.2) | copy-start | bytes 52
  93.9 38.3 %all-to-all-start.2 = ((bf16[32,1,15,8,128]{4,3,2,1,0:T(8,128)(2,1)}), bf16[32,1,15,8,128]{4,3,2,1,0:T(8,128)(2,1)S(1)}, u32[]{:S(2)}, u32[]{:S(2)}) async-start(bf16[32,1,15,8,128]{4,3,2,1,0:T(8,128)(2,1)} %shard_map.87), calls=%async_computation.2 | async-start | bytes 1966080 | tf_op jit(solution)/shard_map/all_to_all | solution.py:324
  111.5 19.0 %collective-permute-start.7 = (f32[4,1,8,2,1280]{4,3,2,1,0:T(2,128)S(1)}, f32[4,1,8,2,1280]{4,3,2,1,0:T(2,128)S(1)}, u32[]{:S(2)}, u32[]{:S(2)}) collective-permute-start(f32[4,1,8,2,1280]{4,3,2,1,0:T(2,128)S(1)} %get-tuple-element.20), channel_id=1, source_target_pairs={{0,1},{1,2},{2,3},{3,0},{4,5},{5,6},{6,7},{7,4},{8,9},{9,10},{10,1... | collective-permute-start | bytes 983048 | tf_op jit(solution)/shard_map/ppermute | solution.py:279
  124.4 49.4 %collective-permute-start.1 = (f32[4,2,8,2,1280]{4,3,2,1,0:T(2,128)}, f32[4,2,8,2,1280]{4,3,2,1,0:T(2,128)}, u32[]{:S(2)}, u32[]{:S(2)}) collective-permute-start(f32[4,2,8,2,1280]{4,3,2,1,0:T(2,128)} %get-tuple-element.16), channel_id=1, source_target_pairs={{0,1},{1,2},{2,3},{3,0},{4,5},{5,6},{6,7},{7,4},{8,9},{9,10},{10,1... | collective-permute-start | bytes 1966088 | tf_op jit(solution)/shard_map/ppermute | solution.py:279
  126.0 50.0 %collective-permute-start.2 = (f32[4,2,8,2,1280]{4,3,2,1,0:T(2,128)}, f32[4,2,8,2,1280]{4,3,2,1,0:T(2,128)}, u32[]{:S(2)}, u32[]{:S(2)}) collective-permute-start(f32[4,2,8,2,1280]{4,3,2,1,0:T(2,128)} %get-tuple-element.17), channel_id=1, source_target_pairs={{0,2},{1,3},{2,0},{3,1},{4,6},{5,7},{6,4},{7,5},{8,10},{9,11},{10,... | collective-permute-start | bytes 1966088 | tf_op jit(solution)/shard_map/ppermute | solution.py:279
  127.5 48.4 %collective-permute-start.3 = (f32[4,2,8,2,1280]{4,3,2,1,0:T(2,128)S(1)}, f32[4,2,8,2,1280]{4,3,2,1,0:T(2,128)}, u32[]{:S(2)}, u32[]{:S(2)}) collective-permute-start(f32[4,2,8,2,1280]{4,3,2,1,0:T(2,128)S(1)} %get-tuple-element.18), channel_id=1, source_target_pairs={{0,3},{1,0},{2,1},{3,2},{4,7},{5,4},{6,5},{7,6},{8,11},{9,8},{10,9... | collective-permute-start | bytes 1966088 | tf_op jit(solution)/shard_map/ppermute | solution.py:279
  129.9 32.2 %collective-permute-start.8 = (f32[4,1,8,2,1280]{4,3,2,1,0:T(2,128)}, f32[4,1,8,2,1280]{4,3,2,1,0:T(2,128)}, u32[]{:S(2)}, u32[]{:S(2)}) collective-permute-start(f32[4,1,8,2,1280]{4,3,2,1,0:T(2,128)} %get-tuple-element.21), channel_id=1, source_target_pairs={{0,2},{1,3},{2,0},{3,1},{4,6},{5,7},{6,4},{7,5},{8,10},{9,11},{10,... | collective-permute-start | bytes 983048 | tf_op jit(solution)/shard_map/ppermute | solution.py:279
  130.5 39.3 %collective-permute-start.9 = (f32[4,1,8,2,1280]{4,3,2,1,0:T(2,128)S(1)}, f32[4,1,8,2,1280]{4,3,2,1,0:T(2,128)}, u32[]{:S(2)}, u32[]{:S(2)}) collective-permute-start(f32[4,1,8,2,1280]{4,3,2,1,0:T(2,128)S(1)} %get-tuple-element.22), channel_id=1, source_target_pairs={{0,3},{1,0},{2,1},{3,2},{4,7},{5,4},{6,5},{7,6},{8,11},{9,8},{10,9... | collective-permute-start | bytes 983048 | tf_op jit(solution)/shard_map/ppermute | solution.py:279
  171.1 10.3 %collective-permute-start.10 = (f32[1,8,2,1280]{3,2,1,0:T(2,128)S(1)}, f32[1,8,2,1280]{3,2,1,0:T(2,128)S(1)}, u32[]{:S(2)}, u32[]{:S(2)}) collective-permute-start(f32[1,8,2,1280]{3,2,1,0:T(2,128)S(1)} %get-tuple-element.32), channel_id=1, source_target_pairs={{0,8},{8,16},{16,24},{24,0},{1,9},{9,17},{17,25},{25,1},{2,10},{10... | collective-permute-start | bytes 245768 | tf_op jit(solution)/shard_map/ppermute | solution.py:279
  172.6 8.8 %collective-permute-start.11 = (f32[1,8,2,1280]{3,2,1,0:T(2,128)S(1)}, f32[1,8,2,1280]{3,2,1,0:T(2,128)S(1)}, u32[]{:S(2)}, u32[]{:S(2)}) collective-permute-start(f32[1,8,2,1280]{3,2,1,0:T(2,128)S(1)} %get-tuple-element.34), channel_id=1, source_target_pairs={{0,16},{8,24},{16,0},{24,8},{1,17},{9,25},{17,1},{25,9},{2,18},{10... | collective-permute-start | bytes 245768 | tf_op jit(solution)/shard_map/ppermute | solution.py:279
  173.8 7.7 %collective-permute-start.12 = (f32[1,8,2,1280]{3,2,1,0:T(2,128)S(1)}, f32[1,8,2,1280]{3,2,1,0:T(2,128)S(1)}, u32[]{:S(2)}, u32[]{:S(2)}) collective-permute-start(f32[1,8,2,1280]{3,2,1,0:T(2,128)S(1)} %get-tuple-element.33), channel_id=1, source_target_pairs={{0,24},{8,0},{16,8},{24,16},{1,25},{9,1},{17,9},{25,17},{2,26},{10... | collective-permute-start | bytes 245768 | tf_op jit(solution)/shard_map/ppermute | solution.py:279
  177.8 5.9 %collective-permute-start.4 = (f32[2,8,2,1280]{3,2,1,0:T(2,128)S(1)}, f32[2,8,2,1280]{3,2,1,0:T(2,128)S(1)}, u32[]{:S(2)}, u32[]{:S(2)}) collective-permute-start(f32[2,8,2,1280]{3,2,1,0:T(2,128)S(1)} %get-tuple-element.29), channel_id=1, source_target_pairs={{0,8},{8,16},{16,24},{24,0},{1,9},{9,17},{17,25},{25,1},{2,10},{10... | collective-permute-start | bytes 491528 | tf_op jit(solution)/shard_map/ppermute | solution.py:279
  177.9 7.5 %collective-permute-start.5 = (f32[2,8,2,1280]{3,2,1,0:T(2,128)S(1)}, f32[2,8,2,1280]{3,2,1,0:T(2,128)S(1)}, u32[]{:S(2)}, u32[]{:S(2)}) collective-permute-start(f32[2,8,2,1280]{3,2,1,0:T(2,128)S(1)} %get-tuple-element.31), channel_id=1, source_target_pairs={{0,16},{8,24},{16,0},{24,8},{1,17},{9,25},{17,1},{25,9},{2,18},{10... | collective-permute-start | bytes 491528 | tf_op jit(solution)/shard_map/ppermute | solution.py:279
  181.4 5.7 %collective-permute-start.6 = (f32[2,8,2,1280]{3,2,1,0:T(2,128)S(1)}, f32[2,8,2,1280]{3,2,1,0:T(2,128)S(1)}, u32[]{:S(2)}, u32[]{:S(2)}) collective-permute-start(f32[2,8,2,1280]{3,2,1,0:T(2,128)S(1)} %get-tuple-element.30), channel_id=1, source_target_pairs={{0,24},{8,0},{16,8},{24,16},{1,25},{9,1},{17,9},{25,17},{2,26},{10... | collective-permute-start | bytes 491528 | tf_op jit(solution)/shard_map/ppermute | solution.py:279
  188.6 14.7 %collective-permute-start.13 = (f32[3,4,2,1280]{3,2,0,1:T(2,128)S(1)}, f32[3,4,2,1280]{3,2,0,1:T(2,128)S(1)}, u32[]{:S(2)}, u32[]{:S(2)}) collective-permute-start(f32[3,4,2,1280]{3,2,0,1:T(2,128)S(1)} %bitcast.74), channel_id=1, source_target_pairs={{0,32},{32,0},{64,96},{96,64},{128,160},{160,128},{192,224},{224,1... | collective-permute-start | bytes 368648 | tf_op jit(solution)/shard_map/ppermute | solution.py:337
  193.8 28.8 %all-to-all-start.3 = ((f16[32,8,1280]{2,1,0:T(8,128)(2,1)}), f16[32,8,1280]{2,1,0:T(8,128)(2,1)S(1)}, u32[]{:S(2)}, u32[]{:S(2)}) async-start(f16[32,8,1280]{2,1,0:T(8,128)(2,1)} %select_convert_fusion), calls=%async_computation.3 | async-start | bytes 1310720 | tf_op jit(solution)/shard_map/all_to_all | solution.py:328
  203.4 15.0 %collective-permute-start.14 = (f32[3,2,1280]{2,1,0:T(2,128)S(1)}, f32[3,2,1280]{2,1,0:T(2,128)S(1)}, u32[]{:S(2)}, u32[]{:S(2)}) collective-permute-start(f32[3,2,1280]{2,1,0:T(2,128)S(1)} %get-tuple-element.37), channel_id=1, source_target_pairs={{0,64},{32,96},{64,0},{96,32},{128,192},{160,224},{192,128},{224,1... | collective-permute-start | bytes 92168 | tf_op jit(solution)/shard_map/ppermute | solution.py:340
  205.8 16.7 %collective-permute-start.15 = (f32[3,2,1280]{2,1,0:T(2,128)S(1)}, f32[3,2,1280]{2,1,0:T(2,128)S(1)}, u32[]{:S(2)}, u32[]{:S(2)}) collective-permute-start(f32[3,2,1280]{2,1,0:T(2,128)S(1)} %get-tuple-element.39), channel_id=1, source_target_pairs={{0,128},{32,160},{64,192},{96,224},{128,0},{160,32},{192,64},{224,... | collective-permute-start | bytes 92168 | tf_op jit(solution)/shard_map/ppermute | solution.py:340
  209.4 13.1 %collective-permute-start.16 = (f32[3,2,1280]{2,1,0:T(2,128)S(1)}, f32[3,2,1280]{2,1,0:T(2,128)S(1)}, u32[]{:S(2)}, u32[]{:S(2)}) collective-permute-start(f32[3,2,1280]{2,1,0:T(2,128)S(1)} %get-tuple-element.38), channel_id=1, source_target_pairs={{0,192},{32,224},{64,128},{96,160},{128,64},{160,96},{192,0},{224,... | collective-permute-start | bytes 92168 | tf_op jit(solution)/shard_map/ppermute | solution.py:340
  222.6 9.1 %copy-start.8 = (f32[48]{0:T(128)S(1)}, f32[48]{0:T(128)}, u32[]{:S(2)}) copy-start(f32[48]{0:T(128)} %param.12) | copy-start | bytes 580
  223.5 9.4 %collective-permute-start.17 = (f32[16,1280]{1,0:T(8,128)S(1)}, f32[16,1280]{1,0:T(8,128)S(1)}, u32[]{:S(2)}, u32[]{:S(2)}) collective-permute-start(f32[16,1280]{1,0:T(8,128)S(1)} %get-tuple-element.41), channel_id=1, source_target_pairs={{0,1},{1,2},{2,3},{3,0},{4,5},{5,6},{6,7},{7,4},{8,9},{9,10},{10,1... | collective-permute-start | bytes 245768 | tf_op jit(solution)/shard_map/ppermute | solution.py:279
  227.4 7.4 %collective-permute-start.18 = (f32[16,1280]{1,0:T(8,128)S(1)}, f32[16,1280]{1,0:T(8,128)S(1)}, u32[]{:S(2)}, u32[]{:S(2)}) collective-permute-start(f32[16,1280]{1,0:T(8,128)S(1)} %get-tuple-element.41), channel_id=1, source_target_pairs={{0,2},{1,3},{2,0},{3,1},{4,6},{5,7},{6,4},{7,5},{8,10},{9,11},{10,... | collective-permute-start | bytes 245768 | tf_op jit(solution)/shard_map/ppermute | solution.py:279
  231.6 4.4 %collective-permute-start.19 = (f32[16,1280]{1,0:T(8,128)S(1)}, f32[16,1280]{1,0:T(8,128)S(1)}, u32[]{:S(2)}, u32[]{:S(2)}) collective-permute-start(f32[16,1280]{1,0:T(8,128)S(1)} %get-tuple-element.41), channel_id=1, source_target_pairs={{0,3},{1,0},{2,1},{3,2},{4,7},{5,4},{6,5},{7,6},{8,11},{9,8},{10,9... | collective-permute-start | bytes 245768 | tf_op jit(solution)/shard_map/ppermute | solution.py:279
